TPU v7x, 32 devices: a whole 2x2x4 slice. The times are simulated.
32 devices in a mesh: gy: 4 (over y, core), gx: 8 (over z, x).
Axes of the slice: x: 2, y: 2, z: 4, core: 2. Of those that a mesh axis runs over, the one named last changes fastest.
Arguments:
- features: bfloat16 [256, 512, 128], P(('gy', 'gx')), may hold values from -6 to 6
- links: int32 [256, 3], P(('gy', 'gx')), may hold values 0 or 1
- block_slot: int32 [256], P(('gy', 'gx')), may hold values from 0 to 15, as said below
- block_level: int32 [256], P(('gy', 'gx')), may hold values from 0 to 3
- slot_column: int32 [32, 16], P(('gy', 'gx')), may hold values from 0 to 31
- conv_first: bfloat16 [7, 128, 128], replicated, may hold values from -0.1875 to 0.1875
- conv_second: bfloat16 [7, 128, 128], replicated, may hold values from -0.1875 to 0.1875
- height_w: bfloat16 [4, 1024, 256], replicated, may hold values from -0.1875 to 0.1875
- plane_first: bfloat16 [3, 3, 256, 256], replicated, may hold values from -0.125 to 0.125
- plane_second: bfloat16 [3, 3, 256, 256], replicated, may hold values from -0.125 to 0.125
Outputs:
- bev_out: bfloat16 [256, 256, 256], P('gy', 'gx')
Inputs may be any that keep to these rules, and one draw needn't show every extreme that they name: No two blocks of one device have both the same block_slot and the same block_level. At most 4 blocks of one device have the same block_slot // 2, and every device has exactly 4 such blocks for some value.
All inputs are finite; a program needn't handle non-finite values. No bound on the sum of `links` on one device may be relied on, other than what follows from the above.
Results may differ from a plain program's by a relative error of at most 0.0065.
Values may be sent and summed in bfloat16 or wider, within the bound.
No kernel may reach another device: no remote copies, remote signals or barrier semaphores. Data moves between devices by JAX's collectives and lax.ppermute only.
A program may use at most 64 MiB of HBM per device.

v0:
```python
import jax
import jax.numpy as jnp
from jax import lax
from jax.sharding import PartitionSpec as P

EDGE = 8
STRIDE_Y = 8
TILE_BR = 8
TILE_BC = 4


def from_behind(block, axis, distance):
    devices = range(lax.axis_size(axis))
    route = [(i - distance, i) for i in devices if i - distance in devices]
    return lax.ppermute(block, axis, route)


def padded_2(cells, sides, width):
    for axis, dim in sides:
        count = lax.axis_size(axis)
        ends = count - 1
        head = lax.slice_in_dim(cells, 0, width, axis=dim)
        tail = lax.slice_in_dim(cells, cells.shape[dim] - width, cells.shape[dim], axis=dim)
        cells = jnp.concatenate(
            [
                lax.ppermute(tail, axis, [(i, (i + 1) % count) for i in range(ends)]),
                cells,
                lax.ppermute(head, axis, [((i + 1) % count, i) for i in range(ends)]),
            ],
            axis=dim,
        )
    return cells


def block_ghosts(blocks, links):
    block_count = blocks.shape[0]
    strides = (1, STRIDE_Y, block_count)
    uppers = []
    lowers = []
    keepers = []
    for axis_num in range(3):
        upper = lax.index_in_dim(blocks, EDGE - 1, axis_num + 1, keepdims=False)
        lower = lax.index_in_dim(blocks, 0, axis_num + 1, keepdims=False)
        keeping = links[:, axis_num].astype(blocks.dtype)[:, None, None, None]
        uppers.append(upper * keeping)
        lowers.append(lower)
        keepers.append(keeping)
    outgoing = [uppers[axis_num][block_count - strides[axis_num] :] for axis_num in range(3)]
    returning = [lowers[axis_num][: strides[axis_num]] for axis_num in range(3)]
    from_below = from_behind((outgoing[0], outgoing[1], outgoing[2]), ("gy", "gx"), 1)
    from_above = from_behind((returning[0], returning[1], returning[2]), ("gy", "gx"), -1)
    ghost_plus = []
    ghost_minus = []
    for axis_num in range(3):
        stride = strides[axis_num]
        ghost_plus.append(
            jnp.concatenate([lowers[axis_num][stride:], from_above[axis_num]], 0)
            * keepers[axis_num]
        )
        ghost_minus.append(
            jnp.concatenate([from_below[axis_num], uppers[axis_num][: block_count - stride]], 0)
        )
    return (ghost_plus, ghost_minus)


def seven_taps(blocks, ghost_plus, ghost_minus, weights):
    channels = blocks.shape[-1]
    result = jnp.dot(blocks.reshape(-1, channels), weights[0], preferred_element_type=jnp.float32)
    for axis_num in range(3):
        axis = axis_num + 1
        upward = jnp.concatenate(
            [
                lax.slice_in_dim(blocks, 1, EDGE, axis=axis),
                jnp.expand_dims(ghost_plus[axis_num], axis),
            ],
            axis,
        )
        downward = jnp.concatenate(
            [
                jnp.expand_dims(ghost_minus[axis_num], axis),
                lax.slice_in_dim(blocks, 0, EDGE - 1, axis=axis),
            ],
            axis,
        )
        result = result + jnp.dot(
            upward.reshape(-1, channels),
            weights[1 + 2 * axis_num],
            preferred_element_type=jnp.float32,
        )
        result = result + jnp.dot(
            downward.reshape(-1, channels),
            weights[2 + 2 * axis_num],
            preferred_element_type=jnp.float32,
        )
    return result.reshape(blocks.shape)


def plane_conv(padded, kernel, rows_out, cols_out):
    result = jnp.zeros((rows_out * cols_out, kernel.shape[3]), jnp.float32)
    for row_off in range(3):
        for col_off in range(3):
            window = padded[row_off : row_off + rows_out, col_off : col_off + cols_out].reshape(
                rows_out * cols_out, -1
            )
            result = result + jnp.dot(
                window, kernel[row_off, col_off], preferred_element_type=jnp.float32
            )
    return result.reshape(rows_out, cols_out, -1)


def tile_rim(plane):
    return padded_2(plane, (("gy", 0), ("gx", 1)), 1)


def local(
    features,
    links,
    block_slot,
    block_level,
    slot_column,
    conv_first,
    conv_second,
    height_w,
    plane_first,
    plane_second,
):
    block_count = features.shape[0]
    channels = features.shape[2]
    blocks = features.reshape(block_count, EDGE, EDGE, EDGE, channels)
    ghost_plus, ghost_minus = block_ghosts(blocks, links)
    hidden = jax.nn.relu(seven_taps(blocks, ghost_plus, ghost_minus, conv_first)).astype(
        jnp.bfloat16
    )
    ghost_plus, ghost_minus = block_ghosts(hidden, links)
    voxel = jax.nn.relu(
        blocks.astype(jnp.float32) + seven_taps(hidden, ghost_plus, ghost_minus, conv_second)
    ).astype(jnp.bfloat16)
    peer_count = lax.axis_size("gx")
    slot_total = slot_column.shape[1]
    per_peer = slot_total // peer_count
    rows_in = voxel.reshape(block_count, EDGE * EDGE, EDGE * channels)
    column_total = TILE_BR * TILE_BC
    chosen = jnp.take(height_w, block_level, axis=0)
    lifted = jnp.einsum("bpk,bkn->bpn", rows_in, chosen, preferred_element_type=jnp.float32)
    slot_pick = (block_slot[None, :] == jnp.arange(slot_total, dtype=jnp.int32)[:, None]).astype(
        jnp.float32
    )
    summed = jnp.dot(
        slot_pick,
        lifted.reshape(block_count, -1),
        precision=lax.Precision.HIGHEST,
        preferred_element_type=jnp.float32,
    )
    column_ids = slot_column.reshape(peer_count, per_peer).astype(jnp.float32)
    arrived_sums, arrived_ids = (
        lax.all_to_all(
            summed.reshape(peer_count, per_peer, -1), "gx", split_axis=0, concat_axis=0, tiled=True
        ),
        lax.all_to_all(column_ids, "gx", split_axis=0, concat_axis=0, tiled=True),
    )
    arrived_sums = arrived_sums.reshape(slot_total, -1)
    arrived_ids = arrived_ids.reshape(1, slot_total)
    column_map = (arrived_ids == jnp.arange(column_total, dtype=jnp.float32)[:, None]).astype(
        jnp.float32
    )
    tile_sum = jnp.dot(
        column_map,
        arrived_sums,
        precision=lax.Precision.HIGHEST,
        preferred_element_type=jnp.float32,
    )
    tile_rows = TILE_BR * EDGE
    tile_cols = TILE_BC * EDGE
    bev = tile_sum.reshape(TILE_BR, TILE_BC, EDGE, EDGE, -1).transpose(0, 2, 1, 3, 4)
    bev = bev.reshape(tile_rows, tile_cols, -1).astype(jnp.bfloat16)
    first = jax.nn.relu(plane_conv(tile_rim(bev), plane_first, tile_rows, tile_cols)).astype(
        jnp.bfloat16
    )
    second = plane_conv(tile_rim(first), plane_second, tile_rows, tile_cols)
    return (second + bev.astype(jnp.float32)).astype(jnp.bfloat16)


def solution(mesh):
    in_specs = (
        P(("gy", "gx"), None, None),
        P(("gy", "gx"), None),
        P(("gy", "gx")),
        P(("gy", "gx")),
        P(("gy", "gx"), None),
        P(),
        P(),
        P(),
        P(),
        P(),
    )
    out_specs = P("gy", "gx", None)
    return jax.shard_map(local, mesh=mesh, in_specs=in_specs, out_specs=out_specs, check_vma=False)
```

profile of v0, /device:TPU:9, one launch (start us, length us, event | category | flops | bytes accessed | tf_op | source)
XLA Modules:
  0.0 182.3 jit_solution(11907539401226740565)
XLA Ops:
  1.5 5.7 %all-to-all-start = ((f32[8,1,2]{2,1,0:T(1,128)}), f32[8,1,2]{2,1,0:T(1,128)}, u32[]{:S(2)}, u32[]{:S(2)}) async-start(f32[8,1,2]{2,1,0:T(1,128)} %bitcast), calls=%async_computation | async-start | bytes 8192 | tf_op jit(solution)/shard_map/all_to_all | solution.py:159
  7.9 3.1 %collective-permute-start = (bf16[1,8,8,128]{3,2,1,0:T(8,128)(2,1)S(1)}, bf16[1,8,8,128]{3,2,1,0:T(8,128)(2,1)S(1)}, u32[]{:S(2)}, u32[]{:S(2)}) collective-permute-start(bf16[1,8,8,128]{3,2,1,0:T(8,128)(2,1)S(1)} %slice_bitcast_fusion.9), channel_id=1, source_target_pairs={{1,0},{2,1},{3,2},{4,3},{5,4},{6,5},{7,6},{8,7},{9,8},{10,9},{11,1... | collective-permute-start | bytes 49160 | tf_op jit(solution)/shard_map/ppermute | solution.py:15
  17.2 7.2 %collective-permute-start.4 = (bf16[8,8,8,128]{3,2,1,0:T(8,128)(2,1)}, bf16[8,8,8,128]{3,2,1,0:T(8,128)(2,1)}, u32[]{:S(2)}, u32[]{:S(2)}) collective-permute-start(bf16[8,8,8,128]{3,2,1,0:T(8,128)(2,1)} %bitcast.262), channel_id=1, source_target_pairs={{1,0},{2,1},{3,2},{4,3},{5,4},{6,5},{7,6},{8,7},{9,8},{10,9},{11,1... | collective-permute-start | bytes 393224 | tf_op jit(solution)/shard_map/ppermute | solution.py:15
  32.7 2.6 %fusion.72 = f32[4096,128]{1,0:T(8,128)} fusion(bf16[4096,128]{1,0:T(8,128)(2,1)S(1)} %bitcast.269, bf16[7,128,128]{2,1,0:T(8,128)(2,1)} %param.15), kind=kOutput, calls=%fused_computation.146 | convolution fusion | flops 134217728 | bytes 3178496 | tf_op jit(solution)/shard_map/dot_general | solution.py:68
  37.4 2.9 %gather_fusion = bf16[8,1024,256]{2,1,0:T(8,128)(2,1)} fusion(bf16[4,1024,256]{2,1,0:T(8,128)(2,1)S(1)} %copy-done, s32[1024]{0:T(1024)} %pad_clamp_fusion), kind=kCustom, calls=%fused_computation | custom fusion | bytes 8388640 | tf_op jit(solution)/shard_map/jit(_take)/gather | solution.py:143
  52.5 3.3 %collective-permute-done.5 = bf16[8,8,8,128]{3,2,1,0:T(8,128)(2,1)S(1)} collective-permute-done((bf16[8,8,8,128]{3,2,1,0:T(8,128)(2,1)S(1)}, bf16[8,8,8,128]{3,2,1,0:T(8,128)(2,1)S(1)}, u32[]{:S(2)}, u32[]{:S(2)}) %collective-permute-start.5) | collective-permute-done | bytes 131104 | tf_op jit(solution)/shard_map/ppermute | solution.py:15
  60.9 3.8 %collective-permute-start.6 = (bf16[1,8,8,128]{3,2,1,0:T(8,128)(2,1)S(1)}, bf16[1,8,8,128]{3,2,1,0:T(8,128)(2,1)S(1)}, u32[]{:S(2)}, u32[]{:S(2)}) collective-permute-start(bf16[1,8,8,128]{3,2,1,0:T(8,128)(2,1)S(1)} %slice_bitcast_fusion.8), channel_id=1, source_target_pairs={{1,0},{2,1},{3,2},{4,3},{5,4},{6,5},{7,6},{8,7},{9,8},{10,9},{11,1... | collective-permute-start | bytes 49160 | tf_op jit(solution)/shard_map/ppermute | solution.py:15
  64.7 7.0 %collective-permute-start.8 = (bf16[8,8,8,128]{3,2,1,0:T(8,128)(2,1)S(1)}, bf16[8,8,8,128]{3,2,1,0:T(8,128)(2,1)S(1)}, u32[]{:S(2)}, u32[]{:S(2)}) collective-permute-start(bf16[8,8,8,128]{3,2,1,0:T(8,128)(2,1)S(1)} %slice_bitcast_fusion.1), channel_id=1, source_target_pairs={{1,0},{2,1},{3,2},{4,3},{5,4},{6,5},{7,6},{8,7},{9,8},{10,9},{11,1... | collective-permute-start | bytes 393224 | tf_op jit(solution)/shard_map/ppermute | solution.py:15
  71.8 2.5 %collective-permute-start.10 = (bf16[8,8,8,128]{3,2,1,0:T(8,128)(2,1)S(1)}, bf16[8,8,8,128]{3,2,1,0:T(8,128)(2,1)S(1)}, u32[]{:S(2)}, u32[]{:S(2)}) collective-permute-start(bf16[8,8,8,128]{3,2,1,0:T(8,128)(2,1)S(1)} %bitcast.322), channel_id=1, source_target_pairs={{1,0},{2,1},{3,2},{4,3},{5,4},{6,5},{7,6},{8,7},{9,8},{10,9},{11,1... | collective-permute-start | bytes 393224 | tf_op jit(solution)/shard_map/ppermute | solution.py:15
  75.8 2.8 %collective-permute-start.7 = (bf16[1,8,8,128]{3,2,1,0:T(8,128)(2,1)S(1)}, bf16[1,8,8,128]{3,2,1,0:T(8,128)(2,1)S(1)}, u32[]{:S(2)}, u32[]{:S(2)}) collective-permute-start(bf16[1,8,8,128]{3,2,1,0:T(8,128)(2,1)S(1)} %slice.423), channel_id=1, source_target_pairs={{0,1},{1,2},{2,3},{3,4},{4,5},{5,6},{6,7},{7,8},{8,9},{9,10},{10,1... | collective-permute-start | bytes 49160 | tf_op jit(solution)/shard_map/ppermute | solution.py:15
  80.7 2.1 %collective-permute-start.11 = (bf16[8,8,8,128]{3,2,1,0:T(8,128)(2,1)S(1)}, bf16[8,8,8,128]{3,2,1,0:T(8,128)(2,1)S(1)}, u32[]{:S(2)}, u32[]{:S(2)}) collective-permute-start(bf16[8,8,8,128]{3,2,1,0:T(8,128)(2,1)S(1)} %get-tuple-element.56), channel_id=1, source_target_pairs={{0,1},{1,2},{2,3},{3,4},{4,5},{5,6},{6,7},{7,8},{8,9},{9,10},{10,1... | collective-permute-start | bytes 393224 | tf_op jit(solution)/shard_map/ppermute | solution.py:15
  84.6 4.3 %collective-permute-done.11 = bf16[8,8,8,128]{3,2,1,0:T(8,128)(2,1)S(1)} collective-permute-done((bf16[8,8,8,128]{3,2,1,0:T(8,128)(2,1)S(1)}, bf16[8,8,8,128]{3,2,1,0:T(8,128)(2,1)S(1)}, u32[]{:S(2)}, u32[]{:S(2)}) %collective-permute-start.11) | collective-permute-done | bytes 131104 | tf_op jit(solution)/shard_map/ppermute | solution.py:15
  92.4 2.9 %reshape.272 = f32[8,64,1024]{2,1,0:T(8,128)} reshape(f32[4096,128]{1,0:T(8,128)} %convolution_add_fusion) | data formatting | bytes 4194304 | tf_op jit(solution)/shard_map/reshape | solution.py:95
  95.3 3.8 %fusion.2 = f32[8,64,256]{2,1,0:T(8,128)S(1)} fusion(bf16[8,1024,256]{2,1,0:T(8,128)(2,1)} %gather_fusion, pred[8]{0:T(512)(128)(4,1)S(1)} %copy-done.20, f32[8,64,1024]{2,1,0:T(8,128)S(1)} %copy-done.3, f32[8,64,1024]{2,1,0:T(8,128)} %reshape.272), kind=kOutput, calls=%fused_computation.15 | convolution fusion | flops 272105472 | bytes 8912904 | tf_op jit(solution)/shard_map/bpk,bkn->bpn/dot_general | solution.py:144
  101.7 7.9 %all-to-all-start.1 = ((f32[8,2,16384]{2,1,0:T(2,128)}), f32[8,2,16384]{2,1,0:T(2,128)S(1)}, u32[]{:S(2)}, u32[]{:S(2)}) async-start(f32[8,2,16384]{2,1,0:T(2,128)} %copy.218), calls=%async_computation.1 | async-start | bytes 2097152 | tf_op jit(solution)/shard_map/all_to_all | solution.py:156
  111.5 22.2 %all-to-all-done.1 = f32[8,2,16384]{2,1,0:T(2,128)S(1)} async-done(((f32[8,2,16384]{2,1,0:T(2,128)}), f32[8,2,16384]{2,1,0:T(2,128)S(1)}, u32[]{:S(2)}, u32[]{:S(2)}) %all-to-all-start.1) | async-done | bytes 1048608 | tf_op jit(solution)/shard_map/all_to_all | solution.py:156
  138.4 2.5 %collective-permute-start.13 = (bf16[1,32,256]{2,1,0:T(8,128)(2,1)S(1)}, bf16[1,32,256]{2,1,0:T(8,128)(2,1)S(1)}, u32[]{:S(2)}, u32[]{:S(2)}) collective-permute-start(bf16[1,32,256]{2,1,0:T(8,128)(2,1)S(1)} %get-tuple-element.32), channel_id=1, source_target_pairs={{8,0},{16,8},{24,16},{9,1},{17,9},{25,17},{10,2},{18,10},{26,18},{... | collective-permute-start | bytes 49160 | tf_op jit(solution)/shard_map/ppermute | solution.py:28
  141.0 2.6 %collective-permute-done.13 = bf16[1,32,256]{2,1,0:T(8,128)(2,1)S(1)} collective-permute-done((bf16[1,32,256]{2,1,0:T(8,128)(2,1)S(1)}, bf16[1,32,256]{2,1,0:T(8,128)(2,1)S(1)}, u32[]{:S(2)}, u32[]{:S(2)}) %collective-permute-start.13) | collective-permute-done | bytes 16416 | tf_op jit(solution)/shard_map/ppermute | solution.py:28
  143.7 2.3 %collective-permute-start.14 = (bf16[66,1,256]{2,1,0:T(2,128)(2,1)S(1)}, bf16[66,1,256]{2,1,0:T(2,128)(2,1)S(1)}, u32[]{:S(2)}, u32[]{:S(2)}) collective-permute-start(bf16[66,1,256]{2,1,0:T(2,128)(2,1)S(1)} %get-tuple-element.23), channel_id=1, source_target_pairs={{0,1},{1,2},{2,3},{3,4},{4,5},{5,6},{6,7},{8,9},{9,10},{10,11},{11... | collective-permute-start | bytes 101384 | tf_op jit(solution)/shard_map/ppermute | solution.py:26
  146.0 4.8 %collective-permute-start.15 = (bf16[66,1,256]{2,1,0:T(2,128)(2,1)S(1)}, bf16[66,1,256]{2,1,0:T(2,128)(2,1)S(1)}, u32[]{:S(2)}, u32[]{:S(2)}) collective-permute-start(bf16[66,1,256]{2,1,0:T(2,128)(2,1)S(1)} %get-tuple-element.24), channel_id=1, source_target_pairs={{1,0},{2,1},{3,2},{4,3},{5,4},{6,5},{7,6},{9,8},{10,9},{11,10},{12... | collective-permute-start | bytes 101384 | tf_op jit(solution)/shard_map/ppermute | solution.py:28
  157.5 2.8 %collective-permute-start.16 = (bf16[1,32,256]{2,1,0:T(8,128)(2,1)S(1)}, bf16[1,32,256]{2,1,0:T(8,128)(2,1)S(1)}, u32[]{:S(2)}, u32[]{:S(2)}) collective-permute-start(bf16[1,32,256]{2,1,0:T(8,128)(2,1)S(1)} %get-tuple-element.27), channel_id=1, source_target_pairs={{0,8},{8,16},{16,24},{1,9},{9,17},{17,25},{2,10},{10,18},{18,26},{... | collective-permute-start | bytes 49160 | tf_op jit(solution)/shard_map/ppermute | solution.py:26
  162.2 3.1 %collective-permute-done.17 = bf16[1,32,256]{2,1,0:T(8,128)(2,1)S(1)} collective-permute-done((bf16[1,32,256]{2,1,0:T(8,128)(2,1)S(1)}, bf16[1,32,256]{2,1,0:T(8,128)(2,1)S(1)}, u32[]{:S(2)}, u32[]{:S(2)}) %collective-permute-start.17) | collective-permute-done | bytes 16416 | tf_op jit(solution)/shard_map/ppermute | solution.py:28
  165.4 4.2 %collective-permute-start.18 = (bf16[66,1,256]{2,1,0:T(2,128)(2,1)S(1)}, bf16[66,1,256]{2,1,0:T(2,128)(2,1)S(1)}, u32[]{:S(2)}, u32[]{:S(2)}) collective-permute-start(bf16[66,1,256]{2,1,0:T(2,128)(2,1)S(1)} %get-tuple-element.19), channel_id=1, source_target_pairs={{0,1},{1,2},{2,3},{3,4},{4,5},{5,6},{6,7},{8,9},{9,10},{10,11},{11... | collective-permute-start | bytes 101384 | tf_op jit(solution)/shard_map/ppermute | solution.py:26
  169.7 2.7 %collective-permute-start.19 = (bf16[66,1,256]{2,1,0:T(2,128)(2,1)S(1)}, bf16[66,1,256]{2,1,0:T(2,128)(2,1)S(1)}, u32[]{:S(2)}, u32[]{:S(2)}) collective-permute-start(bf16[66,1,256]{2,1,0:T(2,128)(2,1)S(1)} %get-tuple-element.20), channel_id=1, source_target_pairs={{1,0},{2,1},{3,2},{4,3},{5,4},{6,5},{7,6},{9,8},{10,9},{11,10},{12... | collective-permute-start | bytes 101384 | tf_op jit(solution)/shard_map/ppermute | solution.py:28
  (173 shorter events, 72.1 us)
Async XLA Ops:
  0.0 37.4 %copy-start = (bf16[4,1024,256]{2,1,0:T(8,128)(2,1)S(1)}, bf16[4,1024,256]{2,1,0:T(8,128)(2,1)}, u32[]{:S(2)}) copy-start(bf16[4,1024,256]{2,1,0:T(8,128)(2,1)} %param.17) | copy-start | bytes 6291460
  0.0 26.3 %copy-start.2 = (bf16[8,512,128]{2,1,0:T(8,128)(2,1)S(1)}, bf16[8,512,128]{2,1,0:T(8,128)(2,1)}, u32[]{:S(2)}) copy-start(bf16[8,512,128]{2,1,0:T(8,128)(2,1)} %param.10) | copy-start | bytes 3145732
  1.5 100.1 %all-to-all-start = ((f32[8,1,2]{2,1,0:T(1,128)}), f32[8,1,2]{2,1,0:T(1,128)}, u32[]{:S(2)}, u32[]{:S(2)}) async-start(f32[8,1,2]{2,1,0:T(1,128)} %bitcast), calls=%async_computation | async-start | bytes 8192 | tf_op jit(solution)/shard_map/all_to_all | solution.py:159
  7.9 32.4 %collective-permute-start = (bf16[1,8,8,128]{3,2,1,0:T(8,128)(2,1)S(1)}, bf16[1,8,8,128]{3,2,1,0:T(8,128)(2,1)S(1)}, u32[]{:S(2)}, u32[]{:S(2)}) collective-permute-start(bf16[1,8,8,128]{3,2,1,0:T(8,128)(2,1)S(1)} %slice_bitcast_fusion.9), channel_id=1, source_target_pairs={{1,0},{2,1},{3,2},{4,3},{5,4},{6,5},{7,6},{8,7},{9,8},{10,9},{11,1... | collective-permute-start | bytes 49160 | tf_op jit(solution)/shard_map/ppermute | solution.py:15
  12.6 30.5 %collective-permute-start.2 = (bf16[8,8,8,128]{3,2,1,0:T(8,128)(2,1)}, bf16[8,8,8,128]{3,2,1,0:T(8,128)(2,1)}, u32[]{:S(2)}, u32[]{:S(2)}) collective-permute-start(bf16[8,8,8,128]{3,2,1,0:T(8,128)(2,1)} %slice_bitcast_fusion.4), channel_id=1, source_target_pairs={{1,0},{2,1},{3,2},{4,3},{5,4},{6,5},{7,6},{8,7},{9,8},{10,9},{11,1... | collective-permute-start | bytes 393224 | tf_op jit(solution)/shard_map/ppermute | solution.py:15
  17.2 31.0 %collective-permute-start.4 = (bf16[8,8,8,128]{3,2,1,0:T(8,128)(2,1)}, bf16[8,8,8,128]{3,2,1,0:T(8,128)(2,1)}, u32[]{:S(2)}, u32[]{:S(2)}) collective-permute-start(bf16[8,8,8,128]{3,2,1,0:T(8,128)(2,1)} %bitcast.262), channel_id=1, source_target_pairs={{1,0},{2,1},{3,2},{4,3},{5,4},{6,5},{7,6},{8,7},{9,8},{10,9},{11,1... | collective-permute-start | bytes 393224 | tf_op jit(solution)/shard_map/ppermute | solution.py:15
  44.4 7.2 %collective-permute-start.1 = (bf16[1,8,8,128]{3,2,1,0:T(8,128)(2,1)S(1)}, bf16[1,8,8,128]{3,2,1,0:T(8,128)(2,1)S(1)}, u32[]{:S(2)}, u32[]{:S(2)}) collective-permute-start(bf16[1,8,8,128]{3,2,1,0:T(8,128)(2,1)S(1)} %slice.408), channel_id=1, source_target_pairs={{0,1},{1,2},{2,3},{3,4},{4,5},{5,6},{6,7},{7,8},{8,9},{9,10},{10,1... | collective-permute-start | bytes 49160 | tf_op jit(solution)/shard_map/ppermute | solution.py:15
  46.3 9.8 %collective-permute-start.3 = (bf16[8,8,8,128]{3,2,1,0:T(8,128)(2,1)S(1)}, bf16[8,8,8,128]{3,2,1,0:T(8,128)(2,1)S(1)}, u32[]{:S(2)}, u32[]{:S(2)}) collective-permute-start(bf16[8,8,8,128]{3,2,1,0:T(8,128)(2,1)S(1)} %get-tuple-element.47), channel_id=1, source_target_pairs={{0,1},{1,2},{2,3},{3,4},{4,5},{5,6},{6,7},{7,8},{8,9},{9,10},{10,1... | collective-permute-start | bytes 393224 | tf_op jit(solution)/shard_map/ppermute | solution.py:15
  49.2 6.6 %collective-permute-start.5 = (bf16[8,8,8,128]{3,2,1,0:T(8,128)(2,1)S(1)}, bf16[8,8,8,128]{3,2,1,0:T(8,128)(2,1)S(1)}, u32[]{:S(2)}, u32[]{:S(2)}) collective-permute-start(bf16[8,8,8,128]{3,2,1,0:T(8,128)(2,1)S(1)} %get-tuple-element.59), channel_id=1, source_target_pairs={{0,1},{1,2},{2,3},{3,4},{4,5},{5,6},{6,7},{7,8},{8,9},{9,10},{10,1... | collective-permute-start | bytes 393224 | tf_op jit(solution)/shard_map/ppermute | solution.py:15
  60.9 14.1 %collective-permute-start.6 = (bf16[1,8,8,128]{3,2,1,0:T(8,128)(2,1)S(1)}, bf16[1,8,8,128]{3,2,1,0:T(8,128)(2,1)S(1)}, u32[]{:S(2)}, u32[]{:S(2)}) collective-permute-start(bf16[1,8,8,128]{3,2,1,0:T(8,128)(2,1)S(1)} %slice_bitcast_fusion.8), channel_id=1, source_target_pairs={{1,0},{2,1},{3,2},{4,3},{5,4},{6,5},{7,6},{8,7},{9,8},{10,9},{11,1... | collective-permute-start | bytes 49160 | tf_op jit(solution)/shard_map/ppermute | solution.py:15
  64.7 11.0 %collective-permute-start.8 = (bf16[8,8,8,128]{3,2,1,0:T(8,128)(2,1)S(1)}, bf16[8,8,8,128]{3,2,1,0:T(8,128)(2,1)S(1)}, u32[]{:S(2)}, u32[]{:S(2)}) collective-permute-start(bf16[8,8,8,128]{3,2,1,0:T(8,128)(2,1)S(1)} %slice_bitcast_fusion.1), channel_id=1, source_target_pairs={{1,0},{2,1},{3,2},{4,3},{5,4},{6,5},{7,6},{8,7},{9,8},{10,9},{11,1... | collective-permute-start | bytes 393224 | tf_op jit(solution)/shard_map/ppermute | solution.py:15
  71.8 8.8 %collective-permute-start.10 = (bf16[8,8,8,128]{3,2,1,0:T(8,128)(2,1)S(1)}, bf16[8,8,8,128]{3,2,1,0:T(8,128)(2,1)S(1)}, u32[]{:S(2)}, u32[]{:S(2)}) collective-permute-start(bf16[8,8,8,128]{3,2,1,0:T(8,128)(2,1)S(1)} %bitcast.322), channel_id=1, source_target_pairs={{1,0},{2,1},{3,2},{4,3},{5,4},{6,5},{7,6},{8,7},{9,8},{10,9},{11,1... | collective-permute-start | bytes 393224 | tf_op jit(solution)/shard_map/ppermute | solution.py:15
  75.8 7.8 %collective-permute-start.7 = (bf16[1,8,8,128]{3,2,1,0:T(8,128)(2,1)S(1)}, bf16[1,8,8,128]{3,2,1,0:T(8,128)(2,1)S(1)}, u32[]{:S(2)}, u32[]{:S(2)}) collective-permute-start(bf16[1,8,8,128]{3,2,1,0:T(8,128)(2,1)S(1)} %slice.423), channel_id=1, source_target_pairs={{0,1},{1,2},{2,3},{3,4},{4,5},{5,6},{6,7},{7,8},{8,9},{9,10},{10,1... | collective-permute-start | bytes 49160 | tf_op jit(solution)/shard_map/ppermute | solution.py:15
  78.6 10.5 %collective-permute-start.9 = (bf16[8,8,8,128]{3,2,1,0:T(8,128)(2,1)S(1)}, bf16[8,8,8,128]{3,2,1,0:T(8,128)(2,1)S(1)}, u32[]{:S(2)}, u32[]{:S(2)}) collective-permute-start(bf16[8,8,8,128]{3,2,1,0:T(8,128)(2,1)S(1)} %get-tuple-element.37), channel_id=1, source_target_pairs={{0,1},{1,2},{2,3},{3,4},{4,5},{5,6},{6,7},{7,8},{8,9},{9,10},{10,1... | collective-permute-start | bytes 393224 | tf_op jit(solution)/shard_map/ppermute | solution.py:15
  80.7 8.3 %collective-permute-start.11 = (bf16[8,8,8,128]{3,2,1,0:T(8,128)(2,1)S(1)}, bf16[8,8,8,128]{3,2,1,0:T(8,128)(2,1)S(1)}, u32[]{:S(2)}, u32[]{:S(2)}) collective-permute-start(bf16[8,8,8,128]{3,2,1,0:T(8,128)(2,1)S(1)} %get-tuple-element.56), channel_id=1, source_target_pairs={{0,1},{1,2},{2,3},{3,4},{4,5},{5,6},{6,7},{7,8},{8,9},{9,10},{10,1... | collective-permute-start | bytes 393224 | tf_op jit(solution)/shard_map/ppermute | solution.py:15
  101.7 32.1 %all-to-all-start.1 = ((f32[8,2,16384]{2,1,0:T(2,128)}), f32[8,2,16384]{2,1,0:T(2,128)S(1)}, u32[]{:S(2)}, u32[]{:S(2)}) async-start(f32[8,2,16384]{2,1,0:T(2,128)} %copy.218), calls=%async_computation.1 | async-start | bytes 2097152 | tf_op jit(solution)/shard_map/all_to_all | solution.py:156
  136.5 4.5 %collective-permute-start.12 = (bf16[1,32,256]{2,1,0:T(8,128)(2,1)S(1)}, bf16[1,32,256]{2,1,0:T(8,128)(2,1)S(1)}, u32[]{:S(2)}, u32[]{:S(2)}) collective-permute-start(bf16[1,32,256]{2,1,0:T(8,128)(2,1)S(1)} %get-tuple-element.31), channel_id=1, source_target_pairs={{0,8},{8,16},{16,24},{1,9},{9,17},{17,25},{2,10},{10,18},{18,26},{... | collective-permute-start | bytes 49160 | tf_op jit(solution)/shard_map/ppermute | solution.py:26
  138.4 5.2 %collective-permute-start.13 = (bf16[1,32,256]{2,1,0:T(8,128)(2,1)S(1)}, bf16[1,32,256]{2,1,0:T(8,128)(2,1)S(1)}, u32[]{:S(2)}, u32[]{:S(2)}) collective-permute-start(bf16[1,32,256]{2,1,0:T(8,128)(2,1)S(1)} %get-tuple-element.32), channel_id=1, source_target_pairs={{8,0},{16,8},{24,16},{9,1},{17,9},{25,17},{10,2},{18,10},{26,18},{... | collective-permute-start | bytes 49160 | tf_op jit(solution)/shard_map/ppermute | solution.py:28
  143.7 7.7 %collective-permute-start.14 = (bf16[66,1,256]{2,1,0:T(2,128)(2,1)S(1)}, bf16[66,1,256]{2,1,0:T(2,128)(2,1)S(1)}, u32[]{:S(2)}, u32[]{:S(2)}) collective-permute-start(bf16[66,1,256]{2,1,0:T(2,128)(2,1)S(1)} %get-tuple-element.23), channel_id=1, source_target_pairs={{0,1},{1,2},{2,3},{3,4},{4,5},{5,6},{6,7},{8,9},{9,10},{10,11},{11... | collective-permute-start | bytes 101384 | tf_op jit(solution)/shard_map/ppermute | solution.py:26
  146.0 5.9 %collective-permute-start.15 = (bf16[66,1,256]{2,1,0:T(2,128)(2,1)S(1)}, bf16[66,1,256]{2,1,0:T(2,128)(2,1)S(1)}, u32[]{:S(2)}, u32[]{:S(2)}) collective-permute-start(bf16[66,1,256]{2,1,0:T(2,128)(2,1)S(1)} %get-tuple-element.24), channel_id=1, source_target_pairs={{1,0},{2,1},{3,2},{4,3},{5,4},{6,5},{7,6},{9,8},{10,9},{11,10},{12... | collective-permute-start | bytes 101384 | tf_op jit(solution)/shard_map/ppermute | solution.py:28
  157.5 4.7 %collective-permute-start.16 = (bf16[1,32,256]{2,1,0:T(8,128)(2,1)S(1)}, bf16[1,32,256]{2,1,0:T(8,128)(2,1)S(1)}, u32[]{:S(2)}, u32[]{:S(2)}) collective-permute-start(bf16[1,32,256]{2,1,0:T(8,128)(2,1)S(1)} %get-tuple-element.27), channel_id=1, source_target_pairs={{0,8},{8,16},{16,24},{1,9},{9,17},{17,25},{2,10},{10,18},{18,26},{... | collective-permute-start | bytes 49160 | tf_op jit(solution)/shard_map/ppermute | solution.py:26
  160.3 5.1 %collective-permute-start.17 = (bf16[1,32,256]{2,1,0:T(8,128)(2,1)S(1)}, bf16[1,32,256]{2,1,0:T(8,128)(2,1)S(1)}, u32[]{:S(2)}, u32[]{:S(2)}) collective-permute-start(bf16[1,32,256]{2,1,0:T(8,128)(2,1)S(1)} %get-tuple-element.28), channel_id=1, source_target_pairs={{8,0},{16,8},{24,16},{9,1},{17,9},{25,17},{10,2},{18,10},{26,18},{... | collective-permute-start | bytes 49160 | tf_op jit(solution)/shard_map/ppermute | solution.py:28
  165.4 7.5 %collective-permute-start.18 = (bf16[66,1,256]{2,1,0:T(2,128)(2,1)S(1)}, bf16[66,1,256]{2,1,0:T(2,128)(2,1)S(1)}, u32[]{:S(2)}, u32[]{:S(2)}) collective-permute-start(bf16[66,1,256]{2,1,0:T(2,128)(2,1)S(1)} %get-tuple-element.19), channel_id=1, source_target_pairs={{0,1},{1,2},{2,3},{3,4},{4,5},{5,6},{6,7},{8,9},{9,10},{10,11},{11... | collective-permute-start | bytes 101384 | tf_op jit(solution)/shard_map/ppermute | solution.py:26
  169.7 5.0 %collective-permute-start.19 = (bf16[66,1,256]{2,1,0:T(2,128)(2,1)S(1)}, bf16[66,1,256]{2,1,0:T(2,128)(2,1)S(1)}, u32[]{:S(2)}, u32[]{:S(2)}) collective-permute-start(bf16[66,1,256]{2,1,0:T(2,128)(2,1)S(1)} %get-tuple-element.20), channel_id=1, source_target_pairs={{1,0},{2,1},{3,2},{4,3},{5,4},{6,5},{7,6},{9,8},{10,9},{11,10},{12... | collective-permute-start | bytes 101384 | tf_op jit(solution)/shard_map/ppermute | solution.py:28
  (19 other events, 86.1 us)
where the time goes:
time: 185 us; the launch traced here: 182 us
  starting transfers between devices  74.9 us (40%)
  waiting for transfers between devices  37.8 us (20%)
  local copies, waits for them, and re-layouts  29.1 us (16%)
  matrix products  23.1 us (12%)
  other arithmetic  16.4 us (9%)
    ppermute x12, starting transfers between devices, from_behind(): return lax.ppermute(block, axis, route)  38.1 us
    all_to_all x1, waiting for transfers between devices, local(): lax.all_to_all(summed.reshape(peer_count, per_peer, -1), 'gx', split_axis...  22.2 us
    ppermute x4, starting transfers between devices, padded_2(): lax.ppermute(head, axis, [((i + 1) % count, i) for i in range(ends)])  12 us
    ppermute x4, starting transfers between devices, padded_2(): lax.ppermute(tail, axis, [(i, (i + 1) % count) for i in range(ends)])  11.2 us
    ppermute x4, waiting for transfers between devices, padded_2(): lax.ppermute(head, axis, [((i + 1) % count, i) for i in range(ends)])  7.98 us
    dot_general x18, matrix products, plane_conv(): jnp.dot(window, kernel[row_off, col_off], preferred_element_type=jnp.floa...  7.93 us
    all_to_all x1, starting transfers between devices, local(): lax.all_to_all(summed.reshape(peer_count, per_peer, -1), 'gx', split_axis...  7.9 us
    ppermute x12, waiting for transfers between devices, from_behind(): return lax.ppermute(block, axis, route)  7.64 us
  transfers between devices with their start and end apart: 22, of which 7 were waited for; matrix products, arithmetic and copies ran while one was open for 27% of the time, Pallas kernels for 0%

commit v1 on v0

v1 whole, which is shorter than its diff:
```python
import functools

import jax
import jax.numpy as jnp
from jax import lax
from jax.experimental import pallas as pl
from jax.experimental.pallas import tpu as pltpu
from jax.sharding import PartitionSpec as P

EDGE = 8
FACE = EDGE * EDGE
CELLS = EDGE * FACE
TILE_BR = 8
TILE_BC = 4
ROWS = TILE_BR * EDGE
COLS = TILE_BC * EDGE
HALO = 2
ID_ROWS = 8
LANES = 128
F32 = jnp.float32
BF16 = jnp.bfloat16

VMEM = pl.BlockSpec(memory_space=pltpu.VMEM)
SMEM = pl.BlockSpec(memory_space=pltpu.SMEM)


def shift(block, axis, distance):
    count = lax.axis_size(axis)
    route = [(i, i + distance) for i in range(count) if 0 <= i + distance < count]
    return lax.ppermute(block, axis, route)


def mm(a, b):
    return jnp.dot(a, b, preferred_element_type=F32)


def link_of(links, block, axis):
    return links[block, axis].astype(F32)


def pack_faces(src, links, up, down):
    count = src.shape[0] // CELLS
    faces = count * FACE
    upper_b, lower_b = [], []
    for j in range(count):
        keep = link_of(links, j, 1)
        for a in range(EDGE):
            base = j * CELLS + a * FACE
            upper_b.append(src[base + FACE - EDGE : base + FACE, :] * keep)
            lower_b.append(src[base : base + EDGE, :])
    up[0:faces, :] = jnp.concatenate(upper_b, 0).astype(BF16)
    down[0:faces, :] = jnp.concatenate(lower_b, 0).astype(BF16)
    upper_c = []
    for j in range(count):
        upper_c.append(
            src[pl.ds(j * CELLS + EDGE - 1, FACE, stride=EDGE), :] * link_of(links, j, 2)
        )
    up[faces : 2 * faces, :] = jnp.concatenate(upper_c, 0).astype(BF16)
    down[faces : 2 * faces, :] = src[pl.ds(0, faces, stride=EDGE), :].astype(BF16)
    last = count * CELLS
    up[2 * faces :, :] = (src[last - FACE : last, :] * link_of(links, count - 1, 0)).astype(BF16)
    down[2 * faces :, :] = src[0:FACE, :].astype(BF16)


def pack_kernel(links, x, up, down, wide):
    wide[...] = x[...].astype(F32)
    pack_faces(wide, links, up, down)


def interior(src, links, weights, out, residual):
    count = src.shape[0] // CELLS
    c_at = lax.broadcasted_iota(jnp.int32, (FACE, EDGE, 128), 1)

    def one(j, carry):
        base = pl.multiple_of(j * CELLS, CELLS)
        rows = src[pl.ds(base, CELLS), :]
        after = jnp.minimum(j + 1, count - 1)
        before = jnp.maximum(j - 1, 0)
        keep_after = jnp.where(j + 1 < count, links[j, 0], 0).astype(F32)
        keep_before = jnp.where(j > 0, links[before, 0], 0).astype(F32)
        over = src[pl.ds(pl.multiple_of(after * CELLS, CELLS), FACE), :]
        under = src[pl.ds(pl.multiple_of(before * CELLS + CELLS - FACE, FACE), FACE), :]
        over = (over.astype(F32) * keep_after).astype(BF16)
        under = (under.astype(F32) * keep_before).astype(BF16)
        wide = rows.astype(F32)
        planes = wide.reshape(EDGE, EDGE, EDGE, 128)
        none = jnp.zeros((EDGE, 1, EDGE, 128), F32)
        lines = wide.reshape(FACE, EDGE, 128)
        taps = [
            rows,
            jnp.concatenate([rows[FACE:], over], 0),
            jnp.concatenate([under, rows[:-FACE]], 0),
            jnp.concatenate([planes[:, 1:], none], 1).reshape(CELLS, 128).astype(BF16),
            jnp.concatenate([none, planes[:, :-1]], 1).reshape(CELLS, 128).astype(BF16),
            jnp.where(c_at == EDGE - 1, 0.0, pltpu.roll(lines, EDGE - 1, 1))
            .reshape(CELLS, 128)
            .astype(BF16),
            jnp.where(c_at == 0, 0.0, pltpu.roll(lines, 1, 1)).reshape(CELLS, 128).astype(BF16),
        ]
        total = mm(jnp.concatenate(taps, 1), weights[...])
        if residual is not None:
            total = total + residual[pl.ds(base, CELLS), :].astype(F32)
        out[pl.ds(base, CELLS), :] = total
        return carry

    lax.fori_loop(0, count, one, 0)


def first_interior_kernel(links, x, weights, out):
    interior(x, links, weights, out, None)


def second_interior_kernel(links, hidden, x, weights, out):
    interior(hidden, links, weights, out, x)


def add_ghosts(total, from_below, from_above, links, weights):
    count = total.shape[0] // CELLS
    faces = count * FACE
    ch = total.shape[1]

    def tap(k):
        return weights[k * ch : (k + 1) * ch, :]

    b_plus = mm(from_above[0:faces, :], tap(3))
    b_minus = mm(from_below[0:faces, :], tap(4))
    for j in range(count):
        keep = link_of(links, j, 1)
        for a in range(EDGE):
            base = j * CELLS + a * FACE
            at = j * FACE + a * EDGE
            total[base + FACE - EDGE : base + FACE, :] += b_plus[at : at + EDGE, :] * keep
            total[base : base + EDGE, :] += b_minus[at : at + EDGE, :]
    c_plus = mm(from_above[faces : 2 * faces, :], tap(5))
    c_minus = mm(from_below[faces : 2 * faces, :], tap(6))
    for j in range(count):
        at = slice(j * FACE, (j + 1) * FACE)
        total[pl.ds(j * CELLS + EDGE - 1, FACE, stride=EDGE), :] += c_plus[at, :] * link_of(
            links, j, 2
        )
        total[pl.ds(j * CELLS, FACE, stride=EDGE), :] += c_minus[at, :]
    last = count * CELLS
    total[last - FACE : last, :] += mm(from_above[2 * faces :, :], tap(1)) * link_of(
        links, count - 1, 0
    )
    total[0:FACE, :] += mm(from_below[2 * faces :, :], tap(2))


def hidden_kernel(links, partial, from_below, from_above, weights, hidden, up, down, total):
    total[...] = partial[...]
    add_ghosts(total, from_below, from_above, links, weights)
    total[...] = jnp.maximum(total[...], 0.0)
    hidden[...] = total[...].astype(BF16)
    pack_faces(total, links, up, down)


def lift_kernel(
    links,
    slots,
    block_levels,
    columns,
    partial,
    from_below,
    from_above,
    weights,
    height,
    out,
    total,
    rows_in,
    sums,
):
    count = partial.shape[0] // CELLS
    faces = count * FACE
    ch = partial.shape[1]
    total[...] = partial[...]
    add_ghosts(total, from_below, from_above, links, weights)
    for c in range(EDGE):
        line = total[pl.ds(c, faces, stride=EDGE), :]
        rows_in[:, c * ch : (c + 1) * ch] = jnp.maximum(line, 0.0).astype(BF16)
    sums[...] = jnp.zeros_like(sums)

    def one(j, carry):
        rows = rows_in[pl.ds(pl.multiple_of(j * FACE, FACE), FACE), :]
        sums[slots[0, j]] += mm(rows, height[block_levels[0, j]])
        return carry

    lax.fori_loop(0, count, one, 0)
    peers = out.shape[0]
    per_peer = sums.shape[0] // peers
    row_at = lax.broadcasted_iota(jnp.int32, (ID_ROWS, out.shape[2]), 0)
    for p in range(peers):
        ids = jnp.zeros(row_at.shape, F32)
        for k in range(per_peer):
            slot = p * per_peer + k
            out[p, k * FACE : (k + 1) * FACE, :] = sums[slot].astype(BF16)
            ids = jnp.where(row_at == k, columns[0, slot].astype(F32), ids)
        out[p, per_peer * FACE :, :] = ids.astype(BF16)


def gather_kernel(arrived, bev, top, bottom, left, right, total):
    peers, rows, ch = arrived.shape
    per_peer = (rows - ID_ROWS) // FACE
    total[...] = jnp.zeros_like(total)
    for p in range(peers):
        ids = arrived[p, per_peer * FACE :, :].astype(F32)
        for k in range(per_peer):
            column = jnp.max(ids[k : k + 1, :]).astype(jnp.int32)
            row_base = (column // TILE_BC) * (EDGE * COLS) + (column % TILE_BC) * EDGE
            block = arrived[p, k * FACE : (k + 1) * FACE, :].astype(F32)
            for a in range(EDGE):
                at = pl.multiple_of(row_base + a * COLS, EDGE)
                for h, lanes in halves(ch):
                    total[h, pl.ds(at, EDGE), :] += block[a * EDGE : (a + 1) * EDGE, lanes]
    for h, lanes in halves(ch):
        bev[:, lanes] = total[h].astype(BF16)
        top[:, lanes] = total[h, 0 : HALO * COLS, :].astype(BF16)
        bottom[:, lanes] = total[h, (ROWS - HALO) * COLS :, :].astype(BF16)
        for x in range(HALO):
            far = COLS - HALO + x
            left[x, :, lanes] = total[h, pl.ds(x, ROWS, stride=COLS), :].astype(BF16)
            right[x, :, lanes] = total[h, pl.ds(far, ROWS, stride=COLS), :].astype(BF16)


def halves(channels):
    return [(h, slice(h * LANES, (h + 1) * LANES)) for h in range(channels // LANES)]


PITCH = COLS + 2 * EDGE
WIDE_ROWS = ROWS + 2 * HALO
MID_ROWS = ROWS + HALO
RIM_ROWS = 72


def side_shifts(padded, before, after, count):
    def one(y, carry):
        at = pl.multiple_of(y * PITCH, EDGE)
        to = pl.multiple_of(y * COLS, COLS)
        for h, lanes in halves(before.shape[1]):
            before[pl.ds(to, COLS), lanes] = padded[h, pl.ds(at + EDGE - 1, COLS), :].astype(BF16)
            after[pl.ds(to, COLS), lanes] = padded[h, pl.ds(at + EDGE + 1, COLS), :].astype(BF16)
        return carry

    lax.fori_loop(0, count, one, 0)


def stacked(sources, first_row, row_count):
    parts = []
    for dy in range(3):
        for source in sources:
            at = pl.multiple_of((first_row + dy) * COLS, COLS)
            parts.append(source[pl.ds(at, row_count * COLS), :])
    return jnp.concatenate(parts, 1)


def plane_kernel(
    flags,
    bev,
    above,
    below,
    left,
    right,
    weights_first,
    weights_second,
    out,
    padded,
    before,
    centre,
    after,
    rim,
):
    ch = bev.shape[1]
    centre[0 : HALO * COLS, :] = above[...]
    centre[HALO * COLS : (HALO + ROWS) * COLS, :] = bev[...]
    centre[(HALO + ROWS) * COLS : WIDE_ROWS * COLS, :] = below[...]

    def widen(y, carry):
        at = pl.multiple_of(y * PITCH + EDGE, EDGE)
        row = centre[pl.ds(pl.multiple_of(y * COLS, COLS), COLS), :].astype(F32)
        for h, lanes in halves(ch):
            padded[h, pl.ds(at, COLS), :] = row[:, lanes]
        return carry

    lax.fori_loop(0, WIDE_ROWS, widen, 0)
    rim[...] = jnp.zeros_like(rim)
    for x in range(HALO):
        lefts = left[x, :, :].astype(F32)
        rights = right[x, :, :].astype(F32)
        rim[x, 0:WIDE_ROWS, :] = lefts
        rim[4 + x, 0:WIDE_ROWS, :] = rights
    for h, lanes in halves(ch):
        own_left = padded[h, pl.ds(EDGE, WIDE_ROWS, stride=PITCH), :]
        own_right = padded[h, pl.ds(EDGE + COLS - 1, WIDE_ROWS, stride=PITCH), :]
        rim[2, 0:WIDE_ROWS, lanes] = own_left
        rim[3, 0:WIDE_ROWS, lanes] = own_right
        padded[h, pl.ds(EDGE - 1, WIDE_ROWS, stride=PITCH), :] = rim[1, 0:WIDE_ROWS, lanes]
        padded[h, pl.ds(EDGE + COLS, WIDE_ROWS, stride=PITCH), :] = rim[4, 0:WIDE_ROWS, lanes]
    side_shifts(padded, before, after, WIDE_ROWS)

    rim_first = []
    for sources in ((0, 1, 2), (3, 4, 5)):
        parts = []
        for dy in range(3):
            for s in sources:
                parts.append(rim[s, dy : dy + RIM_ROWS, :].astype(BF16))
        rim_first.append(jnp.concatenate(parts, 1))
    rim_out = mm(jnp.concatenate(rim_first, 0), weights_first[...])
    rim_out = jnp.maximum(rim_out, 0.0)
    row_at = lax.broadcasted_iota(jnp.int32, (RIM_ROWS, ch), 0)
    inside = jnp.where(
        row_at == 0, flags[0], jnp.where(row_at == MID_ROWS - 1, flags[1], 1)
    ).astype(F32)
    rim_left = rim_out[0:RIM_ROWS, :] * inside * flags[2].astype(F32)
    rim_right = rim_out[RIM_ROWS:, :] * inside * flags[3].astype(F32)

    step = MID_ROWS // 6

    def first_rows(i, carry):
        y = i * step
        block = mm(stacked((before, centre, after), y, step), weights_first[...])
        block = jnp.maximum(block, 0.0)
        for r in range(step):
            keep = jnp.where(
                y + r == 0, flags[0], jnp.where(y + r == MID_ROWS - 1, flags[1], 1)
            ).astype(F32)
            at = pl.multiple_of((y + r) * PITCH + EDGE, EDGE)
            row = block[r * COLS : (r + 1) * COLS, :] * keep
            for h, lanes in halves(ch):
                padded[h, pl.ds(at, COLS), :] = row[:, lanes]
        return carry

    lax.fori_loop(0, MID_ROWS // step, first_rows, 0)
    for h, lanes in halves(ch):
        padded[h, pl.ds(EDGE - 1, MID_ROWS, stride=PITCH), :] = rim_left[0:MID_ROWS, lanes]
        padded[h, pl.ds(EDGE + COLS, MID_ROWS, stride=PITCH), :] = rim_right[0:MID_ROWS, lanes]
    side_shifts(padded, before, after, MID_ROWS)

    def narrow(y, carry):
        at = pl.multiple_of(y * PITCH + EDGE, EDGE)
        to = pl.multiple_of(y * COLS, COLS)
        for h, lanes in halves(ch):
            centre[pl.ds(to, COLS), lanes] = padded[h, pl.ds(at, COLS), :].astype(BF16)
        return carry

    lax.fori_loop(0, MID_ROWS, narrow, 0)
    step2 = 16

    def second_rows(i, carry):
        y = i * step2
        block = mm(stacked((before, centre, after), y, step2), weights_second[...])
        at = pl.multiple_of(y * COLS, COLS)
        own = bev[pl.ds(at, step2 * COLS), :].astype(F32)
        out[pl.ds(at, step2 * COLS), :] = (block + own).astype(BF16)
        return carry

    lax.fori_loop(0, ROWS // step2, second_rows, 0)


def call(kernel, name, out_shape, scalars, arrays, scratch=()):
    multiple = isinstance(out_shape, (list, tuple))
    return pl.pallas_call(
        kernel,
        name=name,
        out_shape=out_shape,
        in_specs=[SMEM] * len(scalars) + [VMEM] * len(arrays),
        out_specs=[VMEM] * len(out_shape) if multiple else VMEM,
        scratch_shapes=list(scratch),
    )(*scalars, *arrays)


def local(
    features,
    links,
    block_slot,
    block_level,
    slot_column,
    conv_first,
    conv_second,
    height_w,
    plane_first,
    plane_second,
):
    count, _, ch = features.shape
    rows = count * CELLS
    faces = (2 * count + 1) * FACE
    mapped = plane_first.shape[3]
    peers = lax.axis_size("gx")
    slot_total = slot_column.shape[1]
    per_peer = slot_total // peers
    x = features.reshape(rows, ch)
    w_first = conv_first.reshape(-1, ch)
    w_second = conv_second.reshape(-1, ch)
    k_first = plane_first.reshape(-1, mapped)
    k_second = plane_second.reshape(-1, mapped)
    slots = block_slot.reshape(1, count)
    block_levels = block_level.reshape(1, count)
    both = ("gy", "gx")

    face_shape = jax.ShapeDtypeStruct((faces, ch), BF16)
    wide = pltpu.VMEM((rows, ch), F32)
    part_shape = jax.ShapeDtypeStruct((rows, ch), F32)

    up, down = call(pack_kernel, "pack", (face_shape, face_shape), (links,), (x,), (wide,))
    from_below = shift(up, both, 1)
    from_above = shift(down, both, -1)
    partial = call(first_interior_kernel, "inside1", part_shape, (links,), (x, w_first))
    hidden, up, down = call(
        hidden_kernel,
        "hidden",
        (jax.ShapeDtypeStruct((rows, ch), BF16), face_shape, face_shape),
        (links,),
        (partial, from_below, from_above, w_first),
        (wide,),
    )
    from_below = shift(up, both, 1)
    from_above = shift(down, both, -1)
    partial = call(second_interior_kernel, "inside2", part_shape, (links,), (hidden, x, w_second))
    outgoing = call(
        lift_kernel,
        "lift",
        jax.ShapeDtypeStruct((peers, per_peer * FACE + ID_ROWS, mapped), BF16),
        (links, slots, block_levels, slot_column),
        (partial, from_below, from_above, w_second, height_w),
        (
            wide,
            pltpu.VMEM((count * FACE, EDGE * ch), BF16),
            pltpu.VMEM((slot_total, FACE, mapped), F32),
        ),
    )
    arrived = lax.all_to_all(outgoing, "gx", split_axis=0, concat_axis=0, tiled=True)

    row_shape = jax.ShapeDtypeStruct((HALO * COLS, mapped), BF16)
    side_shape = jax.ShapeDtypeStruct((HALO, ROWS, mapped), BF16)
    bev, top, bottom, left, right = call(
        gather_kernel,
        "gather",
        (
            jax.ShapeDtypeStruct((ROWS * COLS, mapped), BF16),
            row_shape,
            row_shape,
            side_shape,
            side_shape,
        ),
        (),
        (arrived,),
        (pltpu.VMEM((mapped // LANES, ROWS * COLS, LANES), F32),),
    )
    above = shift(bottom, "gy", 1)
    below = shift(top, "gy", -1)
    corner_above = above.reshape(HALO, COLS, mapped)
    corner_below = below.reshape(HALO, COLS, mapped)

    def side(own, at):
        return jnp.concatenate(
            [
                corner_above[:, at : at + HALO].transpose(1, 0, 2),
                own,
                corner_below[:, at : at + HALO].transpose(1, 0, 2),
            ],
            1,
        )

    from_left = shift(side(right, COLS - HALO), "gx", 1)
    from_right = shift(side(left, 0), "gx", -1)
    gy, gx = lax.axis_index("gy"), lax.axis_index("gx")
    flags = jnp.stack(
        [gy > 0, gy < lax.axis_size("gy") - 1, gx > 0, gx < peers - 1]
    ).astype(jnp.int32)
    out = call(
        plane_kernel,
        "planes",
        jax.ShapeDtypeStruct((ROWS * COLS, mapped), BF16),
        (flags,),
        (bev, above, below, from_left, from_right, k_first, k_second),
        (
            pltpu.VMEM((mapped // LANES, WIDE_ROWS * PITCH, LANES), F32),
            pltpu.VMEM((WIDE_ROWS * COLS, mapped), BF16),
            pltpu.VMEM((WIDE_ROWS * COLS, mapped), BF16),
            pltpu.VMEM((WIDE_ROWS * COLS, mapped), BF16),
            pltpu.VMEM((6, RIM_ROWS + EDGE, mapped), F32),
        ),
    )
    return out.reshape(ROWS, COLS, mapped)


def solution(mesh):
    in_specs = (
        P(("gy", "gx"), None, None),
        P(("gy", "gx"), None),
        P(("gy", "gx")),
        P(("gy", "gx")),
        P(("gy", "gx"), None),
        P(),
        P(),
        P(),
        P(),
        P(),
    )
    out_specs = P("gy", "gx", None)
    return jax.shard_map(local, mesh=mesh, in_specs=in_specs, out_specs=out_specs, check_vma=False)
```

time: 185 us -> 106 us (0.57); the launches traced: 182 us -> 106 us
  starting transfers between devices: 74.9 us -> 22.5 us
  Pallas kernels: 0 us -> 39.1 us
  local copies, waits for them, and re-layouts: 29.1 us -> 3.42 us
  matrix products: 23.1 us -> 0 us
  blocking collectives: 0 us -> 20.9 us
  waiting for transfers between devices: 37.8 us -> 17.3 us
  other arithmetic: 16.4 us -> 2.42 us
    pallas_call x0 -> x7, Pallas kernels: none -> 39.1 us  [call(): pl.pallas_call(kernel, name=name, out_shape=out_shape, in_specs=[SMEM] *...]
    ppermute x20 -> x8, starting transfers between devices: 61.3 us -> 22.5 us  [shift(): return lax.ppermute(block, axis, route)]
    dot_general x35 -> x0, matrix products: 23.1 us -> none  [the longest x18 7.93 us: plane_conv(): jnp.dot(window, kernel[row_off, col_off], preferred_element_type=jnp.floa...]
    all_to_all x2 -> x0, waiting for transfers between devices: 22.2 us -> none  [the longest x1 22.2 us: local(): lax.all_to_all(summed.reshape(peer_count, per_peer, -1), 'gx', split_axis...]
    all_to_all x0 -> x1, blocking collectives: none -> 20.9 us  [local(): lax.all_to_all(outgoing, 'gx', split_axis=0, concat_axis=0, tiled=True)]
    all_to_all x2 -> x0, starting transfers between devices: 13.6 us -> none  [the longest x1 7.9 us: local(): lax.all_to_all(summed.reshape(peer_count, per_peer, -1), 'gx', split_axis...]
    slice x22 -> x2, local copies, waits for them, and re-layouts: 11.6 us -> 0.01 us  [the longest x1 0.01 us: side(): corner_above[:, at:at + HALO].transpose(1, 0, 2)]
    concatenate x15 -> x2, other arithmetic: 6.2 us -> 1.74 us  [side(): jnp.concatenate([corner_above[:, at:at + HALO].transpose(1, 0, 2), own, c...]
  transfers between devices with their start and end apart: 22 -> 8, of which waited for: 7 -> 5; matrix products, arithmetic and copies ran while one was open for 27% -> 1% of each run, Pallas kernels for 0% -> 11%
where the time goes in v1:
time: 106 us
  Pallas kernels  39.1 us (37%)
  starting transfers between devices  22.5 us (21%)
  blocking collectives  20.9 us (20%)
  waiting for transfers between devices  17.3 us (16%)
  local copies, waits for them, and re-layouts  3.42 us (3%)
  other arithmetic  2.42 us (2%)
    pallas_call x7, Pallas kernels, call(): pl.pallas_call(kernel, name=name, out_shape=out_shape, in_specs=[SMEM] *...  39.1 us
    ppermute x8, starting transfers between devices, shift(): return lax.ppermute(block, axis, route)  22.5 us
    all_to_all x1, blocking collectives, local(): lax.all_to_all(outgoing, 'gx', split_axis=0, concat_axis=0, tiled=True)  20.9 us
    ppermute x8, waiting for transfers between devices, shift(): return lax.ppermute(block, axis, route)  17.3 us
    unnamed x17, local copies, waits for them, and re-layouts  3.39 us
  transfers between devices with their start and end apart: 8, of which 5 were waited for; matrix products, arithmetic and copies ran while one was open for 1% of the time, Pallas kernels for 11%

profile of v1, /device:TPU:9, one launch (start us, length us, event | category | flops | bytes accessed | tf_op | source)
XLA Modules:
  0.0 105.7 jit_solution(9691267387834086979)
XLA Ops:
  0.0 1.3 %copy.20.links = s32[8,3]{1,0:T(8,128)} copy(s32[8,3]{0,1:T(4,128)} %param.11) | data formatting | bytes 192 | tf_op args[1]
  1.3 2.4 %pack.1 = (bf16[1088,128]{1,0:T(8,128)(2,1)}, bf16[1088,128]{1,0:T(8,128)(2,1)}) custom-call(s32[8,3]{1,0:T(8,128)} %copy.20.links, bf16[4096,128]{1,0:T(8,128)(2,1)} %bitcast.22), custom_call_target="tpu_custom_call" | custom-call | tf_op jit(solution)/shard_map/pack/pallas_call | solution.py:360
  3.7 3.1 %collective-permute-start = (bf16[1088,128]{1,0:T(8,128)(2,1)}, bf16[1088,128]{1,0:T(8,128)(2,1)S(1)}, u32[]{:S(2)}, u32[]{:S(2)}) collective-permute-start(bf16[1088,128]{1,0:T(8,128)(2,1)} %get-tuple-element.15), channel_id=1, source_target_pairs={{0,1},{1,2},{2,3},{3,4},{4,5},{5,6},{6,7},{7,8},{8,9},{9,10},{10,1... | collective-permute-start | bytes 835592 | tf_op jit(solution)/shard_map/ppermute | solution.py:30
  6.8 3.1 %collective-permute-start.1 = (bf16[1088,128]{1,0:T(8,128)(2,1)}, bf16[1088,128]{1,0:T(8,128)(2,1)S(1)}, u32[]{:S(2)}, u32[]{:S(2)}) collective-permute-start(bf16[1088,128]{1,0:T(8,128)(2,1)} %get-tuple-element.16), channel_id=1, source_target_pairs={{1,0},{2,1},{3,2},{4,3},{5,4},{6,5},{7,6},{8,7},{9,8},{10,9},{11,1... | collective-permute-start | bytes 835592 | tf_op jit(solution)/shard_map/ppermute | solution.py:30
  9.9 5.8 %inside1.1.partial = f32[4096,128]{1,0:T(8,128)} custom-call(s32[8,3]{1,0:T(8,128)} %copy.20.links, bf16[4096,128]{1,0:T(8,128)(2,1)} %bitcast.23, bf16[896,128]{1,0:T(8,128)(2,1)} %bitcast.27), custom_call_target="tpu_custom_call" | custom-call | tf_op jit(solution)/shard_map/inside1/pallas_call | solution.py:360
  15.7 2.6 %collective-permute-done.from_below = bf16[1088,128]{1,0:T(8,128)(2,1)S(1)} collective-permute-done((bf16[1088,128]{1,0:T(8,128)(2,1)}, bf16[1088,128]{1,0:T(8,128)(2,1)S(1)}, u32[]{:S(2)}, u32[]{:S(2)}) %collective-permute-start) | collective-permute-done | bytes 278560 | tf_op jit(solution)/shard_map/ppermute | solution.py:30
  18.3 3.0 %collective-permute-done.1.from_above = bf16[1088,128]{1,0:T(8,128)(2,1)S(1)} collective-permute-done((bf16[1088,128]{1,0:T(8,128)(2,1)}, bf16[1088,128]{1,0:T(8,128)(2,1)S(1)}, u32[]{:S(2)}, u32[]{:S(2)}) %collective-permute-start.1) | collective-permute-done | bytes 278560 | tf_op jit(solution)/shard_map/ppermute | solution.py:30
  22.0 3.6 %hidden.1 = (bf16[4096,128]{1,0:T(8,128)(2,1)}, bf16[1088,128]{1,0:T(8,128)(2,1)}, bf16[1088,128]{1,0:T(8,128)(2,1)}) custom-call(s32[8,3]{1,0:T(8,128)} %copy.20.links, f32[4096,128]{1,0:T(8,128)} %inside1.1.partial, bf16[1088,128]{1,0:T(8,128)(2,1)} %copy-done.2, bf16[1088,128]{1,0:T(8,128)(2,1)} %copy-done.3, bf16[896,128]{1,0:T(8,128)(2,1)} %bitcast.28), custom_call_target="tpu_custom_call" | custom-call | tf_op jit(solution)/shard_map/hidden/pallas_call | solution.py:360
  25.6 1.9 %collective-permute-start.2 = (bf16[1088,128]{1,0:T(8,128)(2,1)}, bf16[1088,128]{1,0:T(8,128)(2,1)S(1)}, u32[]{:S(2)}, u32[]{:S(2)}) collective-permute-start(bf16[1088,128]{1,0:T(8,128)(2,1)} %get-tuple-element.18), channel_id=1, source_target_pairs={{0,1},{1,2},{2,3},{3,4},{4,5},{5,6},{6,7},{7,8},{8,9},{9,10},{10,1... | collective-permute-start | bytes 835592 | tf_op jit(solution)/shard_map/ppermute | solution.py:30
  27.5 4.3 %collective-permute-start.3 = (bf16[1088,128]{1,0:T(8,128)(2,1)}, bf16[1088,128]{1,0:T(8,128)(2,1)S(1)}, u32[]{:S(2)}, u32[]{:S(2)}) collective-permute-start(bf16[1088,128]{1,0:T(8,128)(2,1)} %get-tuple-element.19), channel_id=1, source_target_pairs={{1,0},{2,1},{3,2},{4,3},{5,4},{6,5},{7,6},{8,7},{9,8},{10,9},{11,1... | collective-permute-start | bytes 835592 | tf_op jit(solution)/shard_map/ppermute | solution.py:30
  31.8 6.2 %inside2.1.partial = f32[4096,128]{1,0:T(8,128)} custom-call(s32[8,3]{1,0:T(8,128)} %copy.20.links, bf16[4096,128]{1,0:T(8,128)(2,1)} %get-tuple-element.17.hidden, bf16[4096,128]{1,0:T(8,128)(2,1)} %bitcast.24, bf16[896,128]{1,0:T(8,128)(2,1)} %bitcast.29), custom_call_target="tpu_custom_call" | custom-call | tf_op jit(solution)/shard_map/inside2/pallas_call | solution.py:360
  37.9 5.2 %collective-permute-done.3.from_above = bf16[1088,128]{1,0:T(8,128)(2,1)S(1)} collective-permute-done((bf16[1088,128]{1,0:T(8,128)(2,1)}, bf16[1088,128]{1,0:T(8,128)(2,1)S(1)}, u32[]{:S(2)}, u32[]{:S(2)}) %collective-permute-start.3) | collective-permute-done | bytes 278560 | tf_op jit(solution)/shard_map/ppermute | solution.py:30
  43.8 6.0 %lift.1 = bf16[8,136,256]{2,1,0:T(8,128)(2,1)} custom-call(s32[8,3]{1,0:T(8,128)} %copy.20.links, s32[1,8]{1,0:T(1,128)} %bitcast.33, s32[1,8]{1,0:T(1,128)} %bitcast.34, s32[1,16]{1,0:T(1,128)} %columns.1, f32[4096,128]{1,0:T(8,128)} %inside2.1.partial, bf16[1088,128]{1,0:T(8,128)(2,1)} %copy-done, bf16[1088,128]{1,0:T(8,128)(2,1)} %copy-done.1, ...), custom_call_target="tpu_custom_call" | custom-call | tf_op jit(solution)/shard_map/lift/pallas_call | solution.py:360
  49.8 20.9 %all_to_all.5.arrived = bf16[8,136,256]{2,1,0:T(8,128)(2,1)} all-to-all(bf16[8,136,256]{2,1,0:T(8,128)(2,1)} %lift.1), channel_id=1, replica_groups=mesh['gy'=4,'gx'=8] {'gx'}, dimensions={0} | all-to-all | bytes 1114112 | tf_op jit(solution)/shard_map/all_to_all | solution.py:429
  70.7 2.7 %gather.1 = (bf16[2048,256]{1,0:T(8,128)(2,1)}, bf16[64,256]{1,0:T(8,128)(2,1)}, bf16[64,256]{1,0:T(8,128)(2,1)}, bf16[2,64,256]{2,1,0:T(8,128)(2,1)}, bf16[2,64,256]{2,1,0:T(8,128)(2,1)}) custom-call(bf16[8,136,256]{2,1,0:T(8,128)(2,1)} %all_to_all.5.arrived), custom_call_target="tpu_custom_call" | custom-call | tf_op jit(solution)/shard_map/gather/pallas_call | solution.py:360
  73.4 2.9 %collective-permute-start.4 = (bf16[64,256]{1,0:T(8,128)(2,1)}, bf16[64,256]{1,0:T(8,128)(2,1)S(1)}, u32[]{:S(2)}, u32[]{:S(2)}) collective-permute-start(bf16[64,256]{1,0:T(8,128)(2,1)} %get-tuple-element.21), channel_id=1, source_target_pairs={{0,8},{8,16},{16,24},{1,9},{9,17},{17,25},{2,10},{10,18},{18,26},{... | collective-permute-start | bytes 98312 | tf_op jit(solution)/shard_map/ppermute | solution.py:30
  76.3 2.0 %collective-permute-start.5 = (bf16[64,256]{1,0:T(8,128)(2,1)}, bf16[64,256]{1,0:T(8,128)(2,1)S(1)}, u32[]{:S(2)}, u32[]{:S(2)}) collective-permute-start(bf16[64,256]{1,0:T(8,128)(2,1)} %get-tuple-element.22), channel_id=1, source_target_pairs={{8,0},{16,8},{24,16},{9,1},{17,9},{25,17},{10,2},{18,10},{26,18},{... | collective-permute-start | bytes 98312 | tf_op jit(solution)/shard_map/ppermute | solution.py:30
  78.3 3.4 %collective-permute-done.5.below = bf16[64,256]{1,0:T(8,128)(2,1)S(1)} collective-permute-done((bf16[64,256]{1,0:T(8,128)(2,1)}, bf16[64,256]{1,0:T(8,128)(2,1)S(1)}, u32[]{:S(2)}, u32[]{:S(2)}) %collective-permute-start.5) | collective-permute-done | bytes 32800 | tf_op jit(solution)/shard_map/ppermute | solution.py:30
  81.8 0.9 pad_maximum_fusion.1
  82.6 3.1 %collective-permute-start.7 = (bf16[2,68,256]{2,1,0:T(8,128)(2,1)S(1)}, bf16[2,68,256]{2,1,0:T(8,128)(2,1)S(1)}, u32[]{:S(2)}, u32[]{:S(2)}) collective-permute-start(bf16[2,68,256]{2,1,0:T(8,128)(2,1)S(1)} %pad_maximum_fusion.1), channel_id=1, source_target_pairs={{1,0},{2,1},{3,2},{4,3},{5,4},{6,5},{7,6},{9,8},{10,9},{11,10},{12... | collective-permute-start | bytes 208904 | tf_op jit(solution)/shard_map/ppermute | solution.py:30
  85.8 0.9 pad_maximum_fusion
  86.7 2.1 %collective-permute-start.6 = (bf16[2,68,256]{2,1,0:T(8,128)(2,1)S(1)}, bf16[2,68,256]{2,1,0:T(8,128)(2,1)S(1)}, u32[]{:S(2)}, u32[]{:S(2)}) collective-permute-start(bf16[2,68,256]{2,1,0:T(8,128)(2,1)S(1)} %pad_maximum_fusion), channel_id=1, source_target_pairs={{0,1},{1,2},{2,3},{3,4},{4,5},{5,6},{6,7},{8,9},{9,10},{10,11},{11... | collective-permute-start | bytes 208904 | tf_op jit(solution)/shard_map/ppermute | solution.py:30
  89.5 3.2 %collective-permute-done.6.left = bf16[2,68,256]{2,1,0:T(8,128)(2,1)S(1)} collective-permute-done((bf16[2,68,256]{2,1,0:T(8,128)(2,1)S(1)}, bf16[2,68,256]{2,1,0:T(8,128)(2,1)S(1)}, u32[]{:S(2)}, u32[]{:S(2)}) %collective-permute-start.6) | collective-permute-done | bytes 69664 | tf_op jit(solution)/shard_map/ppermute | solution.py:30
  93.3 12.4 %planes.1 = bf16[2048,256]{1,0:T(8,128)(2,1)} custom-call(s32[4]{0:T(128)} %add_convert_fusion.flags, bf16[2048,256]{1,0:T(8,128)(2,1)} %get-tuple-element.20.bev, bf16[64,256]{1,0:T(8,128)(2,1)} %copy-done.6, bf16[64,256]{1,0:T(8,128)(2,1)} %copy-done.7, bf16[2,68,256]{2,1,0:T(8,128)(2,1)} %copy-done.5, bf16[2,68,256]{2,1,0:T(8,128)(2,1)} %copy-done.4, ...), custom_call_target="tpu_custom_call" | custom-call | tf_op jit(solution)/shard_map/planes/pallas_call | solution.py:360
  (24 shorter events, 2.8 us)
Async XLA Ops:
  3.7 14.6 %collective-permute-start = (bf16[1088,128]{1,0:T(8,128)(2,1)}, bf16[1088,128]{1,0:T(8,128)(2,1)S(1)}, u32[]{:S(2)}, u32[]{:S(2)}) collective-permute-start(bf16[1088,128]{1,0:T(8,128)(2,1)} %get-tuple-element.15), channel_id=1, source_target_pairs={{0,1},{1,2},{2,3},{3,4},{4,5},{5,6},{6,7},{7,8},{8,9},{9,10},{10,1... | collective-permute-start | bytes 835592 | tf_op jit(solution)/shard_map/ppermute | solution.py:30
  6.8 14.4 %collective-permute-start.1 = (bf16[1088,128]{1,0:T(8,128)(2,1)}, bf16[1088,128]{1,0:T(8,128)(2,1)S(1)}, u32[]{:S(2)}, u32[]{:S(2)}) collective-permute-start(bf16[1088,128]{1,0:T(8,128)(2,1)} %get-tuple-element.16), channel_id=1, source_target_pairs={{1,0},{2,1},{3,2},{4,3},{5,4},{6,5},{7,6},{8,7},{9,8},{10,9},{11,1... | collective-permute-start | bytes 835592 | tf_op jit(solution)/shard_map/ppermute | solution.py:30
  18.3 3.0 %copy-start.2 = (bf16[1088,128]{1,0:T(8,128)(2,1)}, bf16[1088,128]{1,0:T(8,128)(2,1)S(1)}, u32[]{:S(2)}) copy-start(bf16[1088,128]{1,0:T(8,128)(2,1)S(1)} %collective-permute-done.from_below) | copy-start | bytes 835588
  21.3 0.7 copy-start.3
  25.6 12.3 %collective-permute-start.2 = (bf16[1088,128]{1,0:T(8,128)(2,1)}, bf16[1088,128]{1,0:T(8,128)(2,1)S(1)}, u32[]{:S(2)}, u32[]{:S(2)}) collective-permute-start(bf16[1088,128]{1,0:T(8,128)(2,1)} %get-tuple-element.18), channel_id=1, source_target_pairs={{0,1},{1,2},{2,3},{3,4},{4,5},{5,6},{6,7},{7,8},{8,9},{9,10},{10,1... | collective-permute-start | bytes 835592 | tf_op jit(solution)/shard_map/ppermute | solution.py:30
  27.5 15.6 %collective-permute-start.3 = (bf16[1088,128]{1,0:T(8,128)(2,1)}, bf16[1088,128]{1,0:T(8,128)(2,1)S(1)}, u32[]{:S(2)}, u32[]{:S(2)}) collective-permute-start(bf16[1088,128]{1,0:T(8,128)(2,1)} %get-tuple-element.19), channel_id=1, source_target_pairs={{1,0},{2,1},{3,2},{4,3},{5,4},{6,5},{7,6},{8,7},{9,8},{10,9},{11,1... | collective-permute-start | bytes 835592 | tf_op jit(solution)/shard_map/ppermute | solution.py:30
  37.9 5.2 %copy-start = (bf16[1088,128]{1,0:T(8,128)(2,1)}, bf16[1088,128]{1,0:T(8,128)(2,1)S(1)}, u32[]{:S(2)}) copy-start(bf16[1088,128]{1,0:T(8,128)(2,1)S(1)} %collective-permute-done.2.from_below) | copy-start | bytes 835588
  43.1 0.7 copy-start.1
  73.4 4.9 %collective-permute-start.4 = (bf16[64,256]{1,0:T(8,128)(2,1)}, bf16[64,256]{1,0:T(8,128)(2,1)S(1)}, u32[]{:S(2)}, u32[]{:S(2)}) collective-permute-start(bf16[64,256]{1,0:T(8,128)(2,1)} %get-tuple-element.21), channel_id=1, source_target_pairs={{0,8},{8,16},{16,24},{1,9},{9,17},{17,25},{2,10},{10,18},{18,26},{... | collective-permute-start | bytes 98312 | tf_op jit(solution)/shard_map/ppermute | solution.py:30
  76.3 5.4 %collective-permute-start.5 = (bf16[64,256]{1,0:T(8,128)(2,1)}, bf16[64,256]{1,0:T(8,128)(2,1)S(1)}, u32[]{:S(2)}, u32[]{:S(2)}) collective-permute-start(bf16[64,256]{1,0:T(8,128)(2,1)} %get-tuple-element.22), channel_id=1, source_target_pairs={{8,0},{16,8},{24,16},{9,1},{17,9},{25,17},{10,2},{18,10},{26,18},{... | collective-permute-start | bytes 98312 | tf_op jit(solution)/shard_map/ppermute | solution.py:30
  78.3 14.3 %copy-start.6 = (bf16[64,256]{1,0:T(8,128)(2,1)}, bf16[64,256]{1,0:T(8,128)(2,1)S(1)}, u32[]{:S(2)}) copy-start(bf16[64,256]{1,0:T(8,128)(2,1)S(1)} %collective-permute-done.4.above) | copy-start | bytes 98308
  81.7 10.9 %copy-start.7 = (bf16[64,256]{1,0:T(8,128)(2,1)}, bf16[64,256]{1,0:T(8,128)(2,1)S(1)}, u32[]{:S(2)}) copy-start(bf16[64,256]{1,0:T(8,128)(2,1)S(1)} %collective-permute-done.5.below) | copy-start | bytes 98308
  82.6 6.9 %collective-permute-start.7 = (bf16[2,68,256]{2,1,0:T(8,128)(2,1)S(1)}, bf16[2,68,256]{2,1,0:T(8,128)(2,1)S(1)}, u32[]{:S(2)}, u32[]{:S(2)}) collective-permute-start(bf16[2,68,256]{2,1,0:T(8,128)(2,1)S(1)} %pad_maximum_fusion.1), channel_id=1, source_target_pairs={{1,0},{2,1},{3,2},{4,3},{5,4},{6,5},{7,6},{9,8},{10,9},{11,10},{12... | collective-permute-start | bytes 208904 | tf_op jit(solution)/shard_map/ppermute | solution.py:30
  86.7 6.0 %collective-permute-start.6 = (bf16[2,68,256]{2,1,0:T(8,128)(2,1)S(1)}, bf16[2,68,256]{2,1,0:T(8,128)(2,1)S(1)}, u32[]{:S(2)}, u32[]{:S(2)}) collective-permute-start(bf16[2,68,256]{2,1,0:T(8,128)(2,1)S(1)} %pad_maximum_fusion), channel_id=1, source_target_pairs={{0,1},{1,2},{2,3},{3,4},{4,5},{5,6},{6,7},{8,9},{9,10},{10,11},{11... | collective-permute-start | bytes 208904 | tf_op jit(solution)/shard_map/ppermute | solution.py:30
  89.5 3.2 %copy-start.4 = (bf16[2,68,256]{2,1,0:T(8,128)(2,1)}, bf16[2,68,256]{2,1,0:T(8,128)(2,1)S(1)}, u32[]{:S(2)}) copy-start(bf16[2,68,256]{2,1,0:T(8,128)(2,1)S(1)} %collective-permute-done.7.right) | copy-start | bytes 208900
  92.7 0.6 copy-start.5

commit v2 on v1

--- a/solution.py
+++ b/solution.py
@@ -35,7 +35,7 @@
 
 
 def link_of(links, block, axis):
-    return links[block, axis].astype(F32)
+    return links[axis, block].astype(F32)
 
 
 def pack_faces(src, links, up, down):
@@ -76,8 +76,8 @@
         rows = src[pl.ds(base, CELLS), :]
         after = jnp.minimum(j + 1, count - 1)
         before = jnp.maximum(j - 1, 0)
-        keep_after = jnp.where(j + 1 < count, links[j, 0], 0).astype(F32)
-        keep_before = jnp.where(j > 0, links[before, 0], 0).astype(F32)
+        keep_after = jnp.where(j + 1 < count, links[0, j], 0).astype(F32)
+        keep_before = jnp.where(j > 0, links[0, before], 0).astype(F32)
         over = src[pl.ds(pl.multiple_of(after * CELLS, CELLS), FACE), :]
         under = src[pl.ds(pl.multiple_of(before * CELLS + CELLS - FACE, FACE), FACE), :]
         over = (over.astype(F32) * keep_after).astype(BF16)
@@ -355,7 +355,7 @@
     lax.fori_loop(0, ROWS // step2, second_rows, 0)
 
 
-def call(kernel, name, out_shape, scalars, arrays, scratch=()):
+def call(kernel, name, out_shape, scalars, arrays, scratch=(), mib=12):
     multiple = isinstance(out_shape, (list, tuple))
     return pl.pallas_call(
         kernel,
@@ -364,6 +364,7 @@
         in_specs=[SMEM] * len(scalars) + [VMEM] * len(arrays),
         out_specs=[VMEM] * len(out_shape) if multiple else VMEM,
         scratch_shapes=list(scratch),
+        compiler_params=pltpu.CompilerParams(vmem_limit_bytes=mib << 20),
     )(*scalars, *arrays)
 
 
@@ -394,6 +395,7 @@
     slots = block_slot.reshape(1, count)
     block_levels = block_level.reshape(1, count)
     both = ("gy", "gx")
+    links = links.T
 
     face_shape = jax.ShapeDtypeStruct((faces, ch), BF16)
     wide = pltpu.VMEM((rows, ch), F32)
@@ -478,6 +480,7 @@
             pltpu.VMEM((WIDE_ROWS * COLS, mapped), BF16),
             pltpu.VMEM((6, RIM_ROWS + EDGE, mapped), F32),
         ),
+        mib=20,
     )
     return out.reshape(ROWS, COLS, mapped)
 

time: 106 us -> 93.8 us (0.88)
  Pallas kernels: 39.1 us -> 25.4 us
  waiting for transfers between devices: 17.3 us -> 20.1 us
  other arithmetic: 2.42 us -> 0.14 us
  blocking collectives: 20.9 us -> 19.2 us
  starting transfers between devices: 22.5 us -> 23.9 us
    pallas_call x7, Pallas kernels: 39.1 us -> 25.4 us  [call(): pl.pallas_call(kernel, name=name, out_shape=out_shape, in_specs=[SMEM] *...]
    ppermute x8, waiting for transfers between devices: 17.3 us -> 20.1 us  [shift(): return lax.ppermute(block, axis, route)]
    concatenate x2, other arithmetic: 1.74 us -> 0.05 us  [side(): jnp.concatenate([corner_above[:, at:at + HALO].transpose(1, 0, 2), own, c...]
    all_to_all x1, blocking collectives: 20.9 us -> 19.2 us  [local(): lax.all_to_all(outgoing, 'gx', split_axis=0, concat_axis=0, tiled=True)]
    ppermute x8, starting transfers between devices: 22.5 us -> 23.9 us  [shift(): return lax.ppermute(block, axis, route)]
    unnamed x17 -> x24, local copies, waits for them, and re-layouts: 3.39 us -> 3.49 us
  transfers between devices with their start and end apart: 8 -> 8, of which waited for: 5 -> 6; matrix products, arithmetic and copies ran while one was open for 1% -> 1% of each run, Pallas kernels for 11% -> 8%
where the time goes in v2:
time: 93.8 us; the launch traced here: 93.3 us
  Pallas kernels  25.4 us (27%)
  starting transfers between devices  23.9 us (25%)
  waiting for transfers between devices  20.1 us (21%)
  blocking collectives  19.2 us (20%)
  local copies, waits for them, and re-layouts  4.23 us (5%)
    pallas_call x7, Pallas kernels, call(): pl.pallas_call(kernel, name=name, out_shape=out_shape, in_specs=[SMEM] *...  25.4 us
    ppermute x8, starting transfers between devices, shift(): return lax.ppermute(block, axis, route)  23.9 us
    ppermute x8, waiting for transfers between devices, shift(): return lax.ppermute(block, axis, route)  20.1 us
    all_to_all x1, blocking collectives, local(): lax.all_to_all(outgoing, 'gx', split_axis=0, concat_axis=0, tiled=True)  19.2 us
    unnamed x24, local copies, waits for them, and re-layouts  3.49 us
  transfers between devices with their start and end apart: 8, of which 6 were waited for; matrix products, arithmetic and copies ran while one was open for 1% of the time, Pallas kernels for 8%

profile of v2, /device:TPU:9, one launch (start us, length us, event | category | flops | bytes accessed | tf_op | source)
XLA Modules:
  0.0 93.3 jit_solution(194103119342428773)
XLA Ops:
  0.0 1.2 %copy-done = bf16[8,512,128]{2,1,0:T(8,128)(2,1)S(1)} copy-done((bf16[8,512,128]{2,1,0:T(8,128)(2,1)S(1)}, bf16[8,512,128]{2,1,0:T(8,128)(2,1)}, u32[]{:S(2)}) %copy-start) | copy-done | bytes 1048600
  1.9 0.9 pack.1
  2.8 3.1 %collective-permute-start = (bf16[1088,128]{1,0:T(8,128)(2,1)S(1)}, bf16[1088,128]{1,0:T(8,128)(2,1)S(1)}, u32[]{:S(2)}, u32[]{:S(2)}) collective-permute-start(bf16[1088,128]{1,0:T(8,128)(2,1)S(1)} %get-tuple-element.15), channel_id=1, source_target_pairs={{0,1},{1,2},{2,3},{3,4},{4,5},{5,6},{6,7},{7,8},{8,9},{9,10},{10,1... | collective-permute-start | bytes 835592 | tf_op jit(solution)/shard_map/ppermute | solution.py:30
  5.9 3.1 %collective-permute-start.1 = (bf16[1088,128]{1,0:T(8,128)(2,1)S(1)}, bf16[1088,128]{1,0:T(8,128)(2,1)S(1)}, u32[]{:S(2)}, u32[]{:S(2)}) collective-permute-start(bf16[1088,128]{1,0:T(8,128)(2,1)S(1)} %get-tuple-element.16), channel_id=1, source_target_pairs={{1,0},{2,1},{3,2},{4,3},{5,4},{6,5},{7,6},{8,7},{9,8},{10,9},{11,1... | collective-permute-start | bytes 835592 | tf_op jit(solution)/shard_map/ppermute | solution.py:30
  9.0 0.9 copy-done.5
  10.0 3.8 %inside1.1.partial = f32[4096,128]{1,0:T(8,128)S(1)} custom-call(s32[3,8]{1,0:T(4,128)S(1)} %bitcast.33, bf16[4096,128]{1,0:T(8,128)(2,1)S(1)} %bitcast.24, bf16[896,128]{1,0:T(8,128)(2,1)S(1)} %bitcast.28), custom_call_target="tpu_custom_call" | custom-call | tf_op jit(solution)/shard_map/inside1/pallas_call | solution.py:360
  13.8 3.3 %collective-permute-done.from_below = bf16[1088,128]{1,0:T(8,128)(2,1)S(1)} collective-permute-done((bf16[1088,128]{1,0:T(8,128)(2,1)S(1)}, bf16[1088,128]{1,0:T(8,128)(2,1)S(1)}, u32[]{:S(2)}, u32[]{:S(2)}) %collective-permute-start) | collective-permute-done | bytes 278560 | tf_op jit(solution)/shard_map/ppermute | solution.py:30
  17.1 3.1 %collective-permute-done.1.from_above = bf16[1088,128]{1,0:T(8,128)(2,1)S(1)} collective-permute-done((bf16[1088,128]{1,0:T(8,128)(2,1)S(1)}, bf16[1088,128]{1,0:T(8,128)(2,1)S(1)}, u32[]{:S(2)}, u32[]{:S(2)}) %collective-permute-start.1) | collective-permute-done | bytes 278560 | tf_op jit(solution)/shard_map/ppermute | solution.py:30
  20.2 1.3 %hidden.1 = (bf16[4096,128]{1,0:T(8,128)(2,1)S(1)}, bf16[1088,128]{1,0:T(8,128)(2,1)S(1)}, bf16[1088,128]{1,0:T(8,128)(2,1)S(1)}) custom-call(s32[3,8]{1,0:T(4,128)S(1)} %bitcast.34, f32[4096,128]{1,0:T(8,128)S(1)} %inside1.1.partial, bf16[1088,128]{1,0:T(8,128)(2,1)S(1)} %collective-permute-done.from_below, ...), custom_call_target="tpu_custom_call" | custom-call | tf_op jit(solution)/shard_map/hidden/pallas_call | solution.py:360
  21.4 1.9 %collective-permute-start.2 = (bf16[1088,128]{1,0:T(8,128)(2,1)S(1)}, bf16[1088,128]{1,0:T(8,128)(2,1)S(1)}, u32[]{:S(2)}, u32[]{:S(2)}) collective-permute-start(bf16[1088,128]{1,0:T(8,128)(2,1)S(1)} %get-tuple-element.18), channel_id=1, source_target_pairs={{0,1},{1,2},{2,3},{3,4},{4,5},{5,6},{6,7},{7,8},{8,9},{9,10},{10,1... | collective-permute-start | bytes 835592 | tf_op jit(solution)/shard_map/ppermute | solution.py:30
  23.4 4.3 %collective-permute-start.3 = (bf16[1088,128]{1,0:T(8,128)(2,1)S(1)}, bf16[1088,128]{1,0:T(8,128)(2,1)S(1)}, u32[]{:S(2)}, u32[]{:S(2)}) collective-permute-start(bf16[1088,128]{1,0:T(8,128)(2,1)S(1)} %get-tuple-element.19), channel_id=1, source_target_pairs={{1,0},{2,1},{3,2},{4,3},{5,4},{6,5},{7,6},{8,7},{9,8},{10,9},{11,1... | collective-permute-start | bytes 835592 | tf_op jit(solution)/shard_map/ppermute | solution.py:30
  27.7 3.8 %inside2.1.partial = f32[4096,128]{1,0:T(8,128)S(1)} custom-call(s32[3,8]{1,0:T(4,128)S(1)} %bitcast.35, bf16[4096,128]{1,0:T(8,128)(2,1)S(1)} %get-tuple-element.17.hidden, bf16[4096,128]{1,0:T(8,128)(2,1)S(1)} %bitcast.25, bf16[896,128]{1,0:T(8,128)(2,1)S(1)} %bitcast.30), custom_call_target="tpu_custom_call" | custom-call | tf_op jit(solution)/shard_map/inside2/pallas_call | solution.py:360
  32.0 6.8 %collective-permute-done.3.from_above = bf16[1088,128]{1,0:T(8,128)(2,1)S(1)} collective-permute-done((bf16[1088,128]{1,0:T(8,128)(2,1)S(1)}, bf16[1088,128]{1,0:T(8,128)(2,1)S(1)}, u32[]{:S(2)}, u32[]{:S(2)}) %collective-permute-start.3) | collective-permute-done | bytes 278560 | tf_op jit(solution)/shard_map/ppermute | solution.py:30
  38.8 3.3 %lift.1 = bf16[8,136,256]{2,1,0:T(8,128)(2,1)S(1)} custom-call(s32[3,8]{1,0:T(4,128)S(1)} %bitcast.36, s32[1,8]{1,0:T(1,128)S(1)} %bitcast.38, s32[1,8]{1,0:T(1,128)S(1)} %bitcast.39, s32[1,16]{1,0:T(1,128)S(1)} %copy-done.10, f32[4096,128]{1,0:T(8,128)S(1)} %inside2.1.partial, bf16[1088,128]{1,0:T(8,128)(2,1)S(1)} %collective-permute-done.2.from_below, ...), custom_call_target="tpu_custom_call" | custom-call | tf_op jit(solution)/shard_map/lift/pallas_call | solution.py:360
  42.1 19.2 %all_to_all.5.arrived = bf16[8,136,256]{2,1,0:T(8,128)(2,1)S(1)} all-to-all(bf16[8,136,256]{2,1,0:T(8,128)(2,1)S(1)} %lift.1), channel_id=1, replica_groups=mesh['gy'=4,'gx'=8] {'gx'}, dimensions={0} | all-to-all | bytes 1114112 | tf_op jit(solution)/shard_map/all_to_all | solution.py:431
  61.3 1.2 %gather.1 = (bf16[2048,256]{1,0:T(8,128)(2,1)S(1)}, bf16[64,256]{1,0:T(8,128)(2,1)S(1)}, bf16[64,256]{1,0:T(8,128)(2,1)}, bf16[2,64,256]{2,1,0:T(8,128)(2,1)S(1)}, bf16[2,64,256]{2,1,0:T(8,128)(2,1)S(1)}) custom-call(bf16[8,136,256]{2,1,0:T(8,128)(2,1)S(1)} %all_to_all.5.arrived), custom_call_target="tpu_custom_call" | custom-call | tf_op jit(solution)/shard_map/gather/pallas_call | solution.py:360
  63.1 4.3 %collective-permute-start.4 = (bf16[64,256]{1,0:T(8,128)(2,1)}, bf16[64,256]{1,0:T(8,128)(2,1)}, u32[]{:S(2)}, u32[]{:S(2)}) collective-permute-start(bf16[64,256]{1,0:T(8,128)(2,1)} %get-tuple-element.21), channel_id=1, source_target_pairs={{0,8},{8,16},{16,24},{1,9},{9,17},{17,25},{2,10},{10,18},{18,26},{... | collective-permute-start | bytes 98312 | tf_op jit(solution)/shard_map/ppermute | solution.py:30
  67.5 1.9 %collective-permute-start.5 = (bf16[64,256]{1,0:T(8,128)(2,1)}, bf16[64,256]{1,0:T(8,128)(2,1)S(1)}, u32[]{:S(2)}, u32[]{:S(2)}) collective-permute-start(bf16[64,256]{1,0:T(8,128)(2,1)} %copy-done.11), channel_id=1, source_target_pairs={{8,0},{16,8},{24,16},{9,1},{17,9},{25,17},{10,2},{18,10},{26,18},{... | collective-permute-start | bytes 98312 | tf_op jit(solution)/shard_map/ppermute | solution.py:30
  69.4 0.7 fusion
  70.2 2.8 %collective-permute-done.5.below = bf16[64,256]{1,0:T(8,128)(2,1)S(1)} collective-permute-done((bf16[64,256]{1,0:T(8,128)(2,1)}, bf16[64,256]{1,0:T(8,128)(2,1)S(1)}, u32[]{:S(2)}, u32[]{:S(2)}) %collective-permute-start.5) | collective-permute-done | bytes 32800 | tf_op jit(solution)/shard_map/ppermute | solution.py:30
  73.0 3.1 %collective-permute-start.7 = (bf16[2,68,256]{2,1,0:T(8,128)(2,1)S(1)}, bf16[2,68,256]{2,1,0:T(8,128)(2,1)S(1)}, u32[]{:S(2)}, u32[]{:S(2)}) collective-permute-start(bf16[2,68,256]{2,1,0:T(8,128)(2,1)S(1)} %pad_maximum_fusion.1), channel_id=1, source_target_pairs={{1,0},{2,1},{3,2},{4,3},{5,4},{6,5},{7,6},{9,8},{10,9},{11,10},{12... | collective-permute-start | bytes 208904 | tf_op jit(solution)/shard_map/ppermute | solution.py:30
  76.2 2.1 %collective-permute-start.6 = (bf16[2,68,256]{2,1,0:T(8,128)(2,1)S(1)}, bf16[2,68,256]{2,1,0:T(8,128)(2,1)S(1)}, u32[]{:S(2)}, u32[]{:S(2)}) collective-permute-start(bf16[2,68,256]{2,1,0:T(8,128)(2,1)S(1)} %pad_maximum_fusion), channel_id=1, source_target_pairs={{0,1},{1,2},{2,3},{3,4},{4,5},{5,6},{6,7},{8,9},{9,10},{10,11},{11... | collective-permute-start | bytes 208904 | tf_op jit(solution)/shard_map/ppermute | solution.py:30
  78.4 3.8 %collective-permute-done.6.left = bf16[2,68,256]{2,1,0:T(8,128)(2,1)S(1)} collective-permute-done((bf16[2,68,256]{2,1,0:T(8,128)(2,1)S(1)}, bf16[2,68,256]{2,1,0:T(8,128)(2,1)S(1)}, u32[]{:S(2)}, u32[]{:S(2)}) %collective-permute-start.6) | collective-permute-done | bytes 69664 | tf_op jit(solution)/shard_map/ppermute | solution.py:30
  82.2 11.1 %planes.1 = bf16[2048,256]{1,0:T(8,128)(2,1)} custom-call(s32[4]{0:T(128)S(1)} %add_convert_fusion.flags, bf16[2048,256]{1,0:T(8,128)(2,1)S(1)} %get-tuple-element.20.bev, bf16[64,256]{1,0:T(8,128)(2,1)} %collective-permute-done.4.above, bf16[64,256]{1,0:T(8,128)(2,1)S(1)} %collective-permute-done.5.below, ...), custom_call_target="tpu_custom_call" | custom-call | tf_op jit(solution)/shard_map/planes/pallas_call | solution.py:360
  (31 shorter events, 2.0 us)
Async XLA Ops:
  0.0 1.2 %copy-start = (bf16[8,512,128]{2,1,0:T(8,128)(2,1)S(1)}, bf16[8,512,128]{2,1,0:T(8,128)(2,1)}, u32[]{:S(2)}) copy-start(bf16[8,512,128]{2,1,0:T(8,128)(2,1)} %param.10) | copy-start | bytes 3145732
  1.2 0.7 copy-start.7
  2.8 14.3 %collective-permute-start = (bf16[1088,128]{1,0:T(8,128)(2,1)S(1)}, bf16[1088,128]{1,0:T(8,128)(2,1)S(1)}, u32[]{:S(2)}, u32[]{:S(2)}) collective-permute-start(bf16[1088,128]{1,0:T(8,128)(2,1)S(1)} %get-tuple-element.15), channel_id=1, source_target_pairs={{0,1},{1,2},{2,3},{3,4},{4,5},{5,6},{6,7},{7,8},{8,9},{9,10},{10,1... | collective-permute-start | bytes 835592 | tf_op jit(solution)/shard_map/ppermute | solution.py:30
  5.9 14.2 %collective-permute-start.1 = (bf16[1088,128]{1,0:T(8,128)(2,1)S(1)}, bf16[1088,128]{1,0:T(8,128)(2,1)S(1)}, u32[]{:S(2)}, u32[]{:S(2)}) collective-permute-start(bf16[1088,128]{1,0:T(8,128)(2,1)S(1)} %get-tuple-element.16), channel_id=1, source_target_pairs={{1,0},{2,1},{3,2},{4,3},{5,4},{6,5},{7,6},{8,7},{9,8},{10,9},{11,1... | collective-permute-start | bytes 835592 | tf_op jit(solution)/shard_map/ppermute | solution.py:30
  9.0 0.9 %copy-start.5 = (bf16[7,128,128]{2,1,0:T(8,128)(2,1)S(1)}, bf16[7,128,128]{2,1,0:T(8,128)(2,1)}, u32[]{:S(2)}) copy-start(bf16[7,128,128]{2,1,0:T(8,128)(2,1)} %param.15) | copy-start | bytes 688132
  13.8 13.9 %copy-start.1 = (bf16[8,512,128]{2,1,0:T(8,128)(2,1)S(1)}, bf16[8,512,128]{2,1,0:T(8,128)(2,1)}, u32[]{:S(2)}) copy-start(bf16[8,512,128]{2,1,0:T(8,128)(2,1)} %param.10) | copy-start | bytes 3145732
  13.8 13.9 %copy-start.6 = (bf16[7,128,128]{2,1,0:T(8,128)(2,1)S(1)}, bf16[7,128,128]{2,1,0:T(8,128)(2,1)}, u32[]{:S(2)}) copy-start(bf16[7,128,128]{2,1,0:T(8,128)(2,1)} %param.16) | copy-start | bytes 688132
  21.4 10.6 %collective-permute-start.2 = (bf16[1088,128]{1,0:T(8,128)(2,1)S(1)}, bf16[1088,128]{1,0:T(8,128)(2,1)S(1)}, u32[]{:S(2)}, u32[]{:S(2)}) collective-permute-start(bf16[1088,128]{1,0:T(8,128)(2,1)S(1)} %get-tuple-element.18), channel_id=1, source_target_pairs={{0,1},{1,2},{2,3},{3,4},{4,5},{5,6},{6,7},{7,8},{8,9},{9,10},{10,1... | collective-permute-start | bytes 835592 | tf_op jit(solution)/shard_map/ppermute | solution.py:30
  23.4 15.4 %collective-permute-start.3 = (bf16[1088,128]{1,0:T(8,128)(2,1)S(1)}, bf16[1088,128]{1,0:T(8,128)(2,1)S(1)}, u32[]{:S(2)}, u32[]{:S(2)}) collective-permute-start(bf16[1088,128]{1,0:T(8,128)(2,1)S(1)} %get-tuple-element.19), channel_id=1, source_target_pairs={{1,0},{2,1},{3,2},{4,3},{5,4},{6,5},{7,6},{8,7},{9,8},{10,9},{11,1... | collective-permute-start | bytes 835592 | tf_op jit(solution)/shard_map/ppermute | solution.py:30
  27.7 11.1 %copy-start.2 = (bf16[4,1024,256]{2,1,0:T(8,128)(2,1)S(1)}, bf16[4,1024,256]{2,1,0:T(8,128)(2,1)}, u32[]{:S(2)}) copy-start(bf16[4,1024,256]{2,1,0:T(8,128)(2,1)} %height.1) | copy-start | bytes 6291460
  27.7 11.1 %copy-start.8 = (s32[8]{0:T(128)S(1)}, s32[8]{0:T(128)}, u32[]{:S(2)}) copy-start(s32[8]{0:T(128)} %param.12) | copy-start | bytes 100
  27.7 11.1 %copy-start.9 = (s32[8]{0:T(128)S(1)}, s32[8]{0:T(128)}, u32[]{:S(2)}) copy-start(s32[8]{0:T(128)} %param.13) | copy-start | bytes 100
  27.7 11.1 %copy-start.10 = (s32[1,16]{1,0:T(1,128)S(1)}, s32[1,16]{1,0:T(1,128)}, u32[]{:S(2)}) copy-start(s32[1,16]{1,0:T(1,128)} %columns.1) | copy-start | bytes 196
  38.8 43.4 %copy-start.4 = (bf16[3,3,256,256]{3,2,1,0:T(8,128)(2,1)S(1)}, bf16[3,3,256,256]{3,2,1,0:T(8,128)(2,1)}, u32[]{:S(2)}) copy-start(bf16[3,3,256,256]{3,2,1,0:T(8,128)(2,1)} %param.19) | copy-start | bytes 3538948
  42.1 40.1 %copy-start.3 = (bf16[3,3,256,256]{3,2,1,0:T(8,128)(2,1)S(1)}, bf16[3,3,256,256]{3,2,1,0:T(8,128)(2,1)}, u32[]{:S(2)}) copy-start(bf16[3,3,256,256]{3,2,1,0:T(8,128)(2,1)} %param.18) | copy-start | bytes 3538948
  62.5 0.6 copy-start.11
  63.1 6.3 %collective-permute-start.4 = (bf16[64,256]{1,0:T(8,128)(2,1)}, bf16[64,256]{1,0:T(8,128)(2,1)}, u32[]{:S(2)}, u32[]{:S(2)}) collective-permute-start(bf16[64,256]{1,0:T(8,128)(2,1)} %get-tuple-element.21), channel_id=1, source_target_pairs={{0,8},{8,16},{16,24},{1,9},{9,17},{17,25},{2,10},{10,18},{18,26},{... | collective-permute-start | bytes 98312 | tf_op jit(solution)/shard_map/ppermute | solution.py:30
  67.5 5.4 %collective-permute-start.5 = (bf16[64,256]{1,0:T(8,128)(2,1)}, bf16[64,256]{1,0:T(8,128)(2,1)S(1)}, u32[]{:S(2)}, u32[]{:S(2)}) collective-permute-start(bf16[64,256]{1,0:T(8,128)(2,1)} %copy-done.11), channel_id=1, source_target_pairs={{8,0},{16,8},{24,16},{9,1},{17,9},{25,17},{10,2},{18,10},{26,18},{... | collective-permute-start | bytes 98312 | tf_op jit(solution)/shard_map/ppermute | solution.py:30
  73.0 5.4 %collective-permute-start.7 = (bf16[2,68,256]{2,1,0:T(8,128)(2,1)S(1)}, bf16[2,68,256]{2,1,0:T(8,128)(2,1)S(1)}, u32[]{:S(2)}, u32[]{:S(2)}) collective-permute-start(bf16[2,68,256]{2,1,0:T(8,128)(2,1)S(1)} %pad_maximum_fusion.1), channel_id=1, source_target_pairs={{1,0},{2,1},{3,2},{4,3},{5,4},{6,5},{7,6},{9,8},{10,9},{11,10},{12... | collective-permute-start | bytes 208904 | tf_op jit(solution)/shard_map/ppermute | solution.py:30
  76.2 6.0 %collective-permute-start.6 = (bf16[2,68,256]{2,1,0:T(8,128)(2,1)S(1)}, bf16[2,68,256]{2,1,0:T(8,128)(2,1)S(1)}, u32[]{:S(2)}, u32[]{:S(2)}) collective-permute-start(bf16[2,68,256]{2,1,0:T(8,128)(2,1)S(1)} %pad_maximum_fusion), channel_id=1, source_target_pairs={{0,1},{1,2},{2,3},{3,4},{4,5},{5,6},{6,7},{8,9},{9,10},{10,11},{11... | collective-permute-start | bytes 208904 | tf_op jit(solution)/shard_map/ppermute | solution.py:30

commit v3 on v2

--- a/solution.py
+++ b/solution.py
@@ -225,134 +225,151 @@
     return [(h, slice(h * LANES, (h + 1) * LANES)) for h in range(channels // LANES)]
 
 
-PITCH = COLS + 2 * EDGE
 WIDE_ROWS = ROWS + 2 * HALO
 MID_ROWS = ROWS + HALO
 RIM_ROWS = 72
-
-
-def side_shifts(padded, before, after, count):
-    def one(y, carry):
-        at = pl.multiple_of(y * PITCH, EDGE)
-        to = pl.multiple_of(y * COLS, COLS)
-        for h, lanes in halves(before.shape[1]):
-            before[pl.ds(to, COLS), lanes] = padded[h, pl.ds(at + EDGE - 1, COLS), :].astype(BF16)
-            after[pl.ds(to, COLS), lanes] = padded[h, pl.ds(at + EDGE + 1, COLS), :].astype(BF16)
-        return carry
-
-    lax.fori_loop(0, count, one, 0)
-
-
-def stacked(sources, first_row, row_count):
+INNER_ROWS = ROWS - 2
+CORE_ROWS = ROWS - 4
+
+
+def tap_columns(weights, dx):
+    return jnp.concatenate([weights[dy * 3 + dx] for dy in range(3)], 0)
+
+
+def three_rows(source, first_row, row_count):
     parts = []
     for dy in range(3):
-        for source in sources:
-            at = pl.multiple_of((first_row + dy) * COLS, COLS)
-            parts.append(source[pl.ds(at, row_count * COLS), :])
+        at = pl.multiple_of((first_row + dy) * COLS, COLS)
+        parts.append(source[pl.ds(at, row_count * COLS), :])
     return jnp.concatenate(parts, 1)
 
 
-def plane_kernel(
+def rows_conv(lhs, weights):
+    count = lhs.shape[0]
+    x = lax.rem(lax.broadcasted_iota(jnp.int32, (count, weights.shape[2]), 0), COLS)
+    from_left = mm(lhs, tap_columns(weights, 0))
+    total = jnp.where(x == 0, 0.0, pltpu.roll(from_left, 1, 0))
+    total = total + mm(lhs, tap_columns(weights, 1))
+    from_right = mm(lhs, tap_columns(weights, 2))
+    return total + jnp.where(x == COLS - 1, 0.0, pltpu.roll(from_right, count - 1, 0))
+
+
+def without_sides(block):
+    x = lax.rem(lax.broadcasted_iota(jnp.int32, block.shape, 0), COLS)
+    return jnp.where((x == 0) | (x == COLS - 1), 0.0, block)
+
+
+def first_inner_kernel(bev, weights, inner):
+    step = INNER_ROWS // 2
+
+    def one(i, carry):
+        block = jnp.maximum(rows_conv(three_rows(bev, i * step, step), weights), 0.0)
+        at = pl.multiple_of(i * step * COLS, COLS)
+        inner[pl.ds(at, step * COLS), :] = without_sides(block).astype(BF16)
+        return carry
+
+    lax.fori_loop(0, INNER_ROWS // step, one, 0)
+
+
+def second_core_kernel(inner, bev, weights, core):
+    step = CORE_ROWS // 4
+
+    def one(i, carry):
+        block = rows_conv(three_rows(inner, i * step, step), weights)
+        at = pl.multiple_of((i * step + 2) * COLS, COLS)
+        block = block + bev[pl.ds(at, step * COLS), :].astype(F32)
+        to = pl.multiple_of(i * step * COLS, COLS)
+        for h, lanes in halves(block.shape[1]):
+            core[h, pl.ds(to, step * COLS), :] = block[:, lanes]
+        return carry
+
+    lax.fori_loop(0, CORE_ROWS // step, one, 0)
+
+
+def edges_kernel(
     flags,
     bev,
+    inner,
+    core,
     above,
     below,
+    own_left,
+    own_right,
     left,
     right,
     weights_first,
     weights_second,
     out,
-    padded,
-    before,
-    centre,
-    after,
-    rim,
+    sides,
+    total,
 ):
     ch = bev.shape[1]
-    centre[0 : HALO * COLS, :] = above[...]
-    centre[HALO * COLS : (HALO + ROWS) * COLS, :] = bev[...]
-    centre[(HALO + ROWS) * COLS : WIDE_ROWS * COLS, :] = below[...]
-
-    def widen(y, carry):
-        at = pl.multiple_of(y * PITCH + EDGE, EDGE)
-        row = centre[pl.ds(pl.multiple_of(y * COLS, COLS), COLS), :].astype(F32)
-        for h, lanes in halves(ch):
-            padded[h, pl.ds(at, COLS), :] = row[:, lanes]
-        return carry
-
-    lax.fori_loop(0, WIDE_ROWS, widen, 0)
-    rim[...] = jnp.zeros_like(rim)
-    for x in range(HALO):
-        lefts = left[x, :, :].astype(F32)
-        rights = right[x, :, :].astype(F32)
-        rim[x, 0:WIDE_ROWS, :] = lefts
-        rim[4 + x, 0:WIDE_ROWS, :] = rights
-    for h, lanes in halves(ch):
-        own_left = padded[h, pl.ds(EDGE, WIDE_ROWS, stride=PITCH), :]
-        own_right = padded[h, pl.ds(EDGE + COLS - 1, WIDE_ROWS, stride=PITCH), :]
-        rim[2, 0:WIDE_ROWS, lanes] = own_left
-        rim[3, 0:WIDE_ROWS, lanes] = own_right
-        padded[h, pl.ds(EDGE - 1, WIDE_ROWS, stride=PITCH), :] = rim[1, 0:WIDE_ROWS, lanes]
-        padded[h, pl.ds(EDGE + COLS, WIDE_ROWS, stride=PITCH), :] = rim[4, 0:WIDE_ROWS, lanes]
-    side_shifts(padded, before, after, WIDE_ROWS)
-
-    rim_first = []
-    for sources in ((0, 1, 2), (3, 4, 5)):
+    two = HALO * COLS
+    four = 2 * two
+    sides[...] = jnp.zeros_like(sides)
+    for base, source in ((0, left), (2, own_left), (4, own_right), (6, right)):
+        for x in range(HALO):
+            sides[base + x, 0:WIDE_ROWS, :] = source[x, :, :].astype(F32)
+    lhs = []
+    for start in (0, 1, 4, 5):
         parts = []
         for dy in range(3):
-            for s in sources:
-                parts.append(rim[s, dy : dy + RIM_ROWS, :].astype(BF16))
-        rim_first.append(jnp.concatenate(parts, 1))
-    rim_out = mm(jnp.concatenate(rim_first, 0), weights_first[...])
-    rim_out = jnp.maximum(rim_out, 0.0)
+            for dx in range(3):
+                parts.append(sides[start + dx, dy : dy + RIM_ROWS, :].astype(BF16))
+        lhs.append(jnp.concatenate(parts, 1))
+    taps = jnp.concatenate([weights_first[t] for t in range(9)], 0)
+    columns = jnp.maximum(mm(jnp.concatenate(lhs, 0), taps), 0.0)
     row_at = lax.broadcasted_iota(jnp.int32, (RIM_ROWS, ch), 0)
-    inside = jnp.where(
-        row_at == 0, flags[0], jnp.where(row_at == MID_ROWS - 1, flags[1], 1)
-    ).astype(F32)
-    rim_left = rim_out[0:RIM_ROWS, :] * inside * flags[2].astype(F32)
-    rim_right = rim_out[RIM_ROWS:, :] * inside * flags[3].astype(F32)
-
-    step = MID_ROWS // 6
-
-    def first_rows(i, carry):
-        y = i * step
-        block = mm(stacked((before, centre, after), y, step), weights_first[...])
-        block = jnp.maximum(block, 0.0)
-        for r in range(step):
-            keep = jnp.where(
-                y + r == 0, flags[0], jnp.where(y + r == MID_ROWS - 1, flags[1], 1)
-            ).astype(F32)
-            at = pl.multiple_of((y + r) * PITCH + EDGE, EDGE)
-            row = block[r * COLS : (r + 1) * COLS, :] * keep
-            for h, lanes in halves(ch):
-                padded[h, pl.ds(at, COLS), :] = row[:, lanes]
-        return carry
-
-    lax.fori_loop(0, MID_ROWS // step, first_rows, 0)
+    keep = jnp.where(row_at == 0, flags[0], jnp.where(row_at == MID_ROWS - 1, flags[1], 1)).astype(
+        F32
+    )
+    for k, side_keep in enumerate((flags[2], 1, 1, flags[3])):
+        block = columns[k * RIM_ROWS : (k + 1) * RIM_ROWS, :] * keep
+        if k in (0, 3):
+            block = block * side_keep.astype(F32)
+        sides[k, 0:RIM_ROWS, :] = block
+
+    high = jnp.concatenate([above[...], bev[0:two, :]], 0)
+    low = jnp.concatenate([bev[ROWS * COLS - two :, :], below[...]], 0)
+
+    def strips(upper, lower):
+        parts = []
+        for source in (upper, lower):
+            rows = [source[dy * COLS : dy * COLS + two] for dy in range(3)]
+            parts.append(jnp.concatenate(rows, 1))
+        return jnp.concatenate(parts, 0)
+
+    strip = without_sides(jnp.maximum(rows_conv(strips(high, low), weights_first), 0.0))
+    line = lax.broadcasted_iota(jnp.int32, (four, ch), 0) // COLS
+    keep = jnp.where(line == 0, flags[0], jnp.where(line == 3, flags[1], 1)).astype(F32)
+    strip = (strip * keep).astype(BF16)
+
+    high = jnp.concatenate([strip[0:two], inner[0:two, :]], 0)
+    low = jnp.concatenate([inner[INNER_ROWS * COLS - two :, :], strip[two:]], 0)
+    strip = rows_conv(strips(high, low), weights_second)
     for h, lanes in halves(ch):
-        padded[h, pl.ds(EDGE - 1, MID_ROWS, stride=PITCH), :] = rim_left[0:MID_ROWS, lanes]
-        padded[h, pl.ds(EDGE + COLS, MID_ROWS, stride=PITCH), :] = rim_right[0:MID_ROWS, lanes]
-    side_shifts(padded, before, after, MID_ROWS)
-
-    def narrow(y, carry):
-        at = pl.multiple_of(y * PITCH + EDGE, EDGE)
-        to = pl.multiple_of(y * COLS, COLS)
+        top_rows = strip[0:two, lanes] + bev[0:two, lanes].astype(F32)
+        low_rows = strip[two:, lanes] + bev[ROWS * COLS - two :, lanes].astype(F32)
+        total[h, 0:two, :] = top_rows
+        total[h, two : ROWS * COLS - two, :] = core[h, :, :]
+        total[h, ROWS * COLS - two :, :] = low_rows
+
+    column = []
+    for k in range(4):
+        rows = [sides[k, dy : dy + ROWS, :].astype(BF16) for dy in range(3)]
+        column.append(jnp.concatenate(rows, 1))
+    w0, w1, w2 = [tap_columns(weights_second, dx) for dx in range(3)]
+    added = (
+        (0, mm(column[0], w0) + mm(column[1], w1)),
+        (1, mm(column[1], w0)),
+        (COLS - 2, mm(column[2], w2)),
+        (COLS - 1, mm(column[2], w1) + mm(column[3], w2)),
+    )
+    for x, block in added:
         for h, lanes in halves(ch):
-            centre[pl.ds(to, COLS), lanes] = padded[h, pl.ds(at, COLS), :].astype(BF16)
-        return carry
-
-    lax.fori_loop(0, MID_ROWS, narrow, 0)
-    step2 = 16
-
-    def second_rows(i, carry):
-        y = i * step2
-        block = mm(stacked((before, centre, after), y, step2), weights_second[...])
-        at = pl.multiple_of(y * COLS, COLS)
-        own = bev[pl.ds(at, step2 * COLS), :].astype(F32)
-        out[pl.ds(at, step2 * COLS), :] = (block + own).astype(BF16)
-        return carry
-
-    lax.fori_loop(0, ROWS // step2, second_rows, 0)
+            total[h, pl.ds(x, ROWS, stride=COLS), :] += block[:, lanes]
+    for h, lanes in halves(ch):
+        out[:, lanes] = total[h].astype(BF16)
 
 
 def call(kernel, name, out_shape, scalars, arrays, scratch=(), mib=12):
@@ -390,8 +407,8 @@
     x = features.reshape(rows, ch)
     w_first = conv_first.reshape(-1, ch)
     w_second = conv_second.reshape(-1, ch)
-    k_first = plane_first.reshape(-1, mapped)
-    k_second = plane_second.reshape(-1, mapped)
+    k_first = plane_first.reshape(9, mapped, mapped)
+    k_second = plane_second.reshape(9, mapped, mapped)
     slots = block_slot.reshape(1, count)
     block_levels = block_level.reshape(1, count)
     both = ("gy", "gx")
@@ -448,6 +465,14 @@
     )
     above = shift(bottom, "gy", 1)
     below = shift(top, "gy", -1)
+    inner = call(
+        first_inner_kernel,
+        "first_inner",
+        jax.ShapeDtypeStruct((INNER_ROWS * COLS, mapped), BF16),
+        (),
+        (bev, k_first),
+    )
+    above, below, inner = lax.optimization_barrier((above, below, inner))
     corner_above = above.reshape(HALO, COLS, mapped)
     corner_below = below.reshape(HALO, COLS, mapped)
 
@@ -461,26 +486,42 @@
             1,
         )
 
-    from_left = shift(side(right, COLS - HALO), "gx", 1)
-    from_right = shift(side(left, 0), "gx", -1)
+    own_left, own_right = side(left, 0), side(right, COLS - HALO)
+    from_left = shift(own_right, "gx", 1)
+    from_right = shift(own_left, "gx", -1)
+    core = call(
+        second_core_kernel,
+        "second_core",
+        jax.ShapeDtypeStruct((mapped // LANES, CORE_ROWS * COLS, LANES), F32),
+        (),
+        (inner, bev, k_second),
+    )
     gy, gx = lax.axis_index("gy"), lax.axis_index("gx")
     flags = jnp.stack(
         [gy > 0, gy < lax.axis_size("gy") - 1, gx > 0, gx < peers - 1]
     ).astype(jnp.int32)
     out = call(
-        plane_kernel,
-        "planes",
+        edges_kernel,
+        "edges",
         jax.ShapeDtypeStruct((ROWS * COLS, mapped), BF16),
         (flags,),
-        (bev, above, below, from_left, from_right, k_first, k_second),
         (
-            pltpu.VMEM((mapped // LANES, WIDE_ROWS * PITCH, LANES), F32),
-            pltpu.VMEM((WIDE_ROWS * COLS, mapped), BF16),
-            pltpu.VMEM((WIDE_ROWS * COLS, mapped), BF16),
-            pltpu.VMEM((WIDE_ROWS * COLS, mapped), BF16),
-            pltpu.VMEM((6, RIM_ROWS + EDGE, mapped), F32),
+            bev,
+            inner,
+            core,
+            above,
+            below,
+            own_left,
+            own_right,
+            from_left,
+            from_right,
+            k_first,
+            k_second,
         ),
-        mib=20,
+        (
+            pltpu.VMEM((8, RIM_ROWS + EDGE, mapped), F32),
+            pltpu.VMEM((mapped // LANES, ROWS * COLS, LANES), F32),
+        ),
     )
     return out.reshape(ROWS, COLS, mapped)
 

time: 93.8 us -> 88.1 us (0.939)
  waiting for transfers between devices: 20.1 us -> 14.5 us
  Pallas kernels: 25.4 us -> 23.9 us
    ppermute x8, waiting for transfers between devices: 20.1 us -> 14.5 us  [shift(): return lax.ppermute(block, axis, route)]
    pallas_call x7 -> x9, Pallas kernels: 25.4 us -> 23.9 us  [call(): pl.pallas_call(kernel, name=name, out_shape=out_shape, in_specs=[SMEM] *...]
    unnamed x24 -> x22, local copies, waits for them, and re-layouts: 3.49 us -> 2.89 us
  transfers between devices with their start and end apart: 8 -> 8, of which waited for: 6 -> 5; matrix products, arithmetic and copies ran while one was open for 1% -> 0% of each run, Pallas kernels for 8% -> 15%
where the time goes in v3:
time: 88.1 us; the launch traced here: 87.2 us
  starting transfers between devices  24.8 us (28%)
  Pallas kernels  23.9 us (27%)
  blocking collectives  19.2 us (22%)
  waiting for transfers between devices  14.5 us (16%)
  local copies, waits for them, and re-layouts  4.34 us (5%)
    ppermute x8, starting transfers between devices, shift(): return lax.ppermute(block, axis, route)  24.8 us
    pallas_call x9, Pallas kernels, call(): pl.pallas_call(kernel, name=name, out_shape=out_shape, in_specs=[SMEM] *...  23.9 us
    all_to_all x1, blocking collectives, local(): lax.all_to_all(outgoing, 'gx', split_axis=0, concat_axis=0, tiled=True)  19.2 us
    ppermute x8, waiting for transfers between devices, shift(): return lax.ppermute(block, axis, route)  14.5 us
    unnamed x22, local copies, waits for them, and re-layouts  2.89 us
  transfers between devices with their start and end apart: 8, of which 5 were waited for; matrix products, arithmetic and copies ran while one was open for 0% of the time, Pallas kernels for 15%

profile of v3, /device:TPU:9, one launch (start us, length us, event | category | flops | bytes accessed | tf_op | source)
XLA Modules:
  0.0 87.2 jit_solution(13515148945207917884)
XLA Ops:
  0.0 1.2 %copy-done = bf16[8,512,128]{2,1,0:T(8,128)(2,1)S(1)} copy-done((bf16[8,512,128]{2,1,0:T(8,128)(2,1)S(1)}, bf16[8,512,128]{2,1,0:T(8,128)(2,1)}, u32[]{:S(2)}) %copy-start) | copy-done | bytes 1048600
  1.9 0.9 %pack.1 = (bf16[1088,128]{1,0:T(8,128)(2,1)S(1)}, bf16[1088,128]{1,0:T(8,128)(2,1)S(1)}) custom-call(s32[3,8]{1,0:T(4,128)S(1)} %bitcast.34, bf16[4096,128]{1,0:T(8,128)(2,1)S(1)} %bitcast.23), custom_call_target="tpu_custom_call" | custom-call | tf_op jit(solution)/shard_map/pack/pallas_call | solution.py:377
  2.8 3.1 %collective-permute-start = (bf16[1088,128]{1,0:T(8,128)(2,1)S(1)}, bf16[1088,128]{1,0:T(8,128)(2,1)S(1)}, u32[]{:S(2)}, u32[]{:S(2)}) collective-permute-start(bf16[1088,128]{1,0:T(8,128)(2,1)S(1)} %get-tuple-element.18), channel_id=1, source_target_pairs={{0,1},{1,2},{2,3},{3,4},{4,5},{5,6},{6,7},{7,8},{8,9},{9,10},{10,1... | collective-permute-start | bytes 835592 | tf_op jit(solution)/shard_map/ppermute | solution.py:30
  5.9 3.1 %collective-permute-start.1 = (bf16[1088,128]{1,0:T(8,128)(2,1)S(1)}, bf16[1088,128]{1,0:T(8,128)(2,1)S(1)}, u32[]{:S(2)}, u32[]{:S(2)}) collective-permute-start(bf16[1088,128]{1,0:T(8,128)(2,1)S(1)} %get-tuple-element.19), channel_id=1, source_target_pairs={{1,0},{2,1},{3,2},{4,3},{5,4},{6,5},{7,6},{8,7},{9,8},{10,9},{11,1... | collective-permute-start | bytes 835592 | tf_op jit(solution)/shard_map/ppermute | solution.py:30
  9.0 0.9 %copy-done.5 = bf16[7,128,128]{2,1,0:T(8,128)(2,1)S(1)} copy-done((bf16[7,128,128]{2,1,0:T(8,128)(2,1)S(1)}, bf16[7,128,128]{2,1,0:T(8,128)(2,1)}, u32[]{:S(2)}) %copy-start.5) | copy-done | bytes 229400
  10.0 3.8 %inside1.1.partial = f32[4096,128]{1,0:T(8,128)S(1)} custom-call(s32[3,8]{1,0:T(4,128)S(1)} %bitcast.35, bf16[4096,128]{1,0:T(8,128)(2,1)S(1)} %bitcast.24, bf16[896,128]{1,0:T(8,128)(2,1)S(1)} %bitcast.30), custom_call_target="tpu_custom_call" | custom-call | tf_op jit(solution)/shard_map/inside1/pallas_call | solution.py:377
  13.8 3.3 %collective-permute-done.from_below = bf16[1088,128]{1,0:T(8,128)(2,1)S(1)} collective-permute-done((bf16[1088,128]{1,0:T(8,128)(2,1)S(1)}, bf16[1088,128]{1,0:T(8,128)(2,1)S(1)}, u32[]{:S(2)}, u32[]{:S(2)}) %collective-permute-start) | collective-permute-done | bytes 278560 | tf_op jit(solution)/shard_map/ppermute | solution.py:30
  17.1 3.1 %collective-permute-done.1.from_above = bf16[1088,128]{1,0:T(8,128)(2,1)S(1)} collective-permute-done((bf16[1088,128]{1,0:T(8,128)(2,1)S(1)}, bf16[1088,128]{1,0:T(8,128)(2,1)S(1)}, u32[]{:S(2)}, u32[]{:S(2)}) %collective-permute-start.1) | collective-permute-done | bytes 278560 | tf_op jit(solution)/shard_map/ppermute | solution.py:30
  20.2 1.3 %hidden.1 = (bf16[4096,128]{1,0:T(8,128)(2,1)S(1)}, bf16[1088,128]{1,0:T(8,128)(2,1)S(1)}, bf16[1088,128]{1,0:T(8,128)(2,1)S(1)}) custom-call(s32[3,8]{1,0:T(4,128)S(1)} %bitcast.36, f32[4096,128]{1,0:T(8,128)S(1)} %inside1.1.partial, bf16[1088,128]{1,0:T(8,128)(2,1)S(1)} %collective-permute-done.from_below, ...), custom_call_target="tpu_custom_call" | custom-call | tf_op jit(solution)/shard_map/hidden/pallas_call | solution.py:377
  21.5 1.9 %collective-permute-start.2 = (bf16[1088,128]{1,0:T(8,128)(2,1)S(1)}, bf16[1088,128]{1,0:T(8,128)(2,1)S(1)}, u32[]{:S(2)}, u32[]{:S(2)}) collective-permute-start(bf16[1088,128]{1,0:T(8,128)(2,1)S(1)} %get-tuple-element.21), channel_id=1, source_target_pairs={{0,1},{1,2},{2,3},{3,4},{4,5},{5,6},{6,7},{7,8},{8,9},{9,10},{10,1... | collective-permute-start | bytes 835592 | tf_op jit(solution)/shard_map/ppermute | solution.py:30
  23.4 4.3 %collective-permute-start.3 = (bf16[1088,128]{1,0:T(8,128)(2,1)S(1)}, bf16[1088,128]{1,0:T(8,128)(2,1)S(1)}, u32[]{:S(2)}, u32[]{:S(2)}) collective-permute-start(bf16[1088,128]{1,0:T(8,128)(2,1)S(1)} %get-tuple-element.22), channel_id=1, source_target_pairs={{1,0},{2,1},{3,2},{4,3},{5,4},{6,5},{7,6},{8,7},{9,8},{10,9},{11,1... | collective-permute-start | bytes 835592 | tf_op jit(solution)/shard_map/ppermute | solution.py:30
  27.7 3.8 %inside2.1.partial = f32[4096,128]{1,0:T(8,128)S(1)} custom-call(s32[3,8]{1,0:T(4,128)S(1)} %bitcast.37, bf16[4096,128]{1,0:T(8,128)(2,1)S(1)} %get-tuple-element.20.hidden, bf16[4096,128]{1,0:T(8,128)(2,1)S(1)} %bitcast.25, bf16[896,128]{1,0:T(8,128)(2,1)S(1)} %bitcast.32), custom_call_target="tpu_custom_call" | custom-call | tf_op jit(solution)/shard_map/inside2/pallas_call | solution.py:377
  32.0 6.8 %collective-permute-done.3.from_above = bf16[1088,128]{1,0:T(8,128)(2,1)S(1)} collective-permute-done((bf16[1088,128]{1,0:T(8,128)(2,1)S(1)}, bf16[1088,128]{1,0:T(8,128)(2,1)S(1)}, u32[]{:S(2)}, u32[]{:S(2)}) %collective-permute-start.3) | collective-permute-done | bytes 278560 | tf_op jit(solution)/shard_map/ppermute | solution.py:30
  38.8 3.3 %lift.1 = bf16[8,136,256]{2,1,0:T(8,128)(2,1)S(1)} custom-call(s32[3,8]{1,0:T(4,128)S(1)} %bitcast.38, s32[1,8]{1,0:T(1,128)S(1)} %bitcast.39, s32[1,8]{1,0:T(1,128)S(1)} %bitcast.40, s32[1,16]{1,0:T(1,128)S(1)} %copy-done.10, f32[4096,128]{1,0:T(8,128)S(1)} %inside2.1.partial, bf16[1088,128]{1,0:T(8,128)(2,1)S(1)} %collective-permute-done.2.from_below, ...), custom_call_target="tpu_custom_call" | custom-call | tf_op jit(solution)/shard_map/lift/pallas_call | solution.py:377
  42.1 19.2 %all_to_all.5.arrived = bf16[8,136,256]{2,1,0:T(8,128)(2,1)S(1)} all-to-all(bf16[8,136,256]{2,1,0:T(8,128)(2,1)S(1)} %lift.1), channel_id=1, replica_groups=mesh['gy'=4,'gx'=8] {'gx'}, dimensions={0} | all-to-all | bytes 1114112 | tf_op jit(solution)/shard_map/all_to_all | solution.py:448
  61.3 1.2 %gather.1 = (bf16[2048,256]{1,0:T(8,128)(2,1)S(1)}, bf16[64,256]{1,0:T(8,128)(2,1)}, bf16[64,256]{1,0:T(8,128)(2,1)}, bf16[2,64,256]{2,1,0:T(8,128)(2,1)S(1)}, bf16[2,64,256]{2,1,0:T(8,128)(2,1)S(1)}) custom-call(bf16[8,136,256]{2,1,0:T(8,128)(2,1)S(1)} %all_to_all.5.arrived), custom_call_target="tpu_custom_call" | custom-call | tf_op jit(solution)/shard_map/gather/pallas_call | solution.py:377
  62.5 4.3 %collective-permute-start.4 = (bf16[64,256]{1,0:T(8,128)(2,1)}, bf16[64,256]{1,0:T(8,128)(2,1)}, u32[]{:S(2)}, u32[]{:S(2)}) collective-permute-start(bf16[64,256]{1,0:T(8,128)(2,1)} %get-tuple-element.24), channel_id=1, source_target_pairs={{0,8},{8,16},{16,24},{1,9},{9,17},{17,25},{2,10},{10,18},{18,26},{... | collective-permute-start | bytes 98312 | tf_op jit(solution)/shard_map/ppermute | solution.py:30
  66.9 1.9 %collective-permute-start.5 = (bf16[64,256]{1,0:T(8,128)(2,1)}, bf16[64,256]{1,0:T(8,128)(2,1)}, u32[]{:S(2)}, u32[]{:S(2)}) collective-permute-start(bf16[64,256]{1,0:T(8,128)(2,1)} %get-tuple-element.25), channel_id=1, source_target_pairs={{8,0},{16,8},{24,16},{9,1},{17,9},{25,17},{10,2},{18,10},{26,18},{... | collective-permute-start | bytes 98312 | tf_op jit(solution)/shard_map/ppermute | solution.py:30
  68.8 2.7 %first_inner.1.inner = bf16[1984,256]{1,0:T(8,128)(2,1)S(1)} custom-call(bf16[2048,256]{1,0:T(8,128)(2,1)S(1)} %get-tuple-element.23.bev, bf16[9,256,256]{2,1,0:T(8,128)(2,1)S(1)} %bitcast.26), custom_call_target="tpu_custom_call" | custom-call | tf_op jit(solution)/shard_map/first_inner/pallas_call | solution.py:377
  71.6 0.9 collective-permute-done.5.below
  73.9 2.1 %collective-permute-start.6 = (bf16[2,68,256]{2,1,0:T(8,128)(2,1)S(1)}, bf16[2,68,256]{2,1,0:T(8,128)(2,1)S(1)}, u32[]{:S(2)}, u32[]{:S(2)}) collective-permute-start(bf16[2,68,256]{2,1,0:T(8,128)(2,1)S(1)} %pad_maximum_fusion.1.own_right), channel_id=1, source_target_pairs={{0,1},{1,2},{2,3},{3,4},{4,5},{5,6},{6,7},{8,9},{9,10},{10,11},{11... | collective-permute-start | bytes 208904 | tf_op jit(solution)/shard_map/ppermute | solution.py:30
  76.1 4.0 %collective-permute-start.7 = (bf16[2,68,256]{2,1,0:T(8,128)(2,1)S(1)}, bf16[2,68,256]{2,1,0:T(8,128)(2,1)S(1)}, u32[]{:S(2)}, u32[]{:S(2)}) collective-permute-start(bf16[2,68,256]{2,1,0:T(8,128)(2,1)S(1)} %pad_maximum_fusion.own_left), channel_id=1, source_target_pairs={{1,0},{2,1},{3,2},{4,3},{5,4},{6,5},{7,6},{9,8},{10,9},{11,10},{12... | collective-permute-start | bytes 208904 | tf_op jit(solution)/shard_map/ppermute | solution.py:30
  80.2 3.0 %second_core.1.core = f32[2,1920,128]{2,1,0:T(8,128)S(1)} custom-call(bf16[1984,256]{1,0:T(8,128)(2,1)S(1)} %first_inner.1.inner, bf16[2048,256]{1,0:T(8,128)(2,1)S(1)} %get-tuple-element.23.bev, bf16[9,256,256]{2,1,0:T(8,128)(2,1)S(1)} %bitcast.28), custom_call_target="tpu_custom_call" | custom-call | tf_op jit(solution)/shard_map/second_core/pallas_call | solution.py:377
  83.3 3.9 %edges.1 = bf16[2048,256]{1,0:T(8,128)(2,1)} custom-call(s32[4]{0:T(128)S(1)} %add_convert_fusion.flags, bf16[2048,256]{1,0:T(8,128)(2,1)S(1)} %get-tuple-element.23.bev, bf16[1984,256]{1,0:T(8,128)(2,1)S(1)} %first_inner.1.inner, f32[2,1920,128]{2,1,0:T(8,128)S(1)} %second_core.1.core, bf16[64,256]{1,0:T(8,128)(2,1)} %collective-permute-done.4.above, ...), custom_call_target="tpu_custom_call" | custom-call | tf_op jit(solution)/shard_map/edges/pallas_call | solution.py:377
  (31 shorter events, 2.8 us)
Async XLA Ops:
  0.0 1.2 %copy-start = (bf16[8,512,128]{2,1,0:T(8,128)(2,1)S(1)}, bf16[8,512,128]{2,1,0:T(8,128)(2,1)}, u32[]{:S(2)}) copy-start(bf16[8,512,128]{2,1,0:T(8,128)(2,1)} %param.10) | copy-start | bytes 3145732
  1.2 0.7 copy-start.7
  2.8 14.3 %collective-permute-start = (bf16[1088,128]{1,0:T(8,128)(2,1)S(1)}, bf16[1088,128]{1,0:T(8,128)(2,1)S(1)}, u32[]{:S(2)}, u32[]{:S(2)}) collective-permute-start(bf16[1088,128]{1,0:T(8,128)(2,1)S(1)} %get-tuple-element.18), channel_id=1, source_target_pairs={{0,1},{1,2},{2,3},{3,4},{4,5},{5,6},{6,7},{7,8},{8,9},{9,10},{10,1... | collective-permute-start | bytes 835592 | tf_op jit(solution)/shard_map/ppermute | solution.py:30
  5.9 14.2 %collective-permute-start.1 = (bf16[1088,128]{1,0:T(8,128)(2,1)S(1)}, bf16[1088,128]{1,0:T(8,128)(2,1)S(1)}, u32[]{:S(2)}, u32[]{:S(2)}) collective-permute-start(bf16[1088,128]{1,0:T(8,128)(2,1)S(1)} %get-tuple-element.19), channel_id=1, source_target_pairs={{1,0},{2,1},{3,2},{4,3},{5,4},{6,5},{7,6},{8,7},{9,8},{10,9},{11,1... | collective-permute-start | bytes 835592 | tf_op jit(solution)/shard_map/ppermute | solution.py:30
  9.0 0.9 %copy-start.5 = (bf16[7,128,128]{2,1,0:T(8,128)(2,1)S(1)}, bf16[7,128,128]{2,1,0:T(8,128)(2,1)}, u32[]{:S(2)}) copy-start(bf16[7,128,128]{2,1,0:T(8,128)(2,1)} %param.15) | copy-start | bytes 688132
  13.8 13.9 %copy-start.1 = (bf16[8,512,128]{2,1,0:T(8,128)(2,1)S(1)}, bf16[8,512,128]{2,1,0:T(8,128)(2,1)}, u32[]{:S(2)}) copy-start(bf16[8,512,128]{2,1,0:T(8,128)(2,1)} %param.10) | copy-start | bytes 3145732
  13.8 13.9 %copy-start.6 = (bf16[7,128,128]{2,1,0:T(8,128)(2,1)S(1)}, bf16[7,128,128]{2,1,0:T(8,128)(2,1)}, u32[]{:S(2)}) copy-start(bf16[7,128,128]{2,1,0:T(8,128)(2,1)} %param.16) | copy-start | bytes 688132
  21.5 10.6 %collective-permute-start.2 = (bf16[1088,128]{1,0:T(8,128)(2,1)S(1)}, bf16[1088,128]{1,0:T(8,128)(2,1)S(1)}, u32[]{:S(2)}, u32[]{:S(2)}) collective-permute-start(bf16[1088,128]{1,0:T(8,128)(2,1)S(1)} %get-tuple-element.21), channel_id=1, source_target_pairs={{0,1},{1,2},{2,3},{3,4},{4,5},{5,6},{6,7},{7,8},{8,9},{9,10},{10,1... | collective-permute-start | bytes 835592 | tf_op jit(solution)/shard_map/ppermute | solution.py:30
  23.4 15.4 %collective-permute-start.3 = (bf16[1088,128]{1,0:T(8,128)(2,1)S(1)}, bf16[1088,128]{1,0:T(8,128)(2,1)S(1)}, u32[]{:S(2)}, u32[]{:S(2)}) collective-permute-start(bf16[1088,128]{1,0:T(8,128)(2,1)S(1)} %get-tuple-element.22), channel_id=1, source_target_pairs={{1,0},{2,1},{3,2},{4,3},{5,4},{6,5},{7,6},{8,7},{9,8},{10,9},{11,1... | collective-permute-start | bytes 835592 | tf_op jit(solution)/shard_map/ppermute | solution.py:30
  27.7 11.1 %copy-start.4 = (bf16[4,1024,256]{2,1,0:T(8,128)(2,1)S(1)}, bf16[4,1024,256]{2,1,0:T(8,128)(2,1)}, u32[]{:S(2)}) copy-start(bf16[4,1024,256]{2,1,0:T(8,128)(2,1)} %height.1) | copy-start | bytes 6291460
  27.7 11.1 %copy-start.8 = (s32[8]{0:T(128)S(1)}, s32[8]{0:T(128)}, u32[]{:S(2)}) copy-start(s32[8]{0:T(128)} %param.12) | copy-start | bytes 100
  27.7 11.1 %copy-start.9 = (s32[8]{0:T(128)S(1)}, s32[8]{0:T(128)}, u32[]{:S(2)}) copy-start(s32[8]{0:T(128)} %param.13) | copy-start | bytes 100
  27.7 11.1 %copy-start.10 = (s32[1,16]{1,0:T(1,128)S(1)}, s32[1,16]{1,0:T(1,128)}, u32[]{:S(2)}) copy-start(s32[1,16]{1,0:T(1,128)} %columns.1) | copy-start | bytes 196
  42.1 26.7 %copy-start.2 = (bf16[3,3,256,256]{3,2,1,0:T(8,128)(2,1)S(1)}, bf16[3,3,256,256]{3,2,1,0:T(8,128)(2,1)}, u32[]{:S(2)}) copy-start(bf16[3,3,256,256]{3,2,1,0:T(8,128)(2,1)} %param.18) | copy-start | bytes 3538948
  61.3 19.0 %copy-start.3 = (bf16[3,3,256,256]{3,2,1,0:T(8,128)(2,1)S(1)}, bf16[3,3,256,256]{3,2,1,0:T(8,128)(2,1)}, u32[]{:S(2)}) copy-start(bf16[3,3,256,256]{3,2,1,0:T(8,128)(2,1)} %param.19) | copy-start | bytes 3538948
  62.5 9.0 %collective-permute-start.4 = (bf16[64,256]{1,0:T(8,128)(2,1)}, bf16[64,256]{1,0:T(8,128)(2,1)}, u32[]{:S(2)}, u32[]{:S(2)}) collective-permute-start(bf16[64,256]{1,0:T(8,128)(2,1)} %get-tuple-element.24), channel_id=1, source_target_pairs={{0,8},{8,16},{16,24},{1,9},{9,17},{17,25},{2,10},{10,18},{18,26},{... | collective-permute-start | bytes 98312 | tf_op jit(solution)/shard_map/ppermute | solution.py:30
  66.9 5.6 %collective-permute-start.5 = (bf16[64,256]{1,0:T(8,128)(2,1)}, bf16[64,256]{1,0:T(8,128)(2,1)}, u32[]{:S(2)}, u32[]{:S(2)}) collective-permute-start(bf16[64,256]{1,0:T(8,128)(2,1)} %get-tuple-element.25), channel_id=1, source_target_pairs={{8,0},{16,8},{24,16},{9,1},{17,9},{25,17},{10,2},{18,10},{26,18},{... | collective-permute-start | bytes 98312 | tf_op jit(solution)/shard_map/ppermute | solution.py:30
  73.9 9.3 %collective-permute-start.6 = (bf16[2,68,256]{2,1,0:T(8,128)(2,1)S(1)}, bf16[2,68,256]{2,1,0:T(8,128)(2,1)S(1)}, u32[]{:S(2)}, u32[]{:S(2)}) collective-permute-start(bf16[2,68,256]{2,1,0:T(8,128)(2,1)S(1)} %pad_maximum_fusion.1.own_right), channel_id=1, source_target_pairs={{0,1},{1,2},{2,3},{3,4},{4,5},{5,6},{6,7},{8,9},{9,10},{10,11},{11... | collective-permute-start | bytes 208904 | tf_op jit(solution)/shard_map/ppermute | solution.py:30
  76.1 7.1 %collective-permute-start.7 = (bf16[2,68,256]{2,1,0:T(8,128)(2,1)S(1)}, bf16[2,68,256]{2,1,0:T(8,128)(2,1)S(1)}, u32[]{:S(2)}, u32[]{:S(2)}) collective-permute-start(bf16[2,68,256]{2,1,0:T(8,128)(2,1)S(1)} %pad_maximum_fusion.own_left), channel_id=1, source_target_pairs={{1,0},{2,1},{3,2},{4,3},{5,4},{6,5},{7,6},{9,8},{10,9},{11,10},{12... | collective-permute-start | bytes 208904 | tf_op jit(solution)/shard_map/ppermute | solution.py:30

commit v4 on v3

--- a/solution.py
+++ b/solution.py
@@ -28,6 +28,26 @@
     count = lax.axis_size(axis)
     route = [(i, i + distance) for i in range(count) if 0 <= i + distance < count]
     return lax.ppermute(block, axis, route)
+
+
+def swap(first, second, axis):
+    count = lax.axis_size(axis)
+    near = [(i, i ^ 1) for i in range(count) if i ^ 1 < count]
+    far = [(i, i + 1 if i % 2 else i - 1) for i in range(1, count)]
+    far = [(i, k) for i, k in far if k < count]
+    return lax.ppermute(first, axis, near), lax.ppermute(second, axis, far)
+
+
+def route(odd, up, down, first, second):
+    @pl.when(odd == 0)
+    def _():
+        first[...] = up[...]
+        second[...] = down[...]
+
+    @pl.when(odd != 0)
+    def _():
+        first[...] = down[...]
+        second[...] = up[...]
 
 
 def mm(a, b):
@@ -62,9 +82,10 @@
     down[2 * faces :, :] = src[0:FACE, :].astype(BF16)
 
 
-def pack_kernel(links, x, up, down, wide):
+def pack_kernel(flags, links, x, first, second, wide, up, down):
     wide[...] = x[...].astype(F32)
     pack_faces(wide, links, up, down)
+    route(flags[4], up, down, first, second)
 
 
 def interior(src, links, weights, out, residual):
@@ -146,33 +167,54 @@
     total[0:FACE, :] += mm(from_below[2 * faces :, :], tap(2))
 
 
-def hidden_kernel(links, partial, from_below, from_above, weights, hidden, up, down, total):
+def hidden_kernel(
+    flags,
+    links,
+    partial,
+    first_in,
+    second_in,
+    weights,
+    hidden,
+    first,
+    second,
+    total,
+    up,
+    down,
+    from_below,
+    from_above,
+):
     total[...] = partial[...]
+    route(flags[4], first_in, second_in, from_above, from_below)
     add_ghosts(total, from_below, from_above, links, weights)
     total[...] = jnp.maximum(total[...], 0.0)
     hidden[...] = total[...].astype(BF16)
     pack_faces(total, links, up, down)
+    route(flags[4], up, down, first, second)
 
 
 def lift_kernel(
+    flags,
     links,
     slots,
     block_levels,
     columns,
     partial,
-    from_below,
-    from_above,
+    first_in,
+    second_in,
     weights,
     height,
     out,
     total,
     rows_in,
     sums,
+    from_below,
+    from_above,
 ):
     count = partial.shape[0] // CELLS
     faces = count * FACE
     ch = partial.shape[1]
     total[...] = partial[...]
+    route(flags[4], first_in, second_in, from_above, from_below)
     add_ghosts(total, from_below, from_above, links, weights)
     for c in range(EDGE):
         line = total[pl.ds(c, faces, stride=EDGE), :]
@@ -295,8 +337,8 @@
     below,
     own_left,
     own_right,
-    left,
-    right,
+    first_in,
+    second_in,
     weights_first,
     weights_second,
     out,
@@ -307,9 +349,24 @@
     two = HALO * COLS
     four = 2 * two
     sides[...] = jnp.zeros_like(sides)
-    for base, source in ((0, left), (2, own_left), (4, own_right), (6, right)):
+
+    def place(base, source):
         for x in range(HALO):
             sides[base + x, 0:WIDE_ROWS, :] = source[x, :, :].astype(F32)
+
+    place(2, own_left)
+    place(4, own_right)
+
+    @pl.when(flags[5] == 0)
+    def _():
+        place(0, second_in)
+        place(6, first_in)
+
+    @pl.when(flags[5] != 0)
+    def _():
+        place(0, first_in)
+        place(6, second_in)
+
     lhs = []
     for start in (0, 1, 4, 5):
         parts = []
@@ -418,31 +475,38 @@
     wide = pltpu.VMEM((rows, ch), F32)
     part_shape = jax.ShapeDtypeStruct((rows, ch), F32)
 
-    up, down = call(pack_kernel, "pack", (face_shape, face_shape), (links,), (x,), (wide,))
-    from_below = shift(up, both, 1)
-    from_above = shift(down, both, -1)
+    gy, gx = lax.axis_index("gy"), lax.axis_index("gx")
+    flags = jnp.stack(
+        [gy > 0, gy < lax.axis_size("gy") - 1, gx > 0, gx < peers - 1, lax.axis_index(both) % 2, gx % 2]
+    ).astype(jnp.int32)
+    face = pltpu.VMEM((faces, ch), BF16)
+    first, second = call(
+        pack_kernel, "pack", (face_shape, face_shape), (flags, links), (x,), (wide, face, face)
+    )
+    first, second = swap(first, second, both)
     partial = call(first_interior_kernel, "inside1", part_shape, (links,), (x, w_first))
-    hidden, up, down = call(
+    hidden, first, second = call(
         hidden_kernel,
         "hidden",
         (jax.ShapeDtypeStruct((rows, ch), BF16), face_shape, face_shape),
-        (links,),
-        (partial, from_below, from_above, w_first),
-        (wide,),
-    )
-    from_below = shift(up, both, 1)
-    from_above = shift(down, both, -1)
+        (flags, links),
+        (partial, first, second, w_first),
+        (wide, face, face, face, face),
+    )
+    first, second = swap(first, second, both)
     partial = call(second_interior_kernel, "inside2", part_shape, (links,), (hidden, x, w_second))
     outgoing = call(
         lift_kernel,
         "lift",
         jax.ShapeDtypeStruct((peers, per_peer * FACE + ID_ROWS, mapped), BF16),
-        (links, slots, block_levels, slot_column),
-        (partial, from_below, from_above, w_second, height_w),
+        (flags, links, slots, block_levels, slot_column),
+        (partial, first, second, w_second, height_w),
         (
             wide,
             pltpu.VMEM((count * FACE, EDGE * ch), BF16),
             pltpu.VMEM((slot_total, FACE, mapped), F32),
+            face,
+            face,
         ),
     )
     arrived = lax.all_to_all(outgoing, "gx", split_axis=0, concat_axis=0, tiled=True)
@@ -487,8 +551,10 @@
         )
 
     own_left, own_right = side(left, 0), side(right, COLS - HALO)
-    from_left = shift(own_right, "gx", 1)
-    from_right = shift(own_left, "gx", -1)
+    odd = gx % 2 == 1
+    first, second = swap(
+        jnp.where(odd, own_left, own_right), jnp.where(odd, own_right, own_left), "gx"
+    )
     core = call(
         second_core_kernel,
         "second_core",
@@ -496,10 +562,6 @@
         (),
         (inner, bev, k_second),
     )
-    gy, gx = lax.axis_index("gy"), lax.axis_index("gx")
-    flags = jnp.stack(
-        [gy > 0, gy < lax.axis_size("gy") - 1, gx > 0, gx < peers - 1]
-    ).astype(jnp.int32)
     out = call(
         edges_kernel,
         "edges",
@@ -513,8 +575,8 @@
             below,
             own_left,
             own_right,
-            from_left,
-            from_right,
+            first,
+            second,
             k_first,
             k_second,
         ),

time: 88.1 us -> 80.6 us (0.915)
  starting transfers between devices: 24.8 us -> 15.1 us
  blocking collectives: 19.2 us -> 23.7 us
  waiting for transfers between devices: 14.5 us -> 11.8 us
    ppermute x8 -> x2, starting transfers between devices: 24.8 us -> 4.9 us  [shift(): return lax.ppermute(block, axis, route)]
    ppermute x8 -> x2, waiting for transfers between devices: 14.5 us -> 0.01 us  [shift(): return lax.ppermute(block, axis, route)]
    ppermute x0 -> x6, waiting for transfers between devices: none -> 11.8 us  [swap(): return (lax.ppermute(first, axis, near), lax.ppermute(second, axis, far))]
    ppermute x0 -> x6, starting transfers between devices: none -> 10.2 us  [swap(): return (lax.ppermute(first, axis, near), lax.ppermute(second, axis, far))]
    all_to_all x1, blocking collectives: 19.2 us -> 23.7 us  [local(): lax.all_to_all(outgoing, 'gx', split_axis=0, concat_axis=0, tiled=True)]
  transfers between devices with their start and end apart: 8 -> 8, of which waited for: 5 -> 3; matrix products, arithmetic and copies ran while one was open for 0% -> 0% of each run, Pallas kernels for 15% -> 17%
where the time goes in v4:
time: 80.6 us; the launch traced here: 79.7 us
  Pallas kernels  24.4 us (30%)
  blocking collectives  23.7 us (29%)
  starting transfers between devices  15.1 us (19%)
  waiting for transfers between devices  11.8 us (15%)
  local copies, waits for them, and re-layouts  4.42 us (5%)
    pallas_call x9, Pallas kernels, call(): pl.pallas_call(kernel, name=name, out_shape=out_shape, in_specs=[SMEM] *...  24.4 us
    all_to_all x1, blocking collectives, local(): lax.all_to_all(outgoing, 'gx', split_axis=0, concat_axis=0, tiled=True)  23.7 us
    ppermute x6, waiting for transfers between devices, swap(): return (lax.ppermute(first, axis, near), lax.ppermute(second, axis, far))  11.8 us
    ppermute x6, starting transfers between devices, swap(): return (lax.ppermute(first, axis, near), lax.ppermute(second, axis, far))  10.2 us
    ppermute x2, starting transfers between devices, shift(): return lax.ppermute(block, axis, route)  4.9 us
    unnamed x22, local copies, waits for them, and re-layouts  2.89 us
  transfers between devices with their start and end apart: 8, of which 3 were waited for; matrix products, arithmetic and copies ran while one was open for 0% of the time, Pallas kernels for 17%

profile of v4, /device:TPU:9, one launch (start us, length us, event | category | flops | bytes accessed | tf_op | source)
XLA Modules:
  0.0 79.7 jit_solution(15991709797454698503)
XLA Ops:
  0.1 1.2 %copy-done = bf16[8,512,128]{2,1,0:T(8,128)(2,1)S(1)} copy-done((bf16[8,512,128]{2,1,0:T(8,128)(2,1)S(1)}, bf16[8,512,128]{2,1,0:T(8,128)(2,1)}, u32[]{:S(2)}) %copy-start) | copy-done | bytes 1048600
  2.0 0.9 %pack.1 = (bf16[1088,128]{1,0:T(8,128)(2,1)S(1)}, bf16[1088,128]{1,0:T(8,128)(2,1)S(1)}) custom-call(s32[6]{0:T(128)S(1)} %stack.43.flags, s32[3,8]{1,0:T(4,128)S(1)} %bitcast.36, bf16[4096,128]{1,0:T(8,128)(2,1)S(1)} %bitcast.25), custom_call_target="tpu_custom_call" | custom-call | tf_op jit(solution)/shard_map/pack/pallas_call | solution.py:434
  2.9 1.3 %collective-permute-start = (bf16[1088,128]{1,0:T(8,128)(2,1)S(1)}, bf16[1088,128]{1,0:T(8,128)(2,1)S(1)}, u32[]{:S(2)}, u32[]{:S(2)}) collective-permute-start(bf16[1088,128]{1,0:T(8,128)(2,1)S(1)} %get-tuple-element.18), channel_id=1, source_target_pairs={{0,1},{1,0},{2,3},{3,2},{4,5},{5,4},{6,7},{7,6},{8,9},{9,8},{10,11... | collective-permute-start | bytes 835592 | tf_op jit(solution)/shard_map/ppermute | solution.py:38
  4.2 1.9 %collective-permute-start.1 = (bf16[1088,128]{1,0:T(8,128)(2,1)S(1)}, bf16[1088,128]{1,0:T(8,128)(2,1)S(1)}, u32[]{:S(2)}, u32[]{:S(2)}) collective-permute-start(bf16[1088,128]{1,0:T(8,128)(2,1)S(1)} %get-tuple-element.19), channel_id=1, source_target_pairs={{1,2},{2,1},{3,4},{4,3},{5,6},{6,5},{7,8},{8,7},{9,10},{10,9},{11,... | collective-permute-start | bytes 835592 | tf_op jit(solution)/shard_map/ppermute | solution.py:38
  6.1 0.9 %copy-done.5 = bf16[7,128,128]{2,1,0:T(8,128)(2,1)S(1)} copy-done((bf16[7,128,128]{2,1,0:T(8,128)(2,1)S(1)}, bf16[7,128,128]{2,1,0:T(8,128)(2,1)}, u32[]{:S(2)}) %copy-start.5) | copy-done | bytes 229400
  7.1 3.8 %inside1.1.partial = f32[4096,128]{1,0:T(8,128)S(1)} custom-call(s32[3,8]{1,0:T(4,128)S(1)} %bitcast.37, bf16[4096,128]{1,0:T(8,128)(2,1)S(1)} %bitcast.26, bf16[896,128]{1,0:T(8,128)(2,1)S(1)} %bitcast.32), custom_call_target="tpu_custom_call" | custom-call | tf_op jit(solution)/shard_map/inside1/pallas_call | solution.py:434
  10.9 5.6 %collective-permute-done.first_in = bf16[1088,128]{1,0:T(8,128)(2,1)S(1)} collective-permute-done((bf16[1088,128]{1,0:T(8,128)(2,1)S(1)}, bf16[1088,128]{1,0:T(8,128)(2,1)S(1)}, u32[]{:S(2)}, u32[]{:S(2)}) %collective-permute-start) | collective-permute-done | bytes 278560 | tf_op jit(solution)/shard_map/ppermute | solution.py:38
  16.5 1.5 %hidden.1 = (bf16[4096,128]{1,0:T(8,128)(2,1)S(1)}, bf16[1088,128]{1,0:T(8,128)(2,1)S(1)}, bf16[1088,128]{1,0:T(8,128)(2,1)S(1)}) custom-call(s32[6]{0:T(128)S(1)} %stack.43.flags, s32[3,8]{1,0:T(4,128)S(1)} %bitcast.38, f32[4096,128]{1,0:T(8,128)S(1)} %inside1.1.partial, bf16[1088,128]{1,0:T(8,128)(2,1)S(1)} %collective-permute-done.first_in, ...), custom_call_target="tpu_custom_call" | custom-call | tf_op jit(solution)/shard_map/hidden/pallas_call | solution.py:434
  18.0 1.3 %collective-permute-start.2 = (bf16[1088,128]{1,0:T(8,128)(2,1)S(1)}, bf16[1088,128]{1,0:T(8,128)(2,1)S(1)}, u32[]{:S(2)}, u32[]{:S(2)}) collective-permute-start(bf16[1088,128]{1,0:T(8,128)(2,1)S(1)} %get-tuple-element.21), channel_id=1, source_target_pairs={{0,1},{1,0},{2,3},{3,2},{4,5},{5,4},{6,7},{7,6},{8,9},{9,8},{10,11... | collective-permute-start | bytes 835592 | tf_op jit(solution)/shard_map/ppermute | solution.py:38
  19.2 2.1 %collective-permute-start.3 = (bf16[1088,128]{1,0:T(8,128)(2,1)S(1)}, bf16[1088,128]{1,0:T(8,128)(2,1)S(1)}, u32[]{:S(2)}, u32[]{:S(2)}) collective-permute-start(bf16[1088,128]{1,0:T(8,128)(2,1)S(1)} %get-tuple-element.22), channel_id=1, source_target_pairs={{1,2},{2,1},{3,4},{4,3},{5,6},{6,5},{7,8},{8,7},{9,10},{10,9},{11,... | collective-permute-start | bytes 835592 | tf_op jit(solution)/shard_map/ppermute | solution.py:38
  21.4 3.8 %inside2.1.partial = f32[4096,128]{1,0:T(8,128)S(1)} custom-call(s32[3,8]{1,0:T(4,128)S(1)} %bitcast.39, bf16[4096,128]{1,0:T(8,128)(2,1)S(1)} %get-tuple-element.20.hidden, bf16[4096,128]{1,0:T(8,128)(2,1)S(1)} %bitcast.27, bf16[896,128]{1,0:T(8,128)(2,1)S(1)} %bitcast.34), custom_call_target="tpu_custom_call" | custom-call | tf_op jit(solution)/shard_map/inside2/pallas_call | solution.py:434
  25.2 4.5 %collective-permute-done.2.first_in = bf16[1088,128]{1,0:T(8,128)(2,1)S(1)} collective-permute-done((bf16[1088,128]{1,0:T(8,128)(2,1)S(1)}, bf16[1088,128]{1,0:T(8,128)(2,1)S(1)}, u32[]{:S(2)}, u32[]{:S(2)}) %collective-permute-start.2) | collective-permute-done | bytes 278560 | tf_op jit(solution)/shard_map/ppermute | solution.py:38
  29.7 3.4 %lift.1 = bf16[8,136,256]{2,1,0:T(8,128)(2,1)S(1)} custom-call(s32[6]{0:T(128)S(1)} %stack.43.flags, s32[3,8]{1,0:T(4,128)S(1)} %bitcast.40, s32[1,8]{1,0:T(1,128)S(1)} %bitcast.41, s32[1,8]{1,0:T(1,128)S(1)} %bitcast.42, s32[1,16]{1,0:T(1,128)S(1)} %copy-done.10, f32[4096,128]{1,0:T(8,128)S(1)} %inside2.1.partial, ...), custom_call_target="tpu_custom_call" | custom-call | tf_op jit(solution)/shard_map/lift/pallas_call | solution.py:434
  33.1 23.7 %all_to_all.5.arrived = bf16[8,136,256]{2,1,0:T(8,128)(2,1)S(1)} all-to-all(bf16[8,136,256]{2,1,0:T(8,128)(2,1)S(1)} %lift.1), channel_id=1, replica_groups=mesh['gy'=4,'gx'=8] {'gx'}, dimensions={0} | all-to-all | bytes 1114112 | tf_op jit(solution)/shard_map/all_to_all | solution.py:512
  56.8 1.2 %gather.1 = (bf16[2048,256]{1,0:T(8,128)(2,1)S(1)}, bf16[64,256]{1,0:T(8,128)(2,1)}, bf16[64,256]{1,0:T(8,128)(2,1)}, bf16[2,64,256]{2,1,0:T(8,128)(2,1)S(1)}, bf16[2,64,256]{2,1,0:T(8,128)(2,1)S(1)}) custom-call(bf16[8,136,256]{2,1,0:T(8,128)(2,1)S(1)} %all_to_all.5.arrived), custom_call_target="tpu_custom_call" | custom-call | tf_op jit(solution)/shard_map/gather/pallas_call | solution.py:434
  58.0 1.9 %collective-permute-start.4 = (bf16[64,256]{1,0:T(8,128)(2,1)}, bf16[64,256]{1,0:T(8,128)(2,1)}, u32[]{:S(2)}, u32[]{:S(2)}) collective-permute-start(bf16[64,256]{1,0:T(8,128)(2,1)} %get-tuple-element.24), channel_id=1, source_target_pairs={{0,8},{8,16},{16,24},{1,9},{9,17},{17,25},{2,10},{10,18},{18,26},{... | collective-permute-start | bytes 98312 | tf_op jit(solution)/shard_map/ppermute | solution.py:30
  60.0 3.0 %collective-permute-start.5 = (bf16[64,256]{1,0:T(8,128)(2,1)}, bf16[64,256]{1,0:T(8,128)(2,1)}, u32[]{:S(2)}, u32[]{:S(2)}) collective-permute-start(bf16[64,256]{1,0:T(8,128)(2,1)} %get-tuple-element.25), channel_id=1, source_target_pairs={{8,0},{16,8},{24,16},{9,1},{17,9},{25,17},{10,2},{18,10},{26,18},{... | collective-permute-start | bytes 98312 | tf_op jit(solution)/shard_map/ppermute | solution.py:30
  63.0 2.7 %first_inner.1.inner = bf16[1984,256]{1,0:T(8,128)(2,1)S(1)} custom-call(bf16[2048,256]{1,0:T(8,128)(2,1)S(1)} %get-tuple-element.23.bev, bf16[9,256,256]{2,1,0:T(8,128)(2,1)S(1)} %bitcast.28), custom_call_target="tpu_custom_call" | custom-call | tf_op jit(solution)/shard_map/first_inner/pallas_call | solution.py:434
  65.7 0.7 fusion.1
  66.4 0.7 fusion
  67.2 3.2 %collective-permute-start.7 = (bf16[2,68,256]{2,1,0:T(8,128)(2,1)S(1)}, bf16[2,68,256]{2,1,0:T(8,128)(2,1)S(1)}, u32[]{:S(2)}, u32[]{:S(2)}) collective-permute-start(bf16[2,68,256]{2,1,0:T(8,128)(2,1)S(1)} %get-tuple-element.31), channel_id=1, source_target_pairs={{1,2},{2,1},{3,4},{4,3},{5,6},{6,5},{9,10},{10,9},{11,12},{12,11},... | collective-permute-start | bytes 208904 | tf_op jit(solution)/shard_map/ppermute | solution.py:38
  71.0 3.0 %second_core.1.core = f32[2,1920,128]{2,1,0:T(8,128)S(1)} custom-call(bf16[1984,256]{1,0:T(8,128)(2,1)S(1)} %first_inner.1.inner, bf16[2048,256]{1,0:T(8,128)(2,1)S(1)} %get-tuple-element.23.bev, bf16[9,256,256]{2,1,0:T(8,128)(2,1)S(1)} %bitcast.30), custom_call_target="tpu_custom_call" | custom-call | tf_op jit(solution)/shard_map/second_core/pallas_call | solution.py:434
  74.0 1.7 %collective-permute-done.6.first_in = bf16[2,68,256]{2,1,0:T(8,128)(2,1)S(1)} collective-permute-done((bf16[2,68,256]{2,1,0:T(8,128)(2,1)S(1)}, bf16[2,68,256]{2,1,0:T(8,128)(2,1)S(1)}, u32[]{:S(2)}, u32[]{:S(2)}) %collective-permute-start.6) | collective-permute-done | bytes 69664 | tf_op jit(solution)/shard_map/ppermute | solution.py:38
  75.7 4.0 %edges.1 = bf16[2048,256]{1,0:T(8,128)(2,1)} custom-call(s32[6]{0:T(128)S(1)} %stack.43.flags, bf16[2048,256]{1,0:T(8,128)(2,1)S(1)} %get-tuple-element.23.bev, bf16[1984,256]{1,0:T(8,128)(2,1)S(1)} %first_inner.1.inner, f32[2,1920,128]{2,1,0:T(8,128)S(1)} %second_core.1.core, bf16[64,256]{1,0:T(8,128)(2,1)} %collective-permute-done.4.above, ...), custom_call_target="tpu_custom_call" | custom-call | tf_op jit(solution)/shard_map/edges/pallas_call | solution.py:434
  (30 shorter events, 1.4 us)
Async XLA Ops:
  0.1 1.2 %copy-start = (bf16[8,512,128]{2,1,0:T(8,128)(2,1)S(1)}, bf16[8,512,128]{2,1,0:T(8,128)(2,1)}, u32[]{:S(2)}) copy-start(bf16[8,512,128]{2,1,0:T(8,128)(2,1)} %param.10) | copy-start | bytes 3145732
  1.3 0.7 copy-start.7
  2.9 13.6 %collective-permute-start = (bf16[1088,128]{1,0:T(8,128)(2,1)S(1)}, bf16[1088,128]{1,0:T(8,128)(2,1)S(1)}, u32[]{:S(2)}, u32[]{:S(2)}) collective-permute-start(bf16[1088,128]{1,0:T(8,128)(2,1)S(1)} %get-tuple-element.18), channel_id=1, source_target_pairs={{0,1},{1,0},{2,3},{3,2},{4,5},{5,4},{6,7},{7,6},{8,9},{9,8},{10,11... | collective-permute-start | bytes 835592 | tf_op jit(solution)/shard_map/ppermute | solution.py:38
  4.2 12.3 %collective-permute-start.1 = (bf16[1088,128]{1,0:T(8,128)(2,1)S(1)}, bf16[1088,128]{1,0:T(8,128)(2,1)S(1)}, u32[]{:S(2)}, u32[]{:S(2)}) collective-permute-start(bf16[1088,128]{1,0:T(8,128)(2,1)S(1)} %get-tuple-element.19), channel_id=1, source_target_pairs={{1,2},{2,1},{3,4},{4,3},{5,6},{6,5},{7,8},{8,7},{9,10},{10,9},{11,... | collective-permute-start | bytes 835592 | tf_op jit(solution)/shard_map/ppermute | solution.py:38
  6.1 0.9 %copy-start.5 = (bf16[7,128,128]{2,1,0:T(8,128)(2,1)S(1)}, bf16[7,128,128]{2,1,0:T(8,128)(2,1)}, u32[]{:S(2)}) copy-start(bf16[7,128,128]{2,1,0:T(8,128)(2,1)} %param.15) | copy-start | bytes 688132
  10.9 10.4 %copy-start.1 = (bf16[8,512,128]{2,1,0:T(8,128)(2,1)S(1)}, bf16[8,512,128]{2,1,0:T(8,128)(2,1)}, u32[]{:S(2)}) copy-start(bf16[8,512,128]{2,1,0:T(8,128)(2,1)} %param.10) | copy-start | bytes 3145732
  10.9 10.4 %copy-start.6 = (bf16[7,128,128]{2,1,0:T(8,128)(2,1)S(1)}, bf16[7,128,128]{2,1,0:T(8,128)(2,1)}, u32[]{:S(2)}) copy-start(bf16[7,128,128]{2,1,0:T(8,128)(2,1)} %param.16) | copy-start | bytes 688132
  18.0 11.7 %collective-permute-start.2 = (bf16[1088,128]{1,0:T(8,128)(2,1)S(1)}, bf16[1088,128]{1,0:T(8,128)(2,1)S(1)}, u32[]{:S(2)}, u32[]{:S(2)}) collective-permute-start(bf16[1088,128]{1,0:T(8,128)(2,1)S(1)} %get-tuple-element.21), channel_id=1, source_target_pairs={{0,1},{1,0},{2,3},{3,2},{4,5},{5,4},{6,7},{7,6},{8,9},{9,8},{10,11... | collective-permute-start | bytes 835592 | tf_op jit(solution)/shard_map/ppermute | solution.py:38
  19.2 10.5 %collective-permute-start.3 = (bf16[1088,128]{1,0:T(8,128)(2,1)S(1)}, bf16[1088,128]{1,0:T(8,128)(2,1)S(1)}, u32[]{:S(2)}, u32[]{:S(2)}) collective-permute-start(bf16[1088,128]{1,0:T(8,128)(2,1)S(1)} %get-tuple-element.22), channel_id=1, source_target_pairs={{1,2},{2,1},{3,4},{4,3},{5,6},{6,5},{7,8},{8,7},{9,10},{10,9},{11,... | collective-permute-start | bytes 835592 | tf_op jit(solution)/shard_map/ppermute | solution.py:38
  21.3 8.4 %copy-start.4 = (bf16[4,1024,256]{2,1,0:T(8,128)(2,1)S(1)}, bf16[4,1024,256]{2,1,0:T(8,128)(2,1)}, u32[]{:S(2)}) copy-start(bf16[4,1024,256]{2,1,0:T(8,128)(2,1)} %height.1) | copy-start | bytes 6291460
  21.3 8.4 %copy-start.8 = (s32[8]{0:T(128)S(1)}, s32[8]{0:T(128)}, u32[]{:S(2)}) copy-start(s32[8]{0:T(128)} %param.12) | copy-start | bytes 100
  21.4 8.4 %copy-start.9 = (s32[8]{0:T(128)S(1)}, s32[8]{0:T(128)}, u32[]{:S(2)}) copy-start(s32[8]{0:T(128)} %param.13) | copy-start | bytes 100
  21.4 8.3 %copy-start.10 = (s32[1,16]{1,0:T(1,128)S(1)}, s32[1,16]{1,0:T(1,128)}, u32[]{:S(2)}) copy-start(s32[1,16]{1,0:T(1,128)} %columns.1) | copy-start | bytes 196
  33.1 29.8 %copy-start.2 = (bf16[3,3,256,256]{3,2,1,0:T(8,128)(2,1)S(1)}, bf16[3,3,256,256]{3,2,1,0:T(8,128)(2,1)}, u32[]{:S(2)}) copy-start(bf16[3,3,256,256]{3,2,1,0:T(8,128)(2,1)} %param.18) | copy-start | bytes 3538948
  56.8 14.2 %copy-start.3 = (bf16[3,3,256,256]{3,2,1,0:T(8,128)(2,1)S(1)}, bf16[3,3,256,256]{3,2,1,0:T(8,128)(2,1)}, u32[]{:S(2)}) copy-start(bf16[3,3,256,256]{3,2,1,0:T(8,128)(2,1)} %param.19) | copy-start | bytes 3538948
  58.0 7.7 %collective-permute-start.4 = (bf16[64,256]{1,0:T(8,128)(2,1)}, bf16[64,256]{1,0:T(8,128)(2,1)}, u32[]{:S(2)}, u32[]{:S(2)}) collective-permute-start(bf16[64,256]{1,0:T(8,128)(2,1)} %get-tuple-element.24), channel_id=1, source_target_pairs={{0,8},{8,16},{16,24},{1,9},{9,17},{17,25},{2,10},{10,18},{18,26},{... | collective-permute-start | bytes 98312 | tf_op jit(solution)/shard_map/ppermute | solution.py:30
  60.0 5.7 %collective-permute-start.5 = (bf16[64,256]{1,0:T(8,128)(2,1)}, bf16[64,256]{1,0:T(8,128)(2,1)}, u32[]{:S(2)}, u32[]{:S(2)}) collective-permute-start(bf16[64,256]{1,0:T(8,128)(2,1)} %get-tuple-element.25), channel_id=1, source_target_pairs={{8,0},{16,8},{24,16},{9,1},{17,9},{25,17},{10,2},{18,10},{26,18},{... | collective-permute-start | bytes 98312 | tf_op jit(solution)/shard_map/ppermute | solution.py:30
  67.2 6.8 %collective-permute-start.7 = (bf16[2,68,256]{2,1,0:T(8,128)(2,1)S(1)}, bf16[2,68,256]{2,1,0:T(8,128)(2,1)S(1)}, u32[]{:S(2)}, u32[]{:S(2)}) collective-permute-start(bf16[2,68,256]{2,1,0:T(8,128)(2,1)S(1)} %get-tuple-element.31), channel_id=1, source_target_pairs={{1,2},{2,1},{3,4},{4,3},{5,6},{6,5},{9,10},{10,9},{11,12},{12,11},... | collective-permute-start | bytes 208904 | tf_op jit(solution)/shard_map/ppermute | solution.py:38
  70.4 5.3 %collective-permute-start.6 = (bf16[2,68,256]{2,1,0:T(8,128)(2,1)S(1)}, bf16[2,68,256]{2,1,0:T(8,128)(2,1)S(1)}, u32[]{:S(2)}, u32[]{:S(2)}) collective-permute-start(bf16[2,68,256]{2,1,0:T(8,128)(2,1)S(1)} %get-tuple-element.32), channel_id=1, source_target_pairs={{0,1},{1,0},{2,3},{3,2},{4,5},{5,4},{6,7},{7,6},{8,9},{9,8},{10,11... | collective-permute-start | bytes 208904 | tf_op jit(solution)/shard_map/ppermute | solution.py:38

commit v5 on v4

--- a/solution.py
+++ b/solution.py
@@ -1,11 +1,10 @@
-import functools
-
 import jax
 import jax.numpy as jnp
 from jax import lax
 from jax.experimental import pallas as pl
 from jax.experimental.pallas import tpu as pltpu
 from jax.sharding import PartitionSpec as P
+
 
 EDGE = 8
 FACE = EDGE * EDGE
@@ -24,18 +23,14 @@
 SMEM = pl.BlockSpec(memory_space=pltpu.SMEM)
 
 
-def shift(block, axis, distance):
-    count = lax.axis_size(axis)
-    route = [(i, i + distance) for i in range(count) if 0 <= i + distance < count]
-    return lax.ppermute(block, axis, route)
-
-
 def swap(first, second, axis):
     count = lax.axis_size(axis)
     near = [(i, i ^ 1) for i in range(count) if i ^ 1 < count]
     far = [(i, i + 1 if i % 2 else i - 1) for i in range(1, count)]
     far = [(i, k) for i, k in far if k < count]
-    return lax.ppermute(first, axis, near), lax.ppermute(second, axis, far)
+    first = lax.ppermute(first, axis, near)
+    second = lax.ppermute(second, axis, far)
+    return first, second
 
 
 def route(odd, up, down, first, second):
@@ -82,10 +77,10 @@
     down[2 * faces :, :] = src[0:FACE, :].astype(BF16)
 
 
-def pack_kernel(flags, links, x, first, second, wide, up, down):
+def pack_kernel(links, x, first, second, wide, up, down):
     wide[...] = x[...].astype(F32)
     pack_faces(wide, links, up, down)
-    route(flags[4], up, down, first, second)
+    route(links[3, 4], up, down, first, second)
 
 
 def interior(src, links, weights, out, residual):
@@ -168,7 +163,6 @@
 
 
 def hidden_kernel(
-    flags,
     links,
     partial,
     first_in,
@@ -184,16 +178,15 @@
     from_above,
 ):
     total[...] = partial[...]
-    route(flags[4], first_in, second_in, from_above, from_below)
+    route(links[3, 4], first_in, second_in, from_above, from_below)
     add_ghosts(total, from_below, from_above, links, weights)
     total[...] = jnp.maximum(total[...], 0.0)
     hidden[...] = total[...].astype(BF16)
     pack_faces(total, links, up, down)
-    route(flags[4], up, down, first, second)
+    route(links[3, 4], up, down, first, second)
 
 
 def lift_kernel(
-    flags,
     links,
     slots,
     block_levels,
@@ -214,7 +207,7 @@
     faces = count * FACE
     ch = partial.shape[1]
     total[...] = partial[...]
-    route(flags[4], first_in, second_in, from_above, from_below)
+    route(links[3, 4], first_in, second_in, from_above, from_below)
     add_ghosts(total, from_below, from_above, links, weights)
     for c in range(EDGE):
         line = total[pl.ds(c, faces, stride=EDGE), :]
@@ -239,7 +232,7 @@
         out[p, per_peer * FACE :, :] = ids.astype(BF16)
 
 
-def gather_kernel(arrived, bev, top, bottom, left, right, total):
+def gather_kernel(links, arrived, bev, first, second, own, total, top, bottom):
     peers, rows, ch = arrived.shape
     per_peer = (rows - ID_ROWS) // FACE
     total[...] = jnp.zeros_like(total)
@@ -259,8 +252,9 @@
         bottom[:, lanes] = total[h, (ROWS - HALO) * COLS :, :].astype(BF16)
         for x in range(HALO):
             far = COLS - HALO + x
-            left[x, :, lanes] = total[h, pl.ds(x, ROWS, stride=COLS), :].astype(BF16)
-            right[x, :, lanes] = total[h, pl.ds(far, ROWS, stride=COLS), :].astype(BF16)
+            own[x, :, lanes] = total[h, pl.ds(x, ROWS, stride=COLS), :].astype(BF16)
+            own[HALO + x, :, lanes] = total[h, pl.ds(far, ROWS, stride=COLS), :].astype(BF16)
+    route(links[3, 6], bottom, top, first, second)
 
 
 def halves(channels):
@@ -313,28 +307,71 @@
     lax.fori_loop(0, INNER_ROWS // step, one, 0)
 
 
-def second_core_kernel(inner, bev, weights, core):
-    step = CORE_ROWS // 4
-
-    def one(i, carry):
-        block = rows_conv(three_rows(inner, i * step, step), weights)
-        at = pl.multiple_of((i * step + 2) * COLS, COLS)
-        block = block + bev[pl.ds(at, step * COLS), :].astype(F32)
-        to = pl.multiple_of(i * step * COLS, COLS)
-        for h, lanes in halves(block.shape[1]):
-            core[h, pl.ds(to, step * COLS), :] = block[:, lanes]
-        return carry
-
-    lax.fori_loop(0, CORE_ROWS // step, one, 0)
-
-
-def edges_kernel(
-    flags,
+def strips(upper, lower):
+    parts = []
+    for source in (upper, lower):
+        rows = [source[dy * COLS : (dy + HALO) * COLS] for dy in range(3)]
+        parts.append(jnp.concatenate(rows, 1))
+    return jnp.concatenate(parts, 0)
+
+
+def second_core_kernel(
+    links,
+    inner,
     bev,
-    inner,
-    core,
+    first_row,
+    second_row,
+    weights_first,
+    weights_second,
+    middle,
+    flanks,
     above,
     below,
+):
+    ch = bev.shape[1]
+    two = HALO * COLS
+    step = CORE_ROWS // 4
+
+    def store(block, row):
+        count = block.shape[0] // COLS
+        at = row * COLS if isinstance(row, int) else pl.multiple_of(row * COLS, COLS)
+        middle[pl.ds(at, count * COLS), :] = block.astype(BF16)
+        lines = block.reshape(count, COLS, ch)
+        for side, x in enumerate((0, COLS - EDGE)):
+            flank = lines[:, x : x + EDGE, :].reshape(count * EDGE, ch)
+            to = side * ROWS * EDGE + row * EDGE
+            to = to if isinstance(row, int) else pl.multiple_of(to, EDGE)
+            for h, lanes in halves(ch):
+                flanks[h, pl.ds(to, count * EDGE), :] = flank[:, lanes]
+
+    def one(i, carry):
+        block = rows_conv(three_rows(inner, i * step, step), weights_second)
+        at = pl.multiple_of((i * step + 2) * COLS, COLS)
+        store(block + bev[pl.ds(at, step * COLS), :].astype(F32), i * step + 2)
+        return carry
+
+    lax.fori_loop(0, CORE_ROWS // step, one, 0)
+
+    route(links[3, 6], first_row, second_row, below, above)
+    top, bottom = bev[0:two, :], bev[ROWS * COLS - two :, :]
+    high = jnp.concatenate([above[...], top], 0)
+    low = jnp.concatenate([bottom, below[...]], 0)
+    strip = without_sides(jnp.maximum(rows_conv(strips(high, low), weights_first), 0.0))
+    line = lax.broadcasted_iota(jnp.int32, strip.shape, 0) // COLS
+    keep = jnp.where(line == 0, links[3, 0], jnp.where(line == 3, links[3, 1], 1)).astype(F32)
+    strip = (strip * keep).astype(BF16)
+
+    high = jnp.concatenate([strip[0:two], inner[0:two, :]], 0)
+    low = jnp.concatenate([inner[INNER_ROWS * COLS - two :, :], strip[two:]], 0)
+    strip = rows_conv(strips(high, low), weights_second)
+    store(strip[0:two] + top.astype(F32), 0)
+    store(strip[two:] + bottom.astype(F32), ROWS - HALO)
+
+
+def edges_kernel(
+    links,
+    middle,
+    flanks,
     own_left,
     own_right,
     first_in,
@@ -345,9 +382,7 @@
     sides,
     total,
 ):
-    ch = bev.shape[1]
-    two = HALO * COLS
-    four = 2 * two
+    ch = middle.shape[1]
     sides[...] = jnp.zeros_like(sides)
 
     def place(base, source):
@@ -357,12 +392,12 @@
     place(2, own_left)
     place(4, own_right)
 
-    @pl.when(flags[5] == 0)
+    @pl.when(links[3, 5] == 0)
     def _():
         place(0, second_in)
         place(6, first_in)
 
-    @pl.when(flags[5] != 0)
+    @pl.when(links[3, 5] != 0)
     def _():
         place(0, first_in)
         place(6, second_in)
@@ -377,39 +412,13 @@
     taps = jnp.concatenate([weights_first[t] for t in range(9)], 0)
     columns = jnp.maximum(mm(jnp.concatenate(lhs, 0), taps), 0.0)
     row_at = lax.broadcasted_iota(jnp.int32, (RIM_ROWS, ch), 0)
-    keep = jnp.where(row_at == 0, flags[0], jnp.where(row_at == MID_ROWS - 1, flags[1], 1)).astype(
-        F32
-    )
-    for k, side_keep in enumerate((flags[2], 1, 1, flags[3])):
+    keep = jnp.where(row_at == MID_ROWS - 1, links[3, 1], 1)
+    keep = jnp.where(row_at == 0, links[3, 0], keep).astype(F32)
+    for k, side_keep in enumerate((links[3, 2], None, None, links[3, 3])):
         block = columns[k * RIM_ROWS : (k + 1) * RIM_ROWS, :] * keep
-        if k in (0, 3):
+        if side_keep is not None:
             block = block * side_keep.astype(F32)
         sides[k, 0:RIM_ROWS, :] = block
-
-    high = jnp.concatenate([above[...], bev[0:two, :]], 0)
-    low = jnp.concatenate([bev[ROWS * COLS - two :, :], below[...]], 0)
-
-    def strips(upper, lower):
-        parts = []
-        for source in (upper, lower):
-            rows = [source[dy * COLS : dy * COLS + two] for dy in range(3)]
-            parts.append(jnp.concatenate(rows, 1))
-        return jnp.concatenate(parts, 0)
-
-    strip = without_sides(jnp.maximum(rows_conv(strips(high, low), weights_first), 0.0))
-    line = lax.broadcasted_iota(jnp.int32, (four, ch), 0) // COLS
-    keep = jnp.where(line == 0, flags[0], jnp.where(line == 3, flags[1], 1)).astype(F32)
-    strip = (strip * keep).astype(BF16)
-
-    high = jnp.concatenate([strip[0:two], inner[0:two, :]], 0)
-    low = jnp.concatenate([inner[INNER_ROWS * COLS - two :, :], strip[two:]], 0)
-    strip = rows_conv(strips(high, low), weights_second)
-    for h, lanes in halves(ch):
-        top_rows = strip[0:two, lanes] + bev[0:two, lanes].astype(F32)
-        low_rows = strip[two:, lanes] + bev[ROWS * COLS - two :, lanes].astype(F32)
-        total[h, 0:two, :] = top_rows
-        total[h, two : ROWS * COLS - two, :] = core[h, :, :]
-        total[h, ROWS * COLS - two :, :] = low_rows
 
     column = []
     for k in range(4):
@@ -419,21 +428,26 @@
     added = (
         (0, mm(column[0], w0) + mm(column[1], w1)),
         (1, mm(column[1], w0)),
-        (COLS - 2, mm(column[2], w2)),
-        (COLS - 1, mm(column[2], w1) + mm(column[3], w2)),
-    )
-    for x, block in added:
+        (ROWS * EDGE + EDGE - 2, mm(column[2], w2)),
+        (ROWS * EDGE + EDGE - 1, mm(column[2], w1) + mm(column[3], w2)),
+    )
+    total[...] = flanks[...]
+    for at, block in added:
         for h, lanes in halves(ch):
-            total[h, pl.ds(x, ROWS, stride=COLS), :] += block[:, lanes]
-    for h, lanes in halves(ch):
-        out[:, lanes] = total[h].astype(BF16)
-
-
-def call(kernel, name, out_shape, scalars, arrays, scratch=(), mib=12):
+            total[h, pl.ds(at, ROWS, stride=EDGE), :] += block[:, lanes]
+    for y in range(ROWS):
+        at = y * COLS
+        out[at + EDGE : at + COLS - EDGE, :] = middle[at + EDGE : at + COLS - EDGE, :]
+        for side, x in enumerate((0, COLS - EDGE)):
+            group = side * ROWS * EDGE + y * EDGE
+            for h, lanes in halves(ch):
+                out[at + x : at + x + EDGE, lanes] = total[h, group : group + EDGE, :].astype(BF16)
+
+
+def call(kernel, out_shape, scalars, arrays, scratch=(), mib=12):
     multiple = isinstance(out_shape, (list, tuple))
     return pl.pallas_call(
         kernel,
-        name=name,
         out_shape=out_shape,
         in_specs=[SMEM] * len(scalars) + [VMEM] * len(arrays),
         out_specs=[VMEM] * len(out_shape) if multiple else VMEM,
@@ -469,37 +483,34 @@
     slots = block_slot.reshape(1, count)
     block_levels = block_level.reshape(1, count)
     both = ("gy", "gx")
-    links = links.T
 
     face_shape = jax.ShapeDtypeStruct((faces, ch), BF16)
     wide = pltpu.VMEM((rows, ch), F32)
     part_shape = jax.ShapeDtypeStruct((rows, ch), F32)
 
     gy, gx = lax.axis_index("gy"), lax.axis_index("gx")
-    flags = jnp.stack(
-        [gy > 0, gy < lax.axis_size("gy") - 1, gx > 0, gx < peers - 1, lax.axis_index(both) % 2, gx % 2]
-    ).astype(jnp.int32)
+    last_y = lax.axis_size("gy") - 1
+    places = [gy > 0, gy < last_y, gx > 0, gx < peers - 1, lax.axis_index(both) % 2, gx % 2, gy % 2]
+    lane = lax.broadcasted_iota(jnp.int32, (1, count), 1)
+    flags = sum(jnp.where(lane == k, jnp.int32(v), 0) for k, v in enumerate(places))
+    links = jnp.concatenate([links.T, flags], 0)
     face = pltpu.VMEM((faces, ch), BF16)
-    first, second = call(
-        pack_kernel, "pack", (face_shape, face_shape), (flags, links), (x,), (wide, face, face)
-    )
+    first, second = call(pack_kernel, (face_shape, face_shape), (links,), (x,), (wide, face, face))
     first, second = swap(first, second, both)
-    partial = call(first_interior_kernel, "inside1", part_shape, (links,), (x, w_first))
+    partial = call(first_interior_kernel, part_shape, (links,), (x, w_first))
     hidden, first, second = call(
         hidden_kernel,
-        "hidden",
         (jax.ShapeDtypeStruct((rows, ch), BF16), face_shape, face_shape),
-        (flags, links),
+        (links,),
         (partial, first, second, w_first),
         (wide, face, face, face, face),
     )
     first, second = swap(first, second, both)
-    partial = call(second_interior_kernel, "inside2", part_shape, (links,), (hidden, x, w_second))
+    partial = call(second_interior_kernel, part_shape, (links,), (hidden, x, w_second))
     outgoing = call(
         lift_kernel,
-        "lift",
         jax.ShapeDtypeStruct((peers, per_peer * FACE + ID_ROWS, mapped), BF16),
-        (flags, links, slots, block_levels, slot_column),
+        (links, slots, block_levels, slot_column),
         (partial, first, second, w_second, height_w),
         (
             wide,
@@ -512,33 +523,30 @@
     arrived = lax.all_to_all(outgoing, "gx", split_axis=0, concat_axis=0, tiled=True)
 
     row_shape = jax.ShapeDtypeStruct((HALO * COLS, mapped), BF16)
-    side_shape = jax.ShapeDtypeStruct((HALO, ROWS, mapped), BF16)
-    bev, top, bottom, left, right = call(
+    row = pltpu.VMEM((HALO * COLS, mapped), BF16)
+    bev, first, second, own = call(
         gather_kernel,
-        "gather",
         (
             jax.ShapeDtypeStruct((ROWS * COLS, mapped), BF16),
             row_shape,
             row_shape,
-            side_shape,
-            side_shape,
+            jax.ShapeDtypeStruct((2 * HALO, ROWS, mapped), BF16),
         ),
-        (),
+        (links,),
         (arrived,),
-        (pltpu.VMEM((mapped // LANES, ROWS * COLS, LANES), F32),),
-    )
-    above = shift(bottom, "gy", 1)
-    below = shift(top, "gy", -1)
+        (pltpu.VMEM((mapped // LANES, ROWS * COLS, LANES), F32), row, row),
+    )
+    first_row, second_row = swap(first, second, "gy")
     inner = call(
         first_inner_kernel,
-        "first_inner",
         jax.ShapeDtypeStruct((INNER_ROWS * COLS, mapped), BF16),
         (),
         (bev, k_first),
     )
-    above, below, inner = lax.optimization_barrier((above, below, inner))
-    corner_above = above.reshape(HALO, COLS, mapped)
-    corner_below = below.reshape(HALO, COLS, mapped)
+    first_row, second_row, inner = lax.optimization_barrier((first_row, second_row, inner))
+    odd_y, odd_x = gy % 2 == 1, gx % 2 == 1
+    corner_above = jnp.where(odd_y, first_row, second_row).reshape(HALO, COLS, mapped)
+    corner_below = jnp.where(odd_y, second_row, first_row).reshape(HALO, COLS, mapped)
 
     def side(own, at):
         return jnp.concatenate(
@@ -550,39 +558,28 @@
             1,
         )
 
-    own_left, own_right = side(left, 0), side(right, COLS - HALO)
-    odd = gx % 2 == 1
+    own_left, own_right = side(own[:HALO], 0), side(own[HALO:], COLS - HALO)
     first, second = swap(
-        jnp.where(odd, own_left, own_right), jnp.where(odd, own_right, own_left), "gx"
-    )
-    core = call(
+        jnp.where(odd_x, own_left, own_right), jnp.where(odd_x, own_right, own_left), "gx"
+    )
+    middle, flanks = call(
         second_core_kernel,
-        "second_core",
-        jax.ShapeDtypeStruct((mapped // LANES, CORE_ROWS * COLS, LANES), F32),
-        (),
-        (inner, bev, k_second),
+        (
+            jax.ShapeDtypeStruct((ROWS * COLS, mapped), BF16),
+            jax.ShapeDtypeStruct((mapped // LANES, 2 * ROWS * EDGE, LANES), F32),
+        ),
+        (links,),
+        (inner, bev, first_row, second_row, k_first, k_second),
+        (row, row),
     )
     out = call(
         edges_kernel,
-        "edges",
         jax.ShapeDtypeStruct((ROWS * COLS, mapped), BF16),
-        (flags,),
-        (
-            bev,
-            inner,
-            core,
-            above,
-            below,
-            own_left,
-            own_right,
-            first,
-            second,
-            k_first,
-            k_second,
-        ),
+        (links,),
+        (middle, flanks, own_left, own_right, first, second, k_first, k_second),
         (
             pltpu.VMEM((8, RIM_ROWS + EDGE, mapped), F32),
-            pltpu.VMEM((mapped // LANES, ROWS * COLS, LANES), F32),
+            pltpu.VMEM((mapped // LANES, 2 * ROWS * EDGE, LANES), F32),
         ),
     )
     return out.reshape(ROWS, COLS, mapped)
@@ -602,4 +599,5 @@
         P(),
     )
     out_specs = P("gy", "gx", None)
+
     return jax.shard_map(local, mesh=mesh, in_specs=in_specs, out_specs=out_specs, check_vma=False)

time: 80.6 us -> 77.9 us (0.967)
  the two profiles are of different devices: /device:TPU:9 before, /device:TPU:1 now
where the time goes in v5:
time: 77.9 us; the launch traced here: 77.5 us
  starting transfers between devices  29.5 us (38%)
  Pallas kernels  25.7 us (33%)
  waiting for transfers between devices  18.9 us (24%)
  local copies, waits for them, and re-layouts  2.24 us (3%)
  other arithmetic  0.78 us (1%)
    pallas_call x9, Pallas kernels, call(): pl.pallas_call(kernel, out_shape=out_shape, in_specs=[SMEM] * len(scalars...  25.7 us
    ppermute x4, starting transfers between devices, swap(): second = lax.ppermute(second, axis, far)  15.5 us
    all_to_all x1, waiting for transfers between devices, local(): lax.all_to_all(outgoing, 'gx', split_axis=0, concat_axis=0, tiled=True)  15.1 us
    ppermute x4, starting transfers between devices, swap(): first = lax.ppermute(first, axis, near)  7.23 us
    all_to_all x1, starting transfers between devices, local(): lax.all_to_all(outgoing, 'gx', split_axis=0, concat_axis=0, tiled=True)  6.81 us
    ppermute x4, waiting for transfers between devices, swap(): second = lax.ppermute(second, axis, far)  3.3 us
    unnamed x20, local copies, waits for them, and re-layouts  2.21 us
  transfers between devices with their start and end apart: 9, of which 5 were waited for; matrix products, arithmetic and copies ran while one was open for 0% of the time, Pallas kernels for 19%

profile of v5, /device:TPU:1, one launch (start us, length us, event | category | flops | bytes accessed | tf_op | source)
XLA Modules:
  0.0 77.5 jit_solution(6120082249022731836)
XLA Ops:
  0.0 0.7 pad_add_fusion.links
  0.7 1.2 %copy-done.1 = bf16[8,512,128]{2,1,0:T(8,128)(2,1)S(1)} copy-done((bf16[8,512,128]{2,1,0:T(8,128)(2,1)S(1)}, bf16[8,512,128]{2,1,0:T(8,128)(2,1)}, u32[]{:S(2)}) %copy-start.1) | copy-done | bytes 1048600
  1.9 0.9 %shard_map.101 = (bf16[1088,128]{1,0:T(8,128)(2,1)S(1)}, bf16[1088,128]{1,0:T(8,128)(2,1)S(1)}) custom-call(s32[4,8]{1,0:T(4,128)S(1)} %pad_add_fusion.links, bf16[4096,128]{1,0:T(8,128)(2,1)S(1)} %bitcast.22), custom_call_target="tpu_custom_call" | custom-call | tf_op jit(solution)/shard_map/pallas_call | solution.py:449
  2.9 2.1 %collective-permute-start = (bf16[1088,128]{1,0:T(8,128)(2,1)S(1)}, bf16[1088,128]{1,0:T(8,128)(2,1)S(1)}, u32[]{:S(2)}, u32[]{:S(2)}) collective-permute-start(bf16[1088,128]{1,0:T(8,128)(2,1)S(1)} %get-tuple-element.19), channel_id=1, source_target_pairs={{0,1},{1,0},{2,3},{3,2},{4,5},{5,4},{6,7},{7,6},{8,9},{9,8},{10,11... | collective-permute-start | bytes 835592 | tf_op jit(solution)/shard_map/ppermute | solution.py:31
  5.0 6.0 %collective-permute-start.1 = (bf16[1088,128]{1,0:T(8,128)(2,1)S(1)}, bf16[1088,128]{1,0:T(8,128)(2,1)S(1)}, u32[]{:S(2)}, u32[]{:S(2)}) collective-permute-start(bf16[1088,128]{1,0:T(8,128)(2,1)S(1)} %get-tuple-element.20), channel_id=1, source_target_pairs={{1,2},{2,1},{3,4},{4,3},{5,6},{6,5},{7,8},{8,7},{9,10},{10,9},{11,... | collective-permute-start | bytes 835592 | tf_op jit(solution)/shard_map/ppermute | solution.py:32
  11.0 0.9 %copy-done.5 = bf16[7,128,128]{2,1,0:T(8,128)(2,1)S(1)} copy-done((bf16[7,128,128]{2,1,0:T(8,128)(2,1)S(1)}, bf16[7,128,128]{2,1,0:T(8,128)(2,1)}, u32[]{:S(2)}) %copy-start.5) | copy-done | bytes 229400
  12.0 3.8 %shard_map.100.partial = f32[4096,128]{1,0:T(8,128)S(1)} custom-call(s32[4,8]{1,0:T(4,128)S(1)} %pad_add_fusion.links, bf16[4096,128]{1,0:T(8,128)(2,1)S(1)} %bitcast.23, bf16[896,128]{1,0:T(8,128)(2,1)S(1)} %bitcast.27), custom_call_target="tpu_custom_call" | custom-call | tf_op jit(solution)/shard_map/pallas_call | solution.py:449
  16.3 1.0 %collective-permute-done.1.second_in = bf16[1088,128]{1,0:T(8,128)(2,1)S(1)} collective-permute-done((bf16[1088,128]{1,0:T(8,128)(2,1)S(1)}, bf16[1088,128]{1,0:T(8,128)(2,1)S(1)}, u32[]{:S(2)}, u32[]{:S(2)}) %collective-permute-start.1) | collective-permute-done | bytes 278560 | tf_op jit(solution)/shard_map/ppermute | solution.py:32
  17.3 1.5 %shard_map.102 = (bf16[4096,128]{1,0:T(8,128)(2,1)S(1)}, bf16[1088,128]{1,0:T(8,128)(2,1)S(1)}, bf16[1088,128]{1,0:T(8,128)(2,1)S(1)}) custom-call(s32[4,8]{1,0:T(4,128)S(1)} %pad_add_fusion.links, f32[4096,128]{1,0:T(8,128)S(1)} %shard_map.100.partial, bf16[1088,128]{1,0:T(8,128)(2,1)S(1)} %collective-permute-done.first_in, ...), custom_call_target="tpu_custom_call" | custom-call | tf_op jit(solution)/shard_map/pallas_call | solution.py:449
  18.7 1.3 %collective-permute-start.2 = (bf16[1088,128]{1,0:T(8,128)(2,1)S(1)}, bf16[1088,128]{1,0:T(8,128)(2,1)S(1)}, u32[]{:S(2)}, u32[]{:S(2)}) collective-permute-start(bf16[1088,128]{1,0:T(8,128)(2,1)S(1)} %get-tuple-element.22), channel_id=1, source_target_pairs={{0,1},{1,0},{2,3},{3,2},{4,5},{5,4},{6,7},{7,6},{8,9},{9,8},{10,11... | collective-permute-start | bytes 835592 | tf_op jit(solution)/shard_map/ppermute | solution.py:31
  20.0 6.9 %collective-permute-start.3 = (bf16[1088,128]{1,0:T(8,128)(2,1)S(1)}, bf16[1088,128]{1,0:T(8,128)(2,1)S(1)}, u32[]{:S(2)}, u32[]{:S(2)}) collective-permute-start(bf16[1088,128]{1,0:T(8,128)(2,1)S(1)} %get-tuple-element.23), channel_id=1, source_target_pairs={{1,2},{2,1},{3,4},{4,3},{5,6},{6,5},{7,8},{8,7},{9,10},{10,9},{11,... | collective-permute-start | bytes 835592 | tf_op jit(solution)/shard_map/ppermute | solution.py:32
  27.0 3.8 %shard_map.103.partial = f32[4096,128]{1,0:T(8,128)S(1)} custom-call(s32[4,8]{1,0:T(4,128)S(1)} %pad_add_fusion.links, bf16[4096,128]{1,0:T(8,128)(2,1)S(1)} %get-tuple-element.21.hidden, bf16[4096,128]{1,0:T(8,128)(2,1)S(1)} %bitcast.24, bf16[896,128]{1,0:T(8,128)(2,1)S(1)} %bitcast.29), custom_call_target="tpu_custom_call" | custom-call | tf_op jit(solution)/shard_map/pallas_call | solution.py:449
  30.8 1.8 %collective-permute-done.3.second_in = bf16[1088,128]{1,0:T(8,128)(2,1)S(1)} collective-permute-done((bf16[1088,128]{1,0:T(8,128)(2,1)S(1)}, bf16[1088,128]{1,0:T(8,128)(2,1)S(1)}, u32[]{:S(2)}, u32[]{:S(2)}) %collective-permute-start.3) | collective-permute-done | bytes 278560 | tf_op jit(solution)/shard_map/ppermute | solution.py:32
  32.6 4.2 %shard_map.104 = bf16[8,136,256]{2,1,0:T(8,128)(2,1)} custom-call(s32[4,8]{1,0:T(4,128)S(1)} %pad_add_fusion.links, s32[1,8]{1,0:T(1,128)S(1)} %bitcast.31, s32[1,8]{1,0:T(1,128)S(1)} %bitcast.32, s32[1,16]{1,0:T(1,128)S(1)} %copy-done.9, f32[4096,128]{1,0:T(8,128)S(1)} %shard_map.103.partial, bf16[1088,128]{1,0:T(8,128)(2,1)S(1)} %collective-permute-done.2.first_in, ...), custom_call_target="tpu_custom_call" | custom-call | tf_op jit(solution)/shard_map/pallas_call | solution.py:449
  36.8 6.8 %all-to-all-start = ((bf16[8,136,256]{2,1,0:T(8,128)(2,1)}), bf16[8,136,256]{2,1,0:T(8,128)(2,1)S(1)}, u32[]{:S(2)}, u32[]{:S(2)}) async-start(bf16[8,136,256]{2,1,0:T(8,128)(2,1)} %shard_map.104), calls=%async_computation | async-start | bytes 1114112 | tf_op jit(solution)/shard_map/all_to_all | solution.py:523
  43.6 15.1 %all-to-all-done.arrived = bf16[8,136,256]{2,1,0:T(8,128)(2,1)S(1)} async-done(((bf16[8,136,256]{2,1,0:T(8,128)(2,1)}), bf16[8,136,256]{2,1,0:T(8,128)(2,1)S(1)}, u32[]{:S(2)}, u32[]{:S(2)}) %all-to-all-start) | async-done | bytes 557088 | tf_op jit(solution)/shard_map/all_to_all | solution.py:523
  58.7 1.3 %shard_map.105 = (bf16[2048,256]{1,0:T(8,128)(2,1)S(1)}, bf16[64,256]{1,0:T(8,128)(2,1)S(1)}, bf16[64,256]{1,0:T(8,128)(2,1)S(1)}, bf16[4,64,256]{2,1,0:T(8,128)(2,1)S(1)}) custom-call(s32[4,8]{1,0:T(4,128)S(1)} %pad_add_fusion.links, bf16[8,136,256]{2,1,0:T(8,128)(2,1)S(1)} %all-to-all-done.arrived), custom_call_target="tpu_custom_call" | custom-call | tf_op jit(solution)/shard_map/pallas_call | solution.py:449
  60.0 1.1 %collective-permute-start.4 = (bf16[64,256]{1,0:T(8,128)(2,1)S(1)}, bf16[64,256]{1,0:T(8,128)(2,1)S(1)}, u32[]{:S(2)}, u32[]{:S(2)}) collective-permute-start(bf16[64,256]{1,0:T(8,128)(2,1)S(1)} %get-tuple-element.24), channel_id=1, source_target_pairs={{0,8},{8,0},{16,24},{24,16},{1,9},{9,1},{17,25},{25,17},{2,10},{10... | collective-permute-start | bytes 98312 | tf_op jit(solution)/shard_map/ppermute | solution.py:31
  61.1 1.9 %collective-permute-start.5 = (bf16[64,256]{1,0:T(8,128)(2,1)S(1)}, bf16[64,256]{1,0:T(8,128)(2,1)S(1)}, u32[]{:S(2)}, u32[]{:S(2)}) collective-permute-start(bf16[64,256]{1,0:T(8,128)(2,1)S(1)} %get-tuple-element.25), channel_id=1, source_target_pairs={{8,16},{16,8},{9,17},{17,9},{10,18},{18,10},{11,19},{19,11},{12,20... | collective-permute-start | bytes 98312 | tf_op jit(solution)/shard_map/ppermute | solution.py:32
  63.0 2.7 %shard_map.106.inner = bf16[1984,256]{1,0:T(8,128)(2,1)S(1)} custom-call(bf16[2048,256]{1,0:T(8,128)(2,1)S(1)} %get-tuple-element.26.bev, bf16[9,256,256]{2,1,0:T(8,128)(2,1)S(1)} %bitcast.19), custom_call_target="tpu_custom_call" | custom-call | tf_op jit(solution)/shard_map/pallas_call | solution.py:449
  66.5 0.7 collective-permute-start.7
  67.1 2.8 %collective-permute-start.6 = (bf16[2,68,256]{2,1,0:T(8,128)(2,1)S(1)}, bf16[2,68,256]{2,1,0:T(8,128)(2,1)S(1)}, u32[]{:S(2)}, u32[]{:S(2)}) collective-permute-start(bf16[2,68,256]{2,1,0:T(8,128)(2,1)S(1)} %get-tuple-element.34), channel_id=1, source_target_pairs={{0,1},{1,0},{2,3},{3,2},{4,5},{5,4},{6,7},{7,6},{8,9},{9,8},{10,11... | collective-permute-start | bytes 208904 | tf_op jit(solution)/shard_map/ppermute | solution.py:31
  69.9 4.3 %shard_map.107 = (bf16[2048,256]{1,0:T(8,128)(2,1)S(1)}, f32[2,1024,128]{2,1,0:T(8,128)S(1)}) custom-call(s32[4,8]{1,0:T(4,128)S(1)} %pad_add_fusion.links, bf16[1984,256]{1,0:T(8,128)(2,1)S(1)} %shard_map.106.inner, bf16[2048,256]{1,0:T(8,128)(2,1)S(1)} %get-tuple-element.26.bev, bf16[64,256]{1,0:T(8,128)(2,1)S(1)} %collective-permute-done.4.first_row, ...), custom_call_target="tpu_custom_call" | custom-call | tf_op jit(solution)/shard_map/pallas_call | solution.py:449
  74.2 3.3 %shard_map.108 = bf16[2048,256]{1,0:T(8,128)(2,1)} custom-call(s32[4,8]{1,0:T(4,128)S(1)} %pad_add_fusion.links, bf16[2048,256]{1,0:T(8,128)(2,1)S(1)} %get-tuple-element.30.middle, f32[2,1024,128]{2,1,0:T(8,128)S(1)} %get-tuple-element.31.flanks, bf16[2,68,256]{2,1,0:T(8,128)(2,1)S(1)} %get-tuple-element.37.own_left, ...), custom_call_target="tpu_custom_call" | custom-call | tf_op jit(solution)/shard_map/pallas_call | solution.py:449
  (32 shorter events, 1.2 us)
Async XLA Ops:
  0.7 1.2 %copy-start.1 = (bf16[8,512,128]{2,1,0:T(8,128)(2,1)S(1)}, bf16[8,512,128]{2,1,0:T(8,128)(2,1)}, u32[]{:S(2)}) copy-start(bf16[8,512,128]{2,1,0:T(8,128)(2,1)} %param.10) | copy-start | bytes 3145732
  2.9 13.4 %collective-permute-start = (bf16[1088,128]{1,0:T(8,128)(2,1)S(1)}, bf16[1088,128]{1,0:T(8,128)(2,1)S(1)}, u32[]{:S(2)}, u32[]{:S(2)}) collective-permute-start(bf16[1088,128]{1,0:T(8,128)(2,1)S(1)} %get-tuple-element.19), channel_id=1, source_target_pairs={{0,1},{1,0},{2,3},{3,2},{4,5},{5,4},{6,7},{7,6},{8,9},{9,8},{10,11... | collective-permute-start | bytes 835592 | tf_op jit(solution)/shard_map/ppermute | solution.py:31
  5.0 12.3 %collective-permute-start.1 = (bf16[1088,128]{1,0:T(8,128)(2,1)S(1)}, bf16[1088,128]{1,0:T(8,128)(2,1)S(1)}, u32[]{:S(2)}, u32[]{:S(2)}) collective-permute-start(bf16[1088,128]{1,0:T(8,128)(2,1)S(1)} %get-tuple-element.20), channel_id=1, source_target_pairs={{1,2},{2,1},{3,4},{4,3},{5,6},{6,5},{7,8},{8,7},{9,10},{10,9},{11,... | collective-permute-start | bytes 835592 | tf_op jit(solution)/shard_map/ppermute | solution.py:32
  11.0 0.9 %copy-start.5 = (bf16[7,128,128]{2,1,0:T(8,128)(2,1)S(1)}, bf16[7,128,128]{2,1,0:T(8,128)(2,1)}, u32[]{:S(2)}) copy-start(bf16[7,128,128]{2,1,0:T(8,128)(2,1)} %param.15) | copy-start | bytes 688132
  15.8 11.1 %copy-start.2 = (bf16[8,512,128]{2,1,0:T(8,128)(2,1)S(1)}, bf16[8,512,128]{2,1,0:T(8,128)(2,1)}, u32[]{:S(2)}) copy-start(bf16[8,512,128]{2,1,0:T(8,128)(2,1)} %param.10) | copy-start | bytes 3145732
  15.8 11.1 %copy-start.6 = (bf16[7,128,128]{2,1,0:T(8,128)(2,1)S(1)}, bf16[7,128,128]{2,1,0:T(8,128)(2,1)}, u32[]{:S(2)}) copy-start(bf16[7,128,128]{2,1,0:T(8,128)(2,1)} %param.16) | copy-start | bytes 688132
  18.7 12.1 %collective-permute-start.2 = (bf16[1088,128]{1,0:T(8,128)(2,1)S(1)}, bf16[1088,128]{1,0:T(8,128)(2,1)S(1)}, u32[]{:S(2)}, u32[]{:S(2)}) collective-permute-start(bf16[1088,128]{1,0:T(8,128)(2,1)S(1)} %get-tuple-element.22), channel_id=1, source_target_pairs={{0,1},{1,0},{2,3},{3,2},{4,5},{5,4},{6,7},{7,6},{8,9},{9,8},{10,11... | collective-permute-start | bytes 835592 | tf_op jit(solution)/shard_map/ppermute | solution.py:31
  20.0 12.6 %collective-permute-start.3 = (bf16[1088,128]{1,0:T(8,128)(2,1)S(1)}, bf16[1088,128]{1,0:T(8,128)(2,1)S(1)}, u32[]{:S(2)}, u32[]{:S(2)}) collective-permute-start(bf16[1088,128]{1,0:T(8,128)(2,1)S(1)} %get-tuple-element.23), channel_id=1, source_target_pairs={{1,2},{2,1},{3,4},{4,3},{5,6},{6,5},{7,8},{8,7},{9,10},{10,9},{11,... | collective-permute-start | bytes 835592 | tf_op jit(solution)/shard_map/ppermute | solution.py:32
  26.9 5.7 %copy-start.4 = (bf16[4,1024,256]{2,1,0:T(8,128)(2,1)S(1)}, bf16[4,1024,256]{2,1,0:T(8,128)(2,1)}, u32[]{:S(2)}) copy-start(bf16[4,1024,256]{2,1,0:T(8,128)(2,1)} %height.1) | copy-start | bytes 6291460
  26.9 5.7 %copy-start.7 = (s32[8]{0:T(128)S(1)}, s32[8]{0:T(128)}, u32[]{:S(2)}) copy-start(s32[8]{0:T(128)} %param.12) | copy-start | bytes 100
  26.9 5.7 %copy-start.8 = (s32[8]{0:T(128)S(1)}, s32[8]{0:T(128)}, u32[]{:S(2)}) copy-start(s32[8]{0:T(128)} %param.13) | copy-start | bytes 100
  27.0 5.6 %copy-start.9 = (s32[1,16]{1,0:T(1,128)S(1)}, s32[1,16]{1,0:T(1,128)}, u32[]{:S(2)}) copy-start(s32[1,16]{1,0:T(1,128)} %columns.1) | copy-start | bytes 196
  36.8 26.3 %copy-start = (bf16[3,3,256,256]{3,2,1,0:T(8,128)(2,1)S(1)}, bf16[3,3,256,256]{3,2,1,0:T(8,128)(2,1)}, u32[]{:S(2)}) copy-start(bf16[3,3,256,256]{3,2,1,0:T(8,128)(2,1)} %param.18) | copy-start | bytes 3538948
  36.8 21.9 %all-to-all-start = ((bf16[8,136,256]{2,1,0:T(8,128)(2,1)}), bf16[8,136,256]{2,1,0:T(8,128)(2,1)S(1)}, u32[]{:S(2)}, u32[]{:S(2)}) async-start(bf16[8,136,256]{2,1,0:T(8,128)(2,1)} %shard_map.104), calls=%async_computation | async-start | bytes 1114112 | tf_op jit(solution)/shard_map/all_to_all | solution.py:523
  60.0 9.9 %copy-start.3 = (bf16[3,3,256,256]{3,2,1,0:T(8,128)(2,1)S(1)}, bf16[3,3,256,256]{3,2,1,0:T(8,128)(2,1)}, u32[]{:S(2)}) copy-start(bf16[3,3,256,256]{3,2,1,0:T(8,128)(2,1)} %param.19) | copy-start | bytes 3538948
  60.0 5.8 %collective-permute-start.4 = (bf16[64,256]{1,0:T(8,128)(2,1)S(1)}, bf16[64,256]{1,0:T(8,128)(2,1)S(1)}, u32[]{:S(2)}, u32[]{:S(2)}) collective-permute-start(bf16[64,256]{1,0:T(8,128)(2,1)S(1)} %get-tuple-element.24), channel_id=1, source_target_pairs={{0,8},{8,0},{16,24},{24,16},{1,9},{9,1},{17,25},{25,17},{2,10},{10... | collective-permute-start | bytes 98312 | tf_op jit(solution)/shard_map/ppermute | solution.py:31
  61.1 5.2 %collective-permute-start.5 = (bf16[64,256]{1,0:T(8,128)(2,1)S(1)}, bf16[64,256]{1,0:T(8,128)(2,1)S(1)}, u32[]{:S(2)}, u32[]{:S(2)}) collective-permute-start(bf16[64,256]{1,0:T(8,128)(2,1)S(1)} %get-tuple-element.25), channel_id=1, source_target_pairs={{8,16},{16,8},{9,17},{17,9},{10,18},{18,10},{11,19},{19,11},{12,20... | collective-permute-start | bytes 98312 | tf_op jit(solution)/shard_map/ppermute | solution.py:32
  66.5 7.8 %collective-permute-start.7 = (bf16[2,68,256]{2,1,0:T(8,128)(2,1)S(1)}, bf16[2,68,256]{2,1,0:T(8,128)(2,1)S(1)}, u32[]{:S(2)}, u32[]{:S(2)}) collective-permute-start(bf16[2,68,256]{2,1,0:T(8,128)(2,1)S(1)} %get-tuple-element.33), channel_id=1, source_target_pairs={{1,2},{2,1},{3,4},{4,3},{5,6},{6,5},{9,10},{10,9},{11,12},{12,11},... | collective-permute-start | bytes 208904 | tf_op jit(solution)/shard_map/ppermute | solution.py:32
  67.1 7.1 %collective-permute-start.6 = (bf16[2,68,256]{2,1,0:T(8,128)(2,1)S(1)}, bf16[2,68,256]{2,1,0:T(8,128)(2,1)S(1)}, u32[]{:S(2)}, u32[]{:S(2)}) collective-permute-start(bf16[2,68,256]{2,1,0:T(8,128)(2,1)S(1)} %get-tuple-element.34), channel_id=1, source_target_pairs={{0,1},{1,0},{2,3},{3,2},{4,5},{5,4},{6,7},{7,6},{8,9},{9,8},{10,11... | collective-permute-start | bytes 208904 | tf_op jit(solution)/shard_map/ppermute | solution.py:31

commit v6 on v5

--- a/solution.py
+++ b/solution.py
@@ -31,6 +31,11 @@
     first = lax.ppermute(first, axis, near)
     second = lax.ppermute(second, axis, far)
     return first, second
+
+
+def trade_order(count):
+    assert count & (count - 1) == 0
+    return [*range(count // 2, count), *range(1, count // 2)]
 
 
 def route(odd, up, down, first, second):
@@ -196,13 +201,9 @@
     second_in,
     weights,
     height,
-    out,
-    total,
-    rows_in,
-    sums,
-    from_below,
-    from_above,
+    *refs,
 ):
+    *outs, total, rows_in, sums, from_below, from_above = refs
     count = partial.shape[0] // CELLS
     faces = count * FACE
     ch = partial.shape[1]
@@ -220,32 +221,38 @@
         return carry
 
     lax.fori_loop(0, count, one, 0)
-    peers = out.shape[0]
+    peers = len(outs)
     per_peer = sums.shape[0] // peers
-    row_at = lax.broadcasted_iota(jnp.int32, (ID_ROWS, out.shape[2]), 0)
-    for p in range(peers):
+    row_at = lax.broadcasted_iota(jnp.int32, (ID_ROWS, LANES), 0)
+    for k, out in enumerate(outs):
         ids = jnp.zeros(row_at.shape, F32)
-        for k in range(per_peer):
-            slot = p * per_peer + k
-            out[p, k * FACE : (k + 1) * FACE, :] = sums[slot].astype(BF16)
-            ids = jnp.where(row_at == k, columns[0, slot].astype(F32), ids)
-        out[p, per_peer * FACE :, :] = ids.astype(BF16)
-
-
-def gather_kernel(links, arrived, bev, first, second, own, total, top, bottom):
-    peers, rows, ch = arrived.shape
-    per_peer = (rows - ID_ROWS) // FACE
+        for i in range(per_peer):
+            slot = (links[3, 7] ^ k) * per_peer + i
+            block = sums[slot].astype(BF16)
+            for h, lanes in halves(block.shape[1]):
+                at = (h * per_peer + i) * FACE
+                out[at : at + FACE, :] = block[:, lanes]
+            ids = jnp.where(row_at == i, columns[0, slot].astype(F32), ids)
+        out[out.shape[0] - ID_ROWS :, :] = ids.astype(BF16)
+
+
+def gather_kernel(links, *refs):
+    *arrived, bev, first, second, own, total, top, bottom = refs
+    ch = bev.shape[1]
+    parts = ch // LANES
+    per_peer = (arrived[0].shape[0] - ID_ROWS) // (parts * FACE)
     total[...] = jnp.zeros_like(total)
-    for p in range(peers):
-        ids = arrived[p, per_peer * FACE :, :].astype(F32)
+    for source in arrived:
+        ids = source[source.shape[0] - ID_ROWS :, :].astype(F32)
         for k in range(per_peer):
             column = jnp.max(ids[k : k + 1, :]).astype(jnp.int32)
             row_base = (column // TILE_BC) * (EDGE * COLS) + (column % TILE_BC) * EDGE
-            block = arrived[p, k * FACE : (k + 1) * FACE, :].astype(F32)
-            for a in range(EDGE):
-                at = pl.multiple_of(row_base + a * COLS, EDGE)
-                for h, lanes in halves(ch):
-                    total[h, pl.ds(at, EDGE), :] += block[a * EDGE : (a + 1) * EDGE, lanes]
+            for h in range(parts):
+                start = (h * per_peer + k) * FACE
+                block = source[start : start + FACE, :].astype(F32)
+                for a in range(EDGE):
+                    at = pl.multiple_of(row_base + a * COLS, EDGE)
+                    total[h, pl.ds(at, EDGE), :] += block[a * EDGE : (a + 1) * EDGE, :]
     for h, lanes in halves(ch):
         bev[:, lanes] = total[h].astype(BF16)
         top[:, lanes] = total[h, 0 : HALO * COLS, :].astype(BF16)
@@ -490,7 +497,7 @@
 
     gy, gx = lax.axis_index("gy"), lax.axis_index("gx")
     last_y = lax.axis_size("gy") - 1
-    places = [gy > 0, gy < last_y, gx > 0, gx < peers - 1, lax.axis_index(both) % 2, gx % 2, gy % 2]
+    places = [gy > 0, gy < last_y, gx > 0, gx < peers - 1, lax.axis_index(both) % 2, gx % 2, gy % 2, gx]
     lane = lax.broadcasted_iota(jnp.int32, (1, count), 1)
     flags = sum(jnp.where(lane == k, jnp.int32(v), 0) for k, v in enumerate(places))
     links = jnp.concatenate([links.T, flags], 0)
@@ -507,9 +514,10 @@
     )
     first, second = swap(first, second, both)
     partial = call(second_interior_kernel, part_shape, (links,), (hidden, x, w_second))
+    payload = (mapped // LANES * per_peer * FACE + ID_ROWS, LANES)
     outgoing = call(
         lift_kernel,
-        jax.ShapeDtypeStruct((peers, per_peer * FACE + ID_ROWS, mapped), BF16),
+        [jax.ShapeDtypeStruct(payload, BF16)] * peers,
         (links, slots, block_levels, slot_column),
         (partial, first, second, w_second, height_w),
         (
@@ -520,7 +528,9 @@
             face,
         ),
     )
-    arrived = lax.all_to_all(outgoing, "gx", split_axis=0, concat_axis=0, tiled=True)
+    arrived = list(outgoing)
+    for k in trade_order(peers):
+        arrived[k] = lax.ppermute(outgoing[k], "gx", [(i, i ^ k) for i in range(peers)])
 
     row_shape = jax.ShapeDtypeStruct((HALO * COLS, mapped), BF16)
     row = pltpu.VMEM((HALO * COLS, mapped), BF16)
@@ -533,7 +543,7 @@
             jax.ShapeDtypeStruct((2 * HALO, ROWS, mapped), BF16),
         ),
         (links,),
-        (arrived,),
+        arrived,
         (pltpu.VMEM((mapped // LANES, ROWS * COLS, LANES), F32), row, row),
     )
     first_row, second_row = swap(first, second, "gy")

time: 77.9 us -> 75 us (0.963)
  the two profiles are of different devices: /device:TPU:1 before, /device:TPU:9 now
where the time goes in v6:
time: 75 us; the launch traced here: 74.1 us
  Pallas kernels  24.9 us (33%)
  starting transfers between devices  24.6 us (33%)
  waiting for transfers between devices  21.3 us (28%)
  local copies, waits for them, and re-layouts  2.25 us (3%)
  other arithmetic  0.78 us (1%)
    pallas_call x9, Pallas kernels, call(): pl.pallas_call(kernel, out_shape=out_shape, in_specs=[SMEM] * len(scalars...  24.9 us
    ppermute x7, starting transfers between devices, local(): lax.ppermute(outgoing[k], 'gx', [(i, i ^ k) for i in range(peers)])  10.7 us
    ppermute x7, waiting for transfers between devices, local(): lax.ppermute(outgoing[k], 'gx', [(i, i ^ k) for i in range(peers)])  10.7 us
    ppermute x4, waiting for transfers between devices, swap(): first = lax.ppermute(first, axis, near)  10.1 us
    ppermute x4, starting transfers between devices, swap(): second = lax.ppermute(second, axis, far)  8.03 us
    ppermute x4, starting transfers between devices, swap(): first = lax.ppermute(first, axis, near)  5.86 us
    unnamed x20, local copies, waits for them, and re-layouts  2.21 us
  transfers between devices with their start and end apart: 15, of which 7 were waited for; matrix products, arithmetic and copies ran while one was open for 0% of the time, Pallas kernels for 20%

profile of v6, /device:TPU:9, one launch (start us, length us, event | category | flops | bytes accessed | tf_op | source)
XLA Modules:
  0.0 74.1 jit_solution(12363018924884383824)
XLA Ops:
  0.7 1.2 %copy-done.1 = bf16[8,512,128]{2,1,0:T(8,128)(2,1)S(1)} copy-done((bf16[8,512,128]{2,1,0:T(8,128)(2,1)S(1)}, bf16[8,512,128]{2,1,0:T(8,128)(2,1)}, u32[]{:S(2)}) %copy-start.1) | copy-done | bytes 1048600
  2.9 1.3 %collective-permute-start = (bf16[1088,128]{1,0:T(8,128)(2,1)S(1)}, bf16[1088,128]{1,0:T(8,128)(2,1)S(1)}, u32[]{:S(2)}, u32[]{:S(2)}) collective-permute-start(bf16[1088,128]{1,0:T(8,128)(2,1)S(1)} %get-tuple-element.27), channel_id=1, source_target_pairs={{0,1},{1,0},{2,3},{3,2},{4,5},{5,4},{6,7},{7,6},{8,9},{9,8},{10,11... | collective-permute-start | bytes 835592 | tf_op jit(solution)/shard_map/ppermute | solution.py:31
  4.2 1.9 %collective-permute-start.1 = (bf16[1088,128]{1,0:T(8,128)(2,1)S(1)}, bf16[1088,128]{1,0:T(8,128)(2,1)S(1)}, u32[]{:S(2)}, u32[]{:S(2)}) collective-permute-start(bf16[1088,128]{1,0:T(8,128)(2,1)S(1)} %get-tuple-element.28), channel_id=1, source_target_pairs={{1,2},{2,1},{3,4},{4,3},{5,6},{6,5},{7,8},{8,7},{9,10},{10,9},{11,... | collective-permute-start | bytes 835592 | tf_op jit(solution)/shard_map/ppermute | solution.py:32
  7.0 3.8 %shard_map.100.partial = f32[4096,128]{1,0:T(8,128)S(1)} custom-call(s32[4,8]{1,0:T(4,128)S(1)} %pad_add_fusion.links, bf16[4096,128]{1,0:T(8,128)(2,1)S(1)} %bitcast.23, bf16[896,128]{1,0:T(8,128)(2,1)S(1)} %bitcast.27), custom_call_target="tpu_custom_call" | custom-call | tf_op jit(solution)/shard_map/pallas_call | solution.py:456
  10.8 5.6 %collective-permute-done.first_in = bf16[1088,128]{1,0:T(8,128)(2,1)S(1)} collective-permute-done((bf16[1088,128]{1,0:T(8,128)(2,1)S(1)}, bf16[1088,128]{1,0:T(8,128)(2,1)S(1)}, u32[]{:S(2)}, u32[]{:S(2)}) %collective-permute-start) | collective-permute-done | bytes 278560 | tf_op jit(solution)/shard_map/ppermute | solution.py:31
  16.5 1.5 %shard_map.102 = (bf16[4096,128]{1,0:T(8,128)(2,1)S(1)}, bf16[1088,128]{1,0:T(8,128)(2,1)S(1)}, bf16[1088,128]{1,0:T(8,128)(2,1)S(1)}) custom-call(s32[4,8]{1,0:T(4,128)S(1)} %pad_add_fusion.links, f32[4096,128]{1,0:T(8,128)S(1)} %shard_map.100.partial, bf16[1088,128]{1,0:T(8,128)(2,1)S(1)} %collective-permute-done.first_in, ...), custom_call_target="tpu_custom_call" | custom-call | tf_op jit(solution)/shard_map/pallas_call | solution.py:456
  17.9 1.3 %collective-permute-start.2 = (bf16[1088,128]{1,0:T(8,128)(2,1)S(1)}, bf16[1088,128]{1,0:T(8,128)(2,1)S(1)}, u32[]{:S(2)}, u32[]{:S(2)}) collective-permute-start(bf16[1088,128]{1,0:T(8,128)(2,1)S(1)} %get-tuple-element.30), channel_id=1, source_target_pairs={{0,1},{1,0},{2,3},{3,2},{4,5},{5,4},{6,7},{7,6},{8,9},{9,8},{10,11... | collective-permute-start | bytes 835592 | tf_op jit(solution)/shard_map/ppermute | solution.py:31
  19.2 2.1 %collective-permute-start.3 = (bf16[1088,128]{1,0:T(8,128)(2,1)S(1)}, bf16[1088,128]{1,0:T(8,128)(2,1)S(1)}, u32[]{:S(2)}, u32[]{:S(2)}) collective-permute-start(bf16[1088,128]{1,0:T(8,128)(2,1)S(1)} %get-tuple-element.31), channel_id=1, source_target_pairs={{1,2},{2,1},{3,4},{4,3},{5,6},{6,5},{7,8},{8,7},{9,10},{10,9},{11,... | collective-permute-start | bytes 835592 | tf_op jit(solution)/shard_map/ppermute | solution.py:32
  21.3 3.8 %shard_map.103.partial = f32[4096,128]{1,0:T(8,128)S(1)} custom-call(s32[4,8]{1,0:T(4,128)S(1)} %pad_add_fusion.links, bf16[4096,128]{1,0:T(8,128)(2,1)S(1)} %get-tuple-element.29.hidden, bf16[4096,128]{1,0:T(8,128)(2,1)S(1)} %bitcast.24, bf16[896,128]{1,0:T(8,128)(2,1)S(1)} %bitcast.29), custom_call_target="tpu_custom_call" | custom-call | tf_op jit(solution)/shard_map/pallas_call | solution.py:456
  25.1 4.5 %collective-permute-done.2.first_in = bf16[1088,128]{1,0:T(8,128)(2,1)S(1)} collective-permute-done((bf16[1088,128]{1,0:T(8,128)(2,1)S(1)}, bf16[1088,128]{1,0:T(8,128)(2,1)S(1)}, u32[]{:S(2)}, u32[]{:S(2)}) %collective-permute-start.2) | collective-permute-done | bytes 278560 | tf_op jit(solution)/shard_map/ppermute | solution.py:31
  29.7 3.4 %shard_map.104 = (bf16[264,128]{1,0:T(8,128)(2,1)S(1)}, bf16[264,128]{1,0:T(8,128)(2,1)S(1)}, bf16[264,128]{1,0:T(8,128)(2,1)S(1)}, bf16[264,128]{1,0:T(8,128)(2...) custom-call(s32[4,8]{1,0:T(4,128)S(1)} %pad_add_fusion.links, ...), custom_call_target="tpu_custom_call" | custom-call | tf_op jit(solution)/shard_map/pallas_call | solution.py:456
  33.0 2.3 %collective-permute-start.4 = (bf16[264,128]{1,0:T(8,128)(2,1)S(1)}, bf16[264,128]{1,0:T(8,128)(2,1)S(1)}, u32[]{:S(2)}, u32[]{:S(2)}) collective-permute-start(bf16[264,128]{1,0:T(8,128)(2,1)S(1)} %get-tuple-element.33), channel_id=1, source_target_pairs={{0,1},{1,0},{2,3},{3,2},{4,5},{5,4},{6,7},{7,6},{8,9},{9,8},{10,11... | collective-permute-start | bytes 202760 | tf_op jit(solution)/shard_map/ppermute | solution.py:533
  36.6 4.6 %collective-permute-start.7 = (bf16[264,128]{1,0:T(8,128)(2,1)S(1)}, bf16[264,128]{1,0:T(8,128)(2,1)S(1)}, u32[]{:S(2)}, u32[]{:S(2)}) collective-permute-start(bf16[264,128]{1,0:T(8,128)(2,1)S(1)} %get-tuple-element.36), channel_id=1, source_target_pairs={{0,4},{1,5},{2,6},{3,7},{4,0},{5,1},{6,2},{7,3},{8,12},{9,13},{10,... | collective-permute-start | bytes 202760 | tf_op jit(solution)/shard_map/ppermute | solution.py:533
  43.8 1.7 %collective-permute-done.7.refs_4_ = bf16[264,128]{1,0:T(8,128)(2,1)S(1)} collective-permute-done((bf16[264,128]{1,0:T(8,128)(2,1)S(1)}, bf16[264,128]{1,0:T(8,128)(2,1)S(1)}, u32[]{:S(2)}, u32[]{:S(2)}) %collective-permute-start.7) | collective-permute-done | bytes 67616 | tf_op jit(solution)/shard_map/ppermute | solution.py:533
  45.5 3.6 %collective-permute-done.8.refs_5_ = bf16[264,128]{1,0:T(8,128)(2,1)S(1)} collective-permute-done((bf16[264,128]{1,0:T(8,128)(2,1)S(1)}, bf16[264,128]{1,0:T(8,128)(2,1)S(1)}, u32[]{:S(2)}, u32[]{:S(2)}) %collective-permute-start.8) | collective-permute-done | bytes 67616 | tf_op jit(solution)/shard_map/ppermute | solution.py:533
  49.1 2.3 %collective-permute-done.9.refs_6_ = bf16[264,128]{1,0:T(8,128)(2,1)S(1)} collective-permute-done((bf16[264,128]{1,0:T(8,128)(2,1)S(1)}, bf16[264,128]{1,0:T(8,128)(2,1)S(1)}, u32[]{:S(2)}, u32[]{:S(2)}) %collective-permute-start.9) | collective-permute-done | bytes 67616 | tf_op jit(solution)/shard_map/ppermute | solution.py:533
  51.4 3.0 %collective-permute-done.10.refs_7_ = bf16[264,128]{1,0:T(8,128)(2,1)S(1)} collective-permute-done((bf16[264,128]{1,0:T(8,128)(2,1)S(1)}, bf16[264,128]{1,0:T(8,128)(2,1)S(1)}, u32[]{:S(2)}, u32[]{:S(2)}) %collective-permute-start.10) | collective-permute-done | bytes 67616 | tf_op jit(solution)/shard_map/ppermute | solution.py:533
  54.4 1.3 %shard_map.105 = (bf16[2048,256]{1,0:T(8,128)(2,1)S(1)}, bf16[64,256]{1,0:T(8,128)(2,1)S(1)}, bf16[64,256]{1,0:T(8,128)(2,1)S(1)}, bf16[4,64,256]{2,1,0:T(8,128)(2,1)S(1)}) custom-call(s32[4,8]{1,0:T(4,128)S(1)} %pad_add_fusion.links, bf16[264,128]{1,0:T(8,128)(2,1)S(1)} %get-tuple-element.32.refs_0_, bf16[264,128]{1,0:T(8,128)(2,1)S(1)} %collective-permute-done.4.refs_1_, ...), custom_call_target="tpu_custom_call" | custom-call | tf_op jit(solution)/shard_map/pallas_call | solution.py:456
  56.6 1.9 %collective-permute-start.12 = (bf16[64,256]{1,0:T(8,128)(2,1)S(1)}, bf16[64,256]{1,0:T(8,128)(2,1)S(1)}, u32[]{:S(2)}, u32[]{:S(2)}) collective-permute-start(bf16[64,256]{1,0:T(8,128)(2,1)S(1)} %get-tuple-element.41), channel_id=1, source_target_pairs={{8,16},{16,8},{9,17},{17,9},{10,18},{18,10},{11,19},{19,11},{12,20... | collective-permute-start | bytes 98312 | tf_op jit(solution)/shard_map/ppermute | solution.py:32
  58.5 2.7 %shard_map.106.inner = bf16[1984,256]{1,0:T(8,128)(2,1)S(1)} custom-call(bf16[2048,256]{1,0:T(8,128)(2,1)S(1)} %get-tuple-element.42.bev, bf16[9,256,256]{2,1,0:T(8,128)(2,1)S(1)} %bitcast.19), custom_call_target="tpu_custom_call" | custom-call | tf_op jit(solution)/shard_map/pallas_call | solution.py:456
  61.9 2.2 %collective-permute-start.14 = (bf16[2,68,256]{2,1,0:T(8,128)(2,1)S(1)}, bf16[2,68,256]{2,1,0:T(8,128)(2,1)S(1)}, u32[]{:S(2)}, u32[]{:S(2)}) collective-permute-start(bf16[2,68,256]{2,1,0:T(8,128)(2,1)S(1)} %get-tuple-element.49), channel_id=1, source_target_pairs={{1,2},{2,1},{3,4},{4,3},{5,6},{6,5},{9,10},{10,9},{11,12},{12,11},... | collective-permute-start | bytes 208904 | tf_op jit(solution)/shard_map/ppermute | solution.py:32
  64.1 2.5 %collective-permute-start.13 = (bf16[2,68,256]{2,1,0:T(8,128)(2,1)S(1)}, bf16[2,68,256]{2,1,0:T(8,128)(2,1)S(1)}, u32[]{:S(2)}, u32[]{:S(2)}) collective-permute-start(bf16[2,68,256]{2,1,0:T(8,128)(2,1)S(1)} %get-tuple-element.50), channel_id=1, source_target_pairs={{0,1},{1,0},{2,3},{3,2},{4,5},{5,4},{6,7},{7,6},{8,9},{9,8},{10,11... | collective-permute-start | bytes 208904 | tf_op jit(solution)/shard_map/ppermute | solution.py:31
  66.6 4.3 %shard_map.107 = (bf16[2048,256]{1,0:T(8,128)(2,1)S(1)}, f32[2,1024,128]{2,1,0:T(8,128)S(1)}) custom-call(s32[4,8]{1,0:T(4,128)S(1)} %pad_add_fusion.links, bf16[1984,256]{1,0:T(8,128)(2,1)S(1)} %shard_map.106.inner, bf16[2048,256]{1,0:T(8,128)(2,1)S(1)} %get-tuple-element.42.bev, bf16[64,256]{1,0:T(8,128)(2,1)S(1)} %collective-permute-done.11.first_row, ...), custom_call_target="tpu_custom_call" | custom-call | tf_op jit(solution)/shard_map/pallas_call | solution.py:456
  70.9 3.3 %shard_map.108 = bf16[2048,256]{1,0:T(8,128)(2,1)} custom-call(s32[4,8]{1,0:T(4,128)S(1)} %pad_add_fusion.links, bf16[2048,256]{1,0:T(8,128)(2,1)S(1)} %get-tuple-element.46.middle, f32[2,1024,128]{2,1,0:T(8,128)S(1)} %get-tuple-element.47.flanks, bf16[2,68,256]{2,1,0:T(8,128)(2,1)S(1)} %get-tuple-element.53.own_left, ...), custom_call_target="tpu_custom_call" | custom-call | tf_op jit(solution)/shard_map/pallas_call | solution.py:456
  (44 shorter events, 8.0 us)
Async XLA Ops:
  0.7 1.2 %copy-start.1 = (bf16[8,512,128]{2,1,0:T(8,128)(2,1)S(1)}, bf16[8,512,128]{2,1,0:T(8,128)(2,1)}, u32[]{:S(2)}) copy-start(bf16[8,512,128]{2,1,0:T(8,128)(2,1)} %param.10) | copy-start | bytes 3145732
  2.9 13.6 %collective-permute-start = (bf16[1088,128]{1,0:T(8,128)(2,1)S(1)}, bf16[1088,128]{1,0:T(8,128)(2,1)S(1)}, u32[]{:S(2)}, u32[]{:S(2)}) collective-permute-start(bf16[1088,128]{1,0:T(8,128)(2,1)S(1)} %get-tuple-element.27), channel_id=1, source_target_pairs={{0,1},{1,0},{2,3},{3,2},{4,5},{5,4},{6,7},{7,6},{8,9},{9,8},{10,11... | collective-permute-start | bytes 835592 | tf_op jit(solution)/shard_map/ppermute | solution.py:31
  4.2 12.3 %collective-permute-start.1 = (bf16[1088,128]{1,0:T(8,128)(2,1)S(1)}, bf16[1088,128]{1,0:T(8,128)(2,1)S(1)}, u32[]{:S(2)}, u32[]{:S(2)}) collective-permute-start(bf16[1088,128]{1,0:T(8,128)(2,1)S(1)} %get-tuple-element.28), channel_id=1, source_target_pairs={{1,2},{2,1},{3,4},{4,3},{5,6},{6,5},{7,8},{8,7},{9,10},{10,9},{11,... | collective-permute-start | bytes 835592 | tf_op jit(solution)/shard_map/ppermute | solution.py:32
  10.8 10.4 %copy-start.2 = (bf16[8,512,128]{2,1,0:T(8,128)(2,1)S(1)}, bf16[8,512,128]{2,1,0:T(8,128)(2,1)}, u32[]{:S(2)}) copy-start(bf16[8,512,128]{2,1,0:T(8,128)(2,1)} %param.10) | copy-start | bytes 3145732
  10.8 10.4 %copy-start.6 = (bf16[7,128,128]{2,1,0:T(8,128)(2,1)S(1)}, bf16[7,128,128]{2,1,0:T(8,128)(2,1)}, u32[]{:S(2)}) copy-start(bf16[7,128,128]{2,1,0:T(8,128)(2,1)} %param.16) | copy-start | bytes 688132
  17.9 11.7 %collective-permute-start.2 = (bf16[1088,128]{1,0:T(8,128)(2,1)S(1)}, bf16[1088,128]{1,0:T(8,128)(2,1)S(1)}, u32[]{:S(2)}, u32[]{:S(2)}) collective-permute-start(bf16[1088,128]{1,0:T(8,128)(2,1)S(1)} %get-tuple-element.30), channel_id=1, source_target_pairs={{0,1},{1,0},{2,3},{3,2},{4,5},{5,4},{6,7},{7,6},{8,9},{9,8},{10,11... | collective-permute-start | bytes 835592 | tf_op jit(solution)/shard_map/ppermute | solution.py:31
  19.2 10.5 %collective-permute-start.3 = (bf16[1088,128]{1,0:T(8,128)(2,1)S(1)}, bf16[1088,128]{1,0:T(8,128)(2,1)S(1)}, u32[]{:S(2)}, u32[]{:S(2)}) collective-permute-start(bf16[1088,128]{1,0:T(8,128)(2,1)S(1)} %get-tuple-element.31), channel_id=1, source_target_pairs={{1,2},{2,1},{3,4},{4,3},{5,6},{6,5},{7,8},{8,7},{9,10},{10,9},{11,... | collective-permute-start | bytes 835592 | tf_op jit(solution)/shard_map/ppermute | solution.py:32
  21.3 8.4 %copy-start.4 = (bf16[4,1024,256]{2,1,0:T(8,128)(2,1)S(1)}, bf16[4,1024,256]{2,1,0:T(8,128)(2,1)}, u32[]{:S(2)}) copy-start(bf16[4,1024,256]{2,1,0:T(8,128)(2,1)} %height.1) | copy-start | bytes 6291460
  21.3 8.4 %copy-start.7 = (s32[8]{0:T(128)S(1)}, s32[8]{0:T(128)}, u32[]{:S(2)}) copy-start(s32[8]{0:T(128)} %param.12) | copy-start | bytes 100
  21.3 8.4 %copy-start.8 = (s32[8]{0:T(128)S(1)}, s32[8]{0:T(128)}, u32[]{:S(2)}) copy-start(s32[8]{0:T(128)} %param.13) | copy-start | bytes 100
  21.3 8.3 %copy-start.9 = (s32[1,16]{1,0:T(1,128)S(1)}, s32[1,16]{1,0:T(1,128)}, u32[]{:S(2)}) copy-start(s32[1,16]{1,0:T(1,128)} %columns.1) | copy-start | bytes 196
  29.7 28.9 %copy-start = (bf16[3,3,256,256]{3,2,1,0:T(8,128)(2,1)S(1)}, bf16[3,3,256,256]{3,2,1,0:T(8,128)(2,1)}, u32[]{:S(2)}) copy-start(bf16[3,3,256,256]{3,2,1,0:T(8,128)(2,1)} %param.18) | copy-start | bytes 3538948
  33.0 9.2 %collective-permute-start.4 = (bf16[264,128]{1,0:T(8,128)(2,1)S(1)}, bf16[264,128]{1,0:T(8,128)(2,1)S(1)}, u32[]{:S(2)}, u32[]{:S(2)}) collective-permute-start(bf16[264,128]{1,0:T(8,128)(2,1)S(1)} %get-tuple-element.33), channel_id=1, source_target_pairs={{0,1},{1,0},{2,3},{3,2},{4,5},{5,4},{6,7},{7,6},{8,9},{9,8},{10,11... | collective-permute-start | bytes 202760 | tf_op jit(solution)/shard_map/ppermute | solution.py:533
  35.3 8.2 %collective-permute-start.5 = (bf16[264,128]{1,0:T(8,128)(2,1)S(1)}, bf16[264,128]{1,0:T(8,128)(2,1)S(1)}, u32[]{:S(2)}, u32[]{:S(2)}) collective-permute-start(bf16[264,128]{1,0:T(8,128)(2,1)S(1)} %get-tuple-element.34), channel_id=1, source_target_pairs={{0,2},{1,3},{2,0},{3,1},{4,6},{5,7},{6,4},{7,5},{8,10},{9,11},{10,... | collective-permute-start | bytes 202760 | tf_op jit(solution)/shard_map/ppermute | solution.py:533
  35.5 8.3 %collective-permute-start.6 = (bf16[264,128]{1,0:T(8,128)(2,1)S(1)}, bf16[264,128]{1,0:T(8,128)(2,1)S(1)}, u32[]{:S(2)}, u32[]{:S(2)}) collective-permute-start(bf16[264,128]{1,0:T(8,128)(2,1)S(1)} %get-tuple-element.35), channel_id=1, source_target_pairs={{0,3},{1,2},{2,1},{3,0},{4,7},{5,6},{6,5},{7,4},{8,11},{9,10},{10,... | collective-permute-start | bytes 202760 | tf_op jit(solution)/shard_map/ppermute | solution.py:533
  36.6 8.8 %collective-permute-start.7 = (bf16[264,128]{1,0:T(8,128)(2,1)S(1)}, bf16[264,128]{1,0:T(8,128)(2,1)S(1)}, u32[]{:S(2)}, u32[]{:S(2)}) collective-permute-start(bf16[264,128]{1,0:T(8,128)(2,1)S(1)} %get-tuple-element.36), channel_id=1, source_target_pairs={{0,4},{1,5},{2,6},{3,7},{4,0},{5,1},{6,2},{7,3},{8,12},{9,13},{10,... | collective-permute-start | bytes 202760 | tf_op jit(solution)/shard_map/ppermute | solution.py:533
  41.2 7.9 %collective-permute-start.8 = (bf16[264,128]{1,0:T(8,128)(2,1)S(1)}, bf16[264,128]{1,0:T(8,128)(2,1)S(1)}, u32[]{:S(2)}, u32[]{:S(2)}) collective-permute-start(bf16[264,128]{1,0:T(8,128)(2,1)S(1)} %get-tuple-element.37), channel_id=1, source_target_pairs={{0,5},{1,4},{2,7},{3,6},{4,1},{5,0},{6,3},{7,2},{8,13},{9,12},{10,... | collective-permute-start | bytes 202760 | tf_op jit(solution)/shard_map/ppermute | solution.py:533
  42.3 9.1 %collective-permute-start.9 = (bf16[264,128]{1,0:T(8,128)(2,1)S(1)}, bf16[264,128]{1,0:T(8,128)(2,1)S(1)}, u32[]{:S(2)}, u32[]{:S(2)}) collective-permute-start(bf16[264,128]{1,0:T(8,128)(2,1)S(1)} %get-tuple-element.38), channel_id=1, source_target_pairs={{0,6},{1,7},{2,4},{3,5},{4,2},{5,3},{6,0},{7,1},{8,14},{9,15},{10,... | collective-permute-start | bytes 202760 | tf_op jit(solution)/shard_map/ppermute | solution.py:533
  43.5 11.0 %collective-permute-start.10 = (bf16[264,128]{1,0:T(8,128)(2,1)S(1)}, bf16[264,128]{1,0:T(8,128)(2,1)S(1)}, u32[]{:S(2)}, u32[]{:S(2)}) collective-permute-start(bf16[264,128]{1,0:T(8,128)(2,1)S(1)} %get-tuple-element.39), channel_id=1, source_target_pairs={{0,7},{1,6},{2,5},{3,4},{4,3},{5,2},{6,1},{7,0},{8,15},{9,14},{10,... | collective-permute-start | bytes 202760 | tf_op jit(solution)/shard_map/ppermute | solution.py:533
  55.7 10.9 %copy-start.3 = (bf16[3,3,256,256]{3,2,1,0:T(8,128)(2,1)S(1)}, bf16[3,3,256,256]{3,2,1,0:T(8,128)(2,1)}, u32[]{:S(2)}) copy-start(bf16[3,3,256,256]{3,2,1,0:T(8,128)(2,1)} %param.19) | copy-start | bytes 3538948
  55.7 5.6 %collective-permute-start.11 = (bf16[64,256]{1,0:T(8,128)(2,1)S(1)}, bf16[64,256]{1,0:T(8,128)(2,1)S(1)}, u32[]{:S(2)}, u32[]{:S(2)}) collective-permute-start(bf16[64,256]{1,0:T(8,128)(2,1)S(1)} %get-tuple-element.40), channel_id=1, source_target_pairs={{0,8},{8,0},{16,24},{24,16},{1,9},{9,1},{17,25},{25,17},{2,10},{10... | collective-permute-start | bytes 98312 | tf_op jit(solution)/shard_map/ppermute | solution.py:31
  56.6 5.2 %collective-permute-start.12 = (bf16[64,256]{1,0:T(8,128)(2,1)S(1)}, bf16[64,256]{1,0:T(8,128)(2,1)S(1)}, u32[]{:S(2)}, u32[]{:S(2)}) collective-permute-start(bf16[64,256]{1,0:T(8,128)(2,1)S(1)} %get-tuple-element.41), channel_id=1, source_target_pairs={{8,16},{16,8},{9,17},{17,9},{10,18},{18,10},{11,19},{19,11},{12,20... | collective-permute-start | bytes 98312 | tf_op jit(solution)/shard_map/ppermute | solution.py:32
  61.9 8.9 %collective-permute-start.14 = (bf16[2,68,256]{2,1,0:T(8,128)(2,1)S(1)}, bf16[2,68,256]{2,1,0:T(8,128)(2,1)S(1)}, u32[]{:S(2)}, u32[]{:S(2)}) collective-permute-start(bf16[2,68,256]{2,1,0:T(8,128)(2,1)S(1)} %get-tuple-element.49), channel_id=1, source_target_pairs={{1,2},{2,1},{3,4},{4,3},{5,6},{6,5},{9,10},{10,9},{11,12},{12,11},... | collective-permute-start | bytes 208904 | tf_op jit(solution)/shard_map/ppermute | solution.py:32
  64.1 6.8 %collective-permute-start.13 = (bf16[2,68,256]{2,1,0:T(8,128)(2,1)S(1)}, bf16[2,68,256]{2,1,0:T(8,128)(2,1)S(1)}, u32[]{:S(2)}, u32[]{:S(2)}) collective-permute-start(bf16[2,68,256]{2,1,0:T(8,128)(2,1)S(1)} %get-tuple-element.50), channel_id=1, source_target_pairs={{0,1},{1,0},{2,3},{3,2},{4,5},{5,4},{6,7},{7,6},{8,9},{9,8},{10,11... | collective-permute-start | bytes 208904 | tf_op jit(solution)/shard_map/ppermute | solution.py:31
  (1 other events, 0.9 us)

commit v7 on v6

--- a/solution.py
+++ b/solution.py
@@ -21,6 +21,7 @@
 
 VMEM = pl.BlockSpec(memory_space=pltpu.VMEM)
 SMEM = pl.BlockSpec(memory_space=pltpu.SMEM)
+ANY = pl.BlockSpec(memory_space=pl.ANY)
 
 
 def swap(first, second, axis):
@@ -330,20 +331,26 @@
     second_row,
     weights_first,
     weights_second,
+    out,
+    flanks,
     middle,
-    flanks,
     above,
     below,
+    sems,
 ):
     ch = bev.shape[1]
     two = HALO * COLS
-    step = CORE_ROWS // 4
+    steps = 4
+    step = CORE_ROWS // steps
+
+    def send(row, count, k):
+        rows = pl.ds(row, count)
+        return pltpu.make_async_copy(middle.at[rows], out.at[rows], sems.at[k])
 
     def store(block, row):
         count = block.shape[0] // COLS
-        at = row * COLS if isinstance(row, int) else pl.multiple_of(row * COLS, COLS)
-        middle[pl.ds(at, count * COLS), :] = block.astype(BF16)
         lines = block.reshape(count, COLS, ch)
+        middle[pl.ds(row, count), :, :] = lines.astype(BF16)
         for side, x in enumerate((0, COLS - EDGE)):
             flank = lines[:, x : x + EDGE, :].reshape(count * EDGE, ch)
             to = side * ROWS * EDGE + row * EDGE
@@ -355,9 +362,10 @@
         block = rows_conv(three_rows(inner, i * step, step), weights_second)
         at = pl.multiple_of((i * step + 2) * COLS, COLS)
         store(block + bev[pl.ds(at, step * COLS), :].astype(F32), i * step + 2)
+        send(i * step + 2, step, i).start()
         return carry
 
-    lax.fori_loop(0, CORE_ROWS // step, one, 0)
+    lax.fori_loop(0, steps, one, 0)
 
     route(links[3, 6], first_row, second_row, below, above)
     top, bottom = bev[0:two, :], bev[ROWS * COLS - two :, :]
@@ -373,11 +381,17 @@
     strip = rows_conv(strips(high, low), weights_second)
     store(strip[0:two] + top.astype(F32), 0)
     store(strip[two:] + bottom.astype(F32), ROWS - HALO)
+    send(0, HALO, steps).start()
+    send(ROWS - HALO, HALO, steps + 1).start()
+    for k in range(steps):
+        send(k * step + 2, step, k).wait()
+    send(0, HALO, steps).wait()
+    send(ROWS - HALO, HALO, steps + 1).wait()
 
 
 def edges_kernel(
     links,
-    middle,
+    unused,
     flanks,
     own_left,
     own_right,
@@ -388,9 +402,11 @@
     out,
     sides,
     total,
+    edge,
+    sems,
 ):
-    ch = middle.shape[1]
-    sides[...] = jnp.zeros_like(sides)
+    ch = out.shape[2]
+    sides[:, WIDE_ROWS:, :] = jnp.zeros_like(sides[:, WIDE_ROWS:, :])
 
     def place(base, source):
         for x in range(HALO):
@@ -409,46 +425,54 @@
         place(0, first_in)
         place(6, second_in)
 
-    lhs = []
-    for start in (0, 1, 4, 5):
-        parts = []
-        for dy in range(3):
-            for dx in range(3):
-                parts.append(sides[start + dx, dy : dy + RIM_ROWS, :].astype(BF16))
-        lhs.append(jnp.concatenate(parts, 1))
-    taps = jnp.concatenate([weights_first[t] for t in range(9)], 0)
-    columns = jnp.maximum(mm(jnp.concatenate(lhs, 0), taps), 0.0)
+    tall = sides.shape[1]
+    total[...] = flanks[...]
+    narrow = [sides[k, :, :].astype(BF16) for k in range(8)]
+    lhs = [jnp.concatenate(narrow[start : start + 3], 1) for start in (0, 1, 4, 5)]
+    lhs = jnp.concatenate(lhs, 0)
+    taps = []
+    for dy in range(3):
+        rows = [weights_first[dy * 3 + dx] for dx in range(3)]
+        taps.append(mm(lhs, jnp.concatenate(rows, 0)))
     row_at = lax.broadcasted_iota(jnp.int32, (RIM_ROWS, ch), 0)
     keep = jnp.where(row_at == MID_ROWS - 1, links[3, 1], 1)
     keep = jnp.where(row_at == 0, links[3, 0], keep).astype(F32)
+    column = []
     for k, side_keep in enumerate((links[3, 2], None, None, links[3, 3])):
-        block = columns[k * RIM_ROWS : (k + 1) * RIM_ROWS, :] * keep
+        at = k * tall
+        block = sum(taps[dy][at + dy : at + dy + RIM_ROWS, :] for dy in range(3))
+        block = jnp.maximum(block, 0.0) * keep
         if side_keep is not None:
             block = block * side_keep.astype(F32)
-        sides[k, 0:RIM_ROWS, :] = block
-
-    column = []
-    for k in range(4):
-        rows = [sides[k, dy : dy + ROWS, :].astype(BF16) for dy in range(3)]
-        column.append(jnp.concatenate(rows, 1))
-    w0, w1, w2 = [tap_columns(weights_second, dx) for dx in range(3)]
+        zeros = jnp.zeros((tall - RIM_ROWS, ch), F32)
+        column.append(jnp.concatenate([block, zeros], 0).astype(BF16))
+
+    parts = []
+    for dx, pair in enumerate(((0, 1), (1, 2), (2, 3))):
+        lhs = jnp.concatenate([column[k] for k in pair], 0)
+        taps = [mm(lhs, weights_second[dy * 3 + dx]) for dy in range(3)]
+        for at in (0, tall):
+            parts.append(sum(taps[dy][at + dy : at + dy + ROWS, :] for dy in range(3)))
     added = (
-        (0, mm(column[0], w0) + mm(column[1], w1)),
-        (1, mm(column[1], w0)),
-        (ROWS * EDGE + EDGE - 2, mm(column[2], w2)),
-        (ROWS * EDGE + EDGE - 1, mm(column[2], w1) + mm(column[3], w2)),
-    )
-    total[...] = flanks[...]
+        (0, parts[0] + parts[2]),
+        (1, parts[1]),
+        (ROWS * EDGE + EDGE - 2, parts[4]),
+        (ROWS * EDGE + EDGE - 1, parts[3] + parts[5]),
+    )
     for at, block in added:
         for h, lanes in halves(ch):
             total[h, pl.ds(at, ROWS, stride=EDGE), :] += block[:, lanes]
-    for y in range(ROWS):
-        at = y * COLS
-        out[at + EDGE : at + COLS - EDGE, :] = middle[at + EDGE : at + COLS - EDGE, :]
-        for side, x in enumerate((0, COLS - EDGE)):
-            group = side * ROWS * EDGE + y * EDGE
-            for h, lanes in halves(ch):
-                out[at + x : at + x + EDGE, lanes] = total[h, group : group + EDGE, :].astype(BF16)
+    copies = []
+    for side, x in enumerate((0, COLS - EDGE)):
+        group = slice(side * ROWS * EDGE, (side + 1) * ROWS * EDGE)
+        for h, lanes in halves(ch):
+            edge[side, :, :, lanes] = total[h, group, :].reshape(ROWS, EDGE, LANES).astype(BF16)
+        copies.append(
+            pltpu.make_async_copy(edge.at[side], out.at[:, x : x + EDGE, :], sems.at[side])
+        )
+        copies[-1].start()
+    for copy in copies:
+        copy.wait()
 
 
 def call(kernel, out_shape, scalars, arrays, scratch=(), mib=12):
@@ -572,27 +596,38 @@
     first, second = swap(
         jnp.where(odd_x, own_left, own_right), jnp.where(odd_x, own_right, own_left), "gx"
     )
-    middle, flanks = call(
+    flank = (mapped // LANES, 2 * ROWS * EDGE, LANES)
+    out_shape = jax.ShapeDtypeStruct((ROWS, COLS, mapped), BF16)
+    limit = pltpu.CompilerParams(vmem_limit_bytes=12 << 20)
+    out, flanks = pl.pallas_call(
         second_core_kernel,
-        (
-            jax.ShapeDtypeStruct((ROWS * COLS, mapped), BF16),
-            jax.ShapeDtypeStruct((mapped // LANES, 2 * ROWS * EDGE, LANES), F32),
-        ),
-        (links,),
-        (inner, bev, first_row, second_row, k_first, k_second),
-        (row, row),
-    )
-    out = call(
+        name="second_core",
+        out_shape=(out_shape, jax.ShapeDtypeStruct(flank, F32)),
+        in_specs=[SMEM] + [VMEM] * 6,
+        out_specs=[ANY, VMEM],
+        scratch_shapes=[
+            pltpu.VMEM((ROWS, COLS, mapped), BF16),
+            row,
+            row,
+            pltpu.SemaphoreType.DMA((6,)),
+        ],
+        compiler_params=limit,
+    )(links, inner, bev, first_row, second_row, k_first, k_second)
+    return pl.pallas_call(
         edges_kernel,
-        jax.ShapeDtypeStruct((ROWS * COLS, mapped), BF16),
-        (links,),
-        (middle, flanks, own_left, own_right, first, second, k_first, k_second),
-        (
+        name="edges",
+        out_shape=out_shape,
+        in_specs=[SMEM, ANY] + [VMEM] * 7,
+        out_specs=ANY,
+        scratch_shapes=[
             pltpu.VMEM((8, RIM_ROWS + EDGE, mapped), F32),
-            pltpu.VMEM((mapped // LANES, 2 * ROWS * EDGE, LANES), F32),
-        ),
-    )
-    return out.reshape(ROWS, COLS, mapped)
+            pltpu.VMEM(flank, F32),
+            pltpu.VMEM((2, ROWS, EDGE, mapped), BF16),
+            pltpu.SemaphoreType.DMA((2,)),
+        ],
+        input_output_aliases={1: 0},
+        compiler_params=limit,
+    )(links, out, flanks, own_left, own_right, first, second, k_first, k_second)
 
 
 def solution(mesh):

time: 75 us -> 74.9 us (level)
    pallas_call x9 -> x7, Pallas kernels: 24.9 us -> 17.4 us  [call(): pl.pallas_call(kernel, out_shape=out_shape, in_specs=[SMEM] * len(scalars...]
    pallas_call x0 -> x2, Pallas kernels: none -> 7.39 us  [the longest x1 4.95 us: local(): pl.pallas_call(second_core_kernel, name='second_core', out_shape=(out_sha...]
  transfers between devices with their start and end apart: 15 -> 15, of which waited for: 7 -> 7; matrix products, arithmetic and copies ran while one was open for 0% -> 0% of each run, Pallas kernels for 20% -> 21%
where the time goes in v7:
time: 74.9 us; the launch traced here: 74 us
  Pallas kernels  24.8 us (33%)
  starting transfers between devices  24.6 us (33%)
  waiting for transfers between devices  21.3 us (28%)
  local copies, waits for them, and re-layouts  2.25 us (3%)
  other arithmetic  0.78 us (1%)
    pallas_call x7, Pallas kernels, call(): pl.pallas_call(kernel, out_shape=out_shape, in_specs=[SMEM] * len(scalars...  17.4 us
    ppermute x7, starting transfers between devices, local(): lax.ppermute(outgoing[k], 'gx', [(i, i ^ k) for i in range(peers)])  10.7 us
    ppermute x7, waiting for transfers between devices, local(): lax.ppermute(outgoing[k], 'gx', [(i, i ^ k) for i in range(peers)])  10.7 us
    ppermute x4, waiting for transfers between devices, swap(): first = lax.ppermute(first, axis, near)  10.1 us
    ppermute x4, starting transfers between devices, swap(): second = lax.ppermute(second, axis, far)  8.03 us
    ppermute x4, starting transfers between devices, swap(): first = lax.ppermute(first, axis, near)  5.86 us
    pallas_call x1, Pallas kernels, local(): pl.pallas_call(second_core_kernel, name='second_core', out_shape=(out_sha...  4.95 us
    pallas_call x1, Pallas kernels, local(): pl.pallas_call(edges_kernel, name='edges', out_shape=out_shape, in_specs=...  2.44 us
  transfers between devices with their start and end apart: 15, of which 7 were waited for; matrix products, arithmetic and copies ran while one was open for 0% of the time, Pallas kernels for 21%

profile of v7, /device:TPU:9, one launch (start us, length us, event | category | flops | bytes accessed | tf_op | source)
XLA Modules:
  0.0 74.0 jit_solution(263455824838875792)
XLA Ops:
  0.7 1.2 %copy-done.1 = bf16[8,512,128]{2,1,0:T(8,128)(2,1)S(1)} copy-done((bf16[8,512,128]{2,1,0:T(8,128)(2,1)S(1)}, bf16[8,512,128]{2,1,0:T(8,128)(2,1)}, u32[]{:S(2)}) %copy-start.1) | copy-done | bytes 1048600
  2.9 1.3 %collective-permute-start = (bf16[1088,128]{1,0:T(8,128)(2,1)S(1)}, bf16[1088,128]{1,0:T(8,128)(2,1)S(1)}, u32[]{:S(2)}, u32[]{:S(2)}) collective-permute-start(bf16[1088,128]{1,0:T(8,128)(2,1)S(1)} %get-tuple-element.27), channel_id=1, source_target_pairs={{0,1},{1,0},{2,3},{3,2},{4,5},{5,4},{6,7},{7,6},{8,9},{9,8},{10,11... | collective-permute-start | bytes 835592 | tf_op jit(solution)/shard_map/ppermute | solution.py:32
  4.2 1.9 %collective-permute-start.1 = (bf16[1088,128]{1,0:T(8,128)(2,1)S(1)}, bf16[1088,128]{1,0:T(8,128)(2,1)S(1)}, u32[]{:S(2)}, u32[]{:S(2)}) collective-permute-start(bf16[1088,128]{1,0:T(8,128)(2,1)S(1)} %get-tuple-element.28), channel_id=1, source_target_pairs={{1,2},{2,1},{3,4},{4,3},{5,6},{6,5},{7,8},{8,7},{9,10},{10,9},{11,... | collective-permute-start | bytes 835592 | tf_op jit(solution)/shard_map/ppermute | solution.py:33
  7.0 3.8 %shard_map.100.partial = f32[4096,128]{1,0:T(8,128)S(1)} custom-call(s32[4,8]{1,0:T(4,128)S(1)} %pad_add_fusion.links, bf16[4096,128]{1,0:T(8,128)(2,1)S(1)} %bitcast.22, bf16[896,128]{1,0:T(8,128)(2,1)S(1)} %bitcast.26), custom_call_target="tpu_custom_call" | custom-call | tf_op jit(solution)/shard_map/pallas_call | solution.py:480
  10.8 5.6 %collective-permute-done.first_in = bf16[1088,128]{1,0:T(8,128)(2,1)S(1)} collective-permute-done((bf16[1088,128]{1,0:T(8,128)(2,1)S(1)}, bf16[1088,128]{1,0:T(8,128)(2,1)S(1)}, u32[]{:S(2)}, u32[]{:S(2)}) %collective-permute-start) | collective-permute-done | bytes 278560 | tf_op jit(solution)/shard_map/ppermute | solution.py:32
  16.5 1.5 %shard_map.102 = (bf16[4096,128]{1,0:T(8,128)(2,1)S(1)}, bf16[1088,128]{1,0:T(8,128)(2,1)S(1)}, bf16[1088,128]{1,0:T(8,128)(2,1)S(1)}) custom-call(s32[4,8]{1,0:T(4,128)S(1)} %pad_add_fusion.links, f32[4096,128]{1,0:T(8,128)S(1)} %shard_map.100.partial, bf16[1088,128]{1,0:T(8,128)(2,1)S(1)} %collective-permute-done.first_in, ...), custom_call_target="tpu_custom_call" | custom-call | tf_op jit(solution)/shard_map/pallas_call | solution.py:480
  17.9 1.3 %collective-permute-start.2 = (bf16[1088,128]{1,0:T(8,128)(2,1)S(1)}, bf16[1088,128]{1,0:T(8,128)(2,1)S(1)}, u32[]{:S(2)}, u32[]{:S(2)}) collective-permute-start(bf16[1088,128]{1,0:T(8,128)(2,1)S(1)} %get-tuple-element.30), channel_id=1, source_target_pairs={{0,1},{1,0},{2,3},{3,2},{4,5},{5,4},{6,7},{7,6},{8,9},{9,8},{10,11... | collective-permute-start | bytes 835592 | tf_op jit(solution)/shard_map/ppermute | solution.py:32
  19.2 2.1 %collective-permute-start.3 = (bf16[1088,128]{1,0:T(8,128)(2,1)S(1)}, bf16[1088,128]{1,0:T(8,128)(2,1)S(1)}, u32[]{:S(2)}, u32[]{:S(2)}) collective-permute-start(bf16[1088,128]{1,0:T(8,128)(2,1)S(1)} %get-tuple-element.31), channel_id=1, source_target_pairs={{1,2},{2,1},{3,4},{4,3},{5,6},{6,5},{7,8},{8,7},{9,10},{10,9},{11,... | collective-permute-start | bytes 835592 | tf_op jit(solution)/shard_map/ppermute | solution.py:33
  21.3 3.8 %shard_map.103.partial = f32[4096,128]{1,0:T(8,128)S(1)} custom-call(s32[4,8]{1,0:T(4,128)S(1)} %pad_add_fusion.links, bf16[4096,128]{1,0:T(8,128)(2,1)S(1)} %get-tuple-element.29.hidden, bf16[4096,128]{1,0:T(8,128)(2,1)S(1)} %bitcast.23, bf16[896,128]{1,0:T(8,128)(2,1)S(1)} %bitcast.28), custom_call_target="tpu_custom_call" | custom-call | tf_op jit(solution)/shard_map/pallas_call | solution.py:480
  25.1 4.5 %collective-permute-done.2.first_in = bf16[1088,128]{1,0:T(8,128)(2,1)S(1)} collective-permute-done((bf16[1088,128]{1,0:T(8,128)(2,1)S(1)}, bf16[1088,128]{1,0:T(8,128)(2,1)S(1)}, u32[]{:S(2)}, u32[]{:S(2)}) %collective-permute-start.2) | collective-permute-done | bytes 278560 | tf_op jit(solution)/shard_map/ppermute | solution.py:32
  29.7 3.4 %shard_map.104 = (bf16[264,128]{1,0:T(8,128)(2,1)S(1)}, bf16[264,128]{1,0:T(8,128)(2,1)S(1)}, bf16[264,128]{1,0:T(8,128)(2,1)S(1)}, bf16[264,128]{1,0:T(8,128)(2...) custom-call(s32[4,8]{1,0:T(4,128)S(1)} %pad_add_fusion.links, ...), custom_call_target="tpu_custom_call" | custom-call | tf_op jit(solution)/shard_map/pallas_call | solution.py:480
  33.0 2.3 %collective-permute-start.4 = (bf16[264,128]{1,0:T(8,128)(2,1)S(1)}, bf16[264,128]{1,0:T(8,128)(2,1)S(1)}, u32[]{:S(2)}, u32[]{:S(2)}) collective-permute-start(bf16[264,128]{1,0:T(8,128)(2,1)S(1)} %get-tuple-element.33), channel_id=1, source_target_pairs={{0,1},{1,0},{2,3},{3,2},{4,5},{5,4},{6,7},{7,6},{8,9},{9,8},{10,11... | collective-permute-start | bytes 202760 | tf_op jit(solution)/shard_map/ppermute | solution.py:557
  36.6 4.6 %collective-permute-start.7 = (bf16[264,128]{1,0:T(8,128)(2,1)S(1)}, bf16[264,128]{1,0:T(8,128)(2,1)S(1)}, u32[]{:S(2)}, u32[]{:S(2)}) collective-permute-start(bf16[264,128]{1,0:T(8,128)(2,1)S(1)} %get-tuple-element.36), channel_id=1, source_target_pairs={{0,4},{1,5},{2,6},{3,7},{4,0},{5,1},{6,2},{7,3},{8,12},{9,13},{10,... | collective-permute-start | bytes 202760 | tf_op jit(solution)/shard_map/ppermute | solution.py:557
  43.8 1.7 %collective-permute-done.7.refs_4_ = bf16[264,128]{1,0:T(8,128)(2,1)S(1)} collective-permute-done((bf16[264,128]{1,0:T(8,128)(2,1)S(1)}, bf16[264,128]{1,0:T(8,128)(2,1)S(1)}, u32[]{:S(2)}, u32[]{:S(2)}) %collective-permute-start.7) | collective-permute-done | bytes 67616 | tf_op jit(solution)/shard_map/ppermute | solution.py:557
  45.5 3.6 %collective-permute-done.8.refs_5_ = bf16[264,128]{1,0:T(8,128)(2,1)S(1)} collective-permute-done((bf16[264,128]{1,0:T(8,128)(2,1)S(1)}, bf16[264,128]{1,0:T(8,128)(2,1)S(1)}, u32[]{:S(2)}, u32[]{:S(2)}) %collective-permute-start.8) | collective-permute-done | bytes 67616 | tf_op jit(solution)/shard_map/ppermute | solution.py:557
  49.1 2.3 %collective-permute-done.9.refs_6_ = bf16[264,128]{1,0:T(8,128)(2,1)S(1)} collective-permute-done((bf16[264,128]{1,0:T(8,128)(2,1)S(1)}, bf16[264,128]{1,0:T(8,128)(2,1)S(1)}, u32[]{:S(2)}, u32[]{:S(2)}) %collective-permute-start.9) | collective-permute-done | bytes 67616 | tf_op jit(solution)/shard_map/ppermute | solution.py:557
  51.4 3.0 %collective-permute-done.10.refs_7_ = bf16[264,128]{1,0:T(8,128)(2,1)S(1)} collective-permute-done((bf16[264,128]{1,0:T(8,128)(2,1)S(1)}, bf16[264,128]{1,0:T(8,128)(2,1)S(1)}, u32[]{:S(2)}, u32[]{:S(2)}) %collective-permute-start.10) | collective-permute-done | bytes 67616 | tf_op jit(solution)/shard_map/ppermute | solution.py:557
  54.4 1.3 %shard_map.105 = (bf16[2048,256]{1,0:T(8,128)(2,1)S(1)}, bf16[64,256]{1,0:T(8,128)(2,1)S(1)}, bf16[64,256]{1,0:T(8,128)(2,1)S(1)}, bf16[4,64,256]{2,1,0:T(8,128)(2,1)S(1)}) custom-call(s32[4,8]{1,0:T(4,128)S(1)} %pad_add_fusion.links, bf16[264,128]{1,0:T(8,128)(2,1)S(1)} %get-tuple-element.32.refs_0_, bf16[264,128]{1,0:T(8,128)(2,1)S(1)} %collective-permute-done.4.refs_1_, ...), custom_call_target="tpu_custom_call" | custom-call | tf_op jit(solution)/shard_map/pallas_call | solution.py:480
  56.6 1.9 %collective-permute-start.12 = (bf16[64,256]{1,0:T(8,128)(2,1)S(1)}, bf16[64,256]{1,0:T(8,128)(2,1)S(1)}, u32[]{:S(2)}, u32[]{:S(2)}) collective-permute-start(bf16[64,256]{1,0:T(8,128)(2,1)S(1)} %get-tuple-element.41), channel_id=1, source_target_pairs={{8,16},{16,8},{9,17},{17,9},{10,18},{18,10},{11,19},{19,11},{12,20... | collective-permute-start | bytes 98312 | tf_op jit(solution)/shard_map/ppermute | solution.py:33
  58.5 2.7 %shard_map.106.inner = bf16[1984,256]{1,0:T(8,128)(2,1)S(1)} custom-call(bf16[2048,256]{1,0:T(8,128)(2,1)S(1)} %get-tuple-element.42.bev, bf16[9,256,256]{2,1,0:T(8,128)(2,1)S(1)} %bitcast.18), custom_call_target="tpu_custom_call" | custom-call | tf_op jit(solution)/shard_map/pallas_call | solution.py:480
  61.9 2.2 %collective-permute-start.14 = (bf16[2,68,256]{2,1,0:T(8,128)(2,1)S(1)}, bf16[2,68,256]{2,1,0:T(8,128)(2,1)S(1)}, u32[]{:S(2)}, u32[]{:S(2)}) collective-permute-start(bf16[2,68,256]{2,1,0:T(8,128)(2,1)S(1)} %get-tuple-element.49), channel_id=1, source_target_pairs={{1,2},{2,1},{3,4},{4,3},{5,6},{6,5},{9,10},{10,9},{11,12},{12,11},... | collective-permute-start | bytes 208904 | tf_op jit(solution)/shard_map/ppermute | solution.py:33
  64.1 2.5 %collective-permute-start.13 = (bf16[2,68,256]{2,1,0:T(8,128)(2,1)S(1)}, bf16[2,68,256]{2,1,0:T(8,128)(2,1)S(1)}, u32[]{:S(2)}, u32[]{:S(2)}) collective-permute-start(bf16[2,68,256]{2,1,0:T(8,128)(2,1)S(1)} %get-tuple-element.50), channel_id=1, source_target_pairs={{0,1},{1,0},{2,3},{3,2},{4,5},{5,4},{6,7},{7,6},{8,9},{9,8},{10,11... | collective-permute-start | bytes 208904 | tf_op jit(solution)/shard_map/ppermute | solution.py:32
  66.6 4.9 %second_core.1 = (bf16[64,32,256]{2,1,0:T(8,128)(2,1)}, f32[2,1024,128]{2,1,0:T(8,128)S(1)}) custom-call(s32[4,8]{1,0:T(4,128)S(1)} %pad_add_fusion.links, bf16[1984,256]{1,0:T(8,128)(2,1)S(1)} %shard_map.106.inner, bf16[2048,256]{1,0:T(8,128)(2,1)S(1)} %get-tuple-element.42.bev, bf16[64,256]{1,0:T(8,128)(2,1)S(1)} %collective-permute-done.11.first_row, ...), custom_call_target="tpu_custom_call" | custom-call | tf_op jit(solution)/shard_map/second_core/pallas_call | solution.py:602
  71.6 2.4 %edges.1 = bf16[64,32,256]{2,1,0:T(8,128)(2,1)} custom-call(s32[4,8]{1,0:T(4,128)S(1)} %pad_add_fusion.links, bf16[64,32,256]{2,1,0:T(8,128)(2,1)} %get-tuple-element.46.unused, f32[2,1024,128]{2,1,0:T(8,128)S(1)} %get-tuple-element.47.flanks, bf16[2,68,256]{2,1,0:T(8,128)(2,1)S(1)} %get-tuple-element.53.own_left, ...), custom_call_target="tpu_custom_call", output_to_operand_aliasing={{}: (1, {})} | custom-call | tf_op jit(solution)/shard_map/edges/pallas_call | solution.py:616
  (44 shorter events, 8.0 us)
Async XLA Ops:
  0.7 1.2 %copy-start.1 = (bf16[8,512,128]{2,1,0:T(8,128)(2,1)S(1)}, bf16[8,512,128]{2,1,0:T(8,128)(2,1)}, u32[]{:S(2)}) copy-start(bf16[8,512,128]{2,1,0:T(8,128)(2,1)} %param.10) | copy-start | bytes 3145732
  2.9 13.6 %collective-permute-start = (bf16[1088,128]{1,0:T(8,128)(2,1)S(1)}, bf16[1088,128]{1,0:T(8,128)(2,1)S(1)}, u32[]{:S(2)}, u32[]{:S(2)}) collective-permute-start(bf16[1088,128]{1,0:T(8,128)(2,1)S(1)} %get-tuple-element.27), channel_id=1, source_target_pairs={{0,1},{1,0},{2,3},{3,2},{4,5},{5,4},{6,7},{7,6},{8,9},{9,8},{10,11... | collective-permute-start | bytes 835592 | tf_op jit(solution)/shard_map/ppermute | solution.py:32
  4.2 12.3 %collective-permute-start.1 = (bf16[1088,128]{1,0:T(8,128)(2,1)S(1)}, bf16[1088,128]{1,0:T(8,128)(2,1)S(1)}, u32[]{:S(2)}, u32[]{:S(2)}) collective-permute-start(bf16[1088,128]{1,0:T(8,128)(2,1)S(1)} %get-tuple-element.28), channel_id=1, source_target_pairs={{1,2},{2,1},{3,4},{4,3},{5,6},{6,5},{7,8},{8,7},{9,10},{10,9},{11,... | collective-permute-start | bytes 835592 | tf_op jit(solution)/shard_map/ppermute | solution.py:33
  10.8 10.4 %copy-start.2 = (bf16[8,512,128]{2,1,0:T(8,128)(2,1)S(1)}, bf16[8,512,128]{2,1,0:T(8,128)(2,1)}, u32[]{:S(2)}) copy-start(bf16[8,512,128]{2,1,0:T(8,128)(2,1)} %param.10) | copy-start | bytes 3145732
  10.8 10.4 %copy-start.6 = (bf16[7,128,128]{2,1,0:T(8,128)(2,1)S(1)}, bf16[7,128,128]{2,1,0:T(8,128)(2,1)}, u32[]{:S(2)}) copy-start(bf16[7,128,128]{2,1,0:T(8,128)(2,1)} %param.16) | copy-start | bytes 688132
  17.9 11.7 %collective-permute-start.2 = (bf16[1088,128]{1,0:T(8,128)(2,1)S(1)}, bf16[1088,128]{1,0:T(8,128)(2,1)S(1)}, u32[]{:S(2)}, u32[]{:S(2)}) collective-permute-start(bf16[1088,128]{1,0:T(8,128)(2,1)S(1)} %get-tuple-element.30), channel_id=1, source_target_pairs={{0,1},{1,0},{2,3},{3,2},{4,5},{5,4},{6,7},{7,6},{8,9},{9,8},{10,11... | collective-permute-start | bytes 835592 | tf_op jit(solution)/shard_map/ppermute | solution.py:32
  19.2 10.5 %collective-permute-start.3 = (bf16[1088,128]{1,0:T(8,128)(2,1)S(1)}, bf16[1088,128]{1,0:T(8,128)(2,1)S(1)}, u32[]{:S(2)}, u32[]{:S(2)}) collective-permute-start(bf16[1088,128]{1,0:T(8,128)(2,1)S(1)} %get-tuple-element.31), channel_id=1, source_target_pairs={{1,2},{2,1},{3,4},{4,3},{5,6},{6,5},{7,8},{8,7},{9,10},{10,9},{11,... | collective-permute-start | bytes 835592 | tf_op jit(solution)/shard_map/ppermute | solution.py:33
  21.3 8.4 %copy-start.4 = (bf16[4,1024,256]{2,1,0:T(8,128)(2,1)S(1)}, bf16[4,1024,256]{2,1,0:T(8,128)(2,1)}, u32[]{:S(2)}) copy-start(bf16[4,1024,256]{2,1,0:T(8,128)(2,1)} %height.1) | copy-start | bytes 6291460
  21.3 8.4 %copy-start.7 = (s32[8]{0:T(128)S(1)}, s32[8]{0:T(128)}, u32[]{:S(2)}) copy-start(s32[8]{0:T(128)} %param.12) | copy-start | bytes 100
  21.3 8.4 %copy-start.8 = (s32[8]{0:T(128)S(1)}, s32[8]{0:T(128)}, u32[]{:S(2)}) copy-start(s32[8]{0:T(128)} %param.13) | copy-start | bytes 100
  21.3 8.3 %copy-start.9 = (s32[1,16]{1,0:T(1,128)S(1)}, s32[1,16]{1,0:T(1,128)}, u32[]{:S(2)}) copy-start(s32[1,16]{1,0:T(1,128)} %columns.1) | copy-start | bytes 196
  29.7 28.9 %copy-start = (bf16[3,3,256,256]{3,2,1,0:T(8,128)(2,1)S(1)}, bf16[3,3,256,256]{3,2,1,0:T(8,128)(2,1)}, u32[]{:S(2)}) copy-start(bf16[3,3,256,256]{3,2,1,0:T(8,128)(2,1)} %param.18) | copy-start | bytes 3538948
  33.0 9.2 %collective-permute-start.4 = (bf16[264,128]{1,0:T(8,128)(2,1)S(1)}, bf16[264,128]{1,0:T(8,128)(2,1)S(1)}, u32[]{:S(2)}, u32[]{:S(2)}) collective-permute-start(bf16[264,128]{1,0:T(8,128)(2,1)S(1)} %get-tuple-element.33), channel_id=1, source_target_pairs={{0,1},{1,0},{2,3},{3,2},{4,5},{5,4},{6,7},{7,6},{8,9},{9,8},{10,11... | collective-permute-start | bytes 202760 | tf_op jit(solution)/shard_map/ppermute | solution.py:557
  35.3 8.2 %collective-permute-start.5 = (bf16[264,128]{1,0:T(8,128)(2,1)S(1)}, bf16[264,128]{1,0:T(8,128)(2,1)S(1)}, u32[]{:S(2)}, u32[]{:S(2)}) collective-permute-start(bf16[264,128]{1,0:T(8,128)(2,1)S(1)} %get-tuple-element.34), channel_id=1, source_target_pairs={{0,2},{1,3},{2,0},{3,1},{4,6},{5,7},{6,4},{7,5},{8,10},{9,11},{10,... | collective-permute-start | bytes 202760 | tf_op jit(solution)/shard_map/ppermute | solution.py:557
  35.5 8.3 %collective-permute-start.6 = (bf16[264,128]{1,0:T(8,128)(2,1)S(1)}, bf16[264,128]{1,0:T(8,128)(2,1)S(1)}, u32[]{:S(2)}, u32[]{:S(2)}) collective-permute-start(bf16[264,128]{1,0:T(8,128)(2,1)S(1)} %get-tuple-element.35), channel_id=1, source_target_pairs={{0,3},{1,2},{2,1},{3,0},{4,7},{5,6},{6,5},{7,4},{8,11},{9,10},{10,... | collective-permute-start | bytes 202760 | tf_op jit(solution)/shard_map/ppermute | solution.py:557
  36.6 8.8 %collective-permute-start.7 = (bf16[264,128]{1,0:T(8,128)(2,1)S(1)}, bf16[264,128]{1,0:T(8,128)(2,1)S(1)}, u32[]{:S(2)}, u32[]{:S(2)}) collective-permute-start(bf16[264,128]{1,0:T(8,128)(2,1)S(1)} %get-tuple-element.36), channel_id=1, source_target_pairs={{0,4},{1,5},{2,6},{3,7},{4,0},{5,1},{6,2},{7,3},{8,12},{9,13},{10,... | collective-permute-start | bytes 202760 | tf_op jit(solution)/shard_map/ppermute | solution.py:557
  41.2 7.9 %collective-permute-start.8 = (bf16[264,128]{1,0:T(8,128)(2,1)S(1)}, bf16[264,128]{1,0:T(8,128)(2,1)S(1)}, u32[]{:S(2)}, u32[]{:S(2)}) collective-permute-start(bf16[264,128]{1,0:T(8,128)(2,1)S(1)} %get-tuple-element.37), channel_id=1, source_target_pairs={{0,5},{1,4},{2,7},{3,6},{4,1},{5,0},{6,3},{7,2},{8,13},{9,12},{10,... | collective-permute-start | bytes 202760 | tf_op jit(solution)/shard_map/ppermute | solution.py:557
  42.3 9.1 %collective-permute-start.9 = (bf16[264,128]{1,0:T(8,128)(2,1)S(1)}, bf16[264,128]{1,0:T(8,128)(2,1)S(1)}, u32[]{:S(2)}, u32[]{:S(2)}) collective-permute-start(bf16[264,128]{1,0:T(8,128)(2,1)S(1)} %get-tuple-element.38), channel_id=1, source_target_pairs={{0,6},{1,7},{2,4},{3,5},{4,2},{5,3},{6,0},{7,1},{8,14},{9,15},{10,... | collective-permute-start | bytes 202760 | tf_op jit(solution)/shard_map/ppermute | solution.py:557
  43.5 11.0 %collective-permute-start.10 = (bf16[264,128]{1,0:T(8,128)(2,1)S(1)}, bf16[264,128]{1,0:T(8,128)(2,1)S(1)}, u32[]{:S(2)}, u32[]{:S(2)}) collective-permute-start(bf16[264,128]{1,0:T(8,128)(2,1)S(1)} %get-tuple-element.39), channel_id=1, source_target_pairs={{0,7},{1,6},{2,5},{3,4},{4,3},{5,2},{6,1},{7,0},{8,15},{9,14},{10,... | collective-permute-start | bytes 202760 | tf_op jit(solution)/shard_map/ppermute | solution.py:557
  55.7 10.9 %copy-start.3 = (bf16[3,3,256,256]{3,2,1,0:T(8,128)(2,1)S(1)}, bf16[3,3,256,256]{3,2,1,0:T(8,128)(2,1)}, u32[]{:S(2)}) copy-start(bf16[3,3,256,256]{3,2,1,0:T(8,128)(2,1)} %param.19) | copy-start | bytes 3538948
  55.7 5.6 %collective-permute-start.11 = (bf16[64,256]{1,0:T(8,128)(2,1)S(1)}, bf16[64,256]{1,0:T(8,128)(2,1)S(1)}, u32[]{:S(2)}, u32[]{:S(2)}) collective-permute-start(bf16[64,256]{1,0:T(8,128)(2,1)S(1)} %get-tuple-element.40), channel_id=1, source_target_pairs={{0,8},{8,0},{16,24},{24,16},{1,9},{9,1},{17,25},{25,17},{2,10},{10... | collective-permute-start | bytes 98312 | tf_op jit(solution)/shard_map/ppermute | solution.py:32
  56.6 5.2 %collective-permute-start.12 = (bf16[64,256]{1,0:T(8,128)(2,1)S(1)}, bf16[64,256]{1,0:T(8,128)(2,1)S(1)}, u32[]{:S(2)}, u32[]{:S(2)}) collective-permute-start(bf16[64,256]{1,0:T(8,128)(2,1)S(1)} %get-tuple-element.41), channel_id=1, source_target_pairs={{8,16},{16,8},{9,17},{17,9},{10,18},{18,10},{11,19},{19,11},{12,20... | collective-permute-start | bytes 98312 | tf_op jit(solution)/shard_map/ppermute | solution.py:33
  61.9 9.6 %collective-permute-start.14 = (bf16[2,68,256]{2,1,0:T(8,128)(2,1)S(1)}, bf16[2,68,256]{2,1,0:T(8,128)(2,1)S(1)}, u32[]{:S(2)}, u32[]{:S(2)}) collective-permute-start(bf16[2,68,256]{2,1,0:T(8,128)(2,1)S(1)} %get-tuple-element.49), channel_id=1, source_target_pairs={{1,2},{2,1},{3,4},{4,3},{5,6},{6,5},{9,10},{10,9},{11,12},{12,11},... | collective-permute-start | bytes 208904 | tf_op jit(solution)/shard_map/ppermute | solution.py:33
  64.1 7.4 %collective-permute-start.13 = (bf16[2,68,256]{2,1,0:T(8,128)(2,1)S(1)}, bf16[2,68,256]{2,1,0:T(8,128)(2,1)S(1)}, u32[]{:S(2)}, u32[]{:S(2)}) collective-permute-start(bf16[2,68,256]{2,1,0:T(8,128)(2,1)S(1)} %get-tuple-element.50), channel_id=1, source_target_pairs={{0,1},{1,0},{2,3},{3,2},{4,5},{5,4},{6,7},{7,6},{8,9},{9,8},{10,11... | collective-permute-start | bytes 208904 | tf_op jit(solution)/shard_map/ppermute | solution.py:32
  (1 other events, 0.9 us)
